TPU v7x, 32 devices: a whole 2x2x4 slice. The times are simulated.
32 devices in a mesh: row: 8 (over z, y), col: 4 (over x, core).
Axes of the slice: x: 2, y: 2, z: 4, core: 2. Of those that a mesh axis runs over, the one named last changes fastest.
Arguments:
- matrix: bfloat16 [12, 8, 256, 24, 4, 256], P(None, 'row', None, None, 'col'), as said below
- inv_first: bfloat16 [512, 512], replicated, as said below
- inv_second: bfloat16 [512, 512], replicated, as said below
Outputs:
- panels: bfloat16 [12, 8, 256, 1024], P(None, 'row')
- trailing: bfloat16 [12, 8, 256, 24, 4, 256], P(None, 'row', None, None, 'col')
Inputs may be any that keep to these rules, and one draw needn't show every extreme that they name: `matrix`: symmetric: the entry at (i, j) of M equals the entry at (j, i). `inv_first`: lower triangular: entries above the diagonal are zero, diagonal entries are positive. `inv_second`: lower triangular: entries above the diagonal are zero, diagonal entries are positive.
All inputs are finite; a program needn't handle non-finite values.
Results may differ from a plain program's by a relative error of at most 0.0065.
Values may be sent and summed in bfloat16 or wider, within the bound.
No kernel may reach another device: no remote copies, remote signals or barrier semaphores. Data moves between devices by JAX's collectives and lax.ppermute only.
A program may use at most 256 MiB of HBM per device.

v0:
```python
import jax
import jax.numpy as jnp
from jax import lax
from jax.sharding import PartitionSpec as P


def from_root(value, axis, source):
    kept = jnp.where(lax.axis_index(axis) == source, value, 0).astype(value.dtype)
    return lax.psum(kept, axis)


def outer_minus(target, left_rows, right_rows):
    product = lax.dot_general(
        left_rows, right_rows, (((1,), (1,)), ((), ())), preferred_element_type=jnp.float32
    )
    return (target.astype(jnp.float32) - product).astype(jnp.bfloat16)


def panel_columns(first_tile, step_index):
    halves = []
    for half_index in range(2):
        halves.append(from_root(first_tile, "col", 2 * step_index + half_index))
    return jnp.concatenate(halves, axis=1)


def column_factor(row_factor, col_id, row_count, col_count):
    owner_count = row_count // col_count
    received = []
    for owner_slot in range(owner_count):
        received.append(from_root(row_factor, "row", owner_slot * col_count + col_id))
    gathered = jnp.stack(received, axis=1)
    return gathered.reshape(-1, gathered.shape[-1])


def local(matrix, inv_first, inv_second):
    row_count = lax.axis_size("row")
    col_count = lax.axis_size("col")
    row_id = lax.axis_index("row")
    col_id = lax.axis_index("col")
    tile_rows = matrix.shape[0]
    tile_size = matrix.shape[2]
    tile_cols = matrix.shape[3]
    width = inv_first.shape[0]
    local_rows = tile_rows * tile_size
    local_cols = tile_cols * tile_size
    current = matrix.reshape(local_rows, local_cols)
    row_position = jnp.arange(local_rows, dtype=jnp.int32)
    global_rows = (
        row_position // tile_size * row_count + row_id
    ) * tile_size + row_position % tile_size
    col_position = jnp.arange(local_cols, dtype=jnp.int32)
    global_cols = (
        col_position // tile_size * col_count + col_id
    ) * tile_size + col_position % tile_size

    def factor_rows(first_tile, inverse, step_index):
        columns = panel_columns(first_tile, step_index)
        product = lax.dot_general(
            columns, inverse, (((1,), (1,)), ((), ())), preferred_element_type=jnp.float32
        )
        keep_rows = (global_rows >= (step_index + 1) * width)[:, None]
        return jnp.where(keep_rows, product, jnp.zeros_like(product)).astype(jnp.bfloat16)

    def spread_columns(row_factor):
        shaped = row_factor.reshape(tile_rows, tile_size, width)
        return column_factor(shaped, col_id, row_count, col_count)

    row_first = factor_rows(current[:, :tile_size], inv_first, 0)
    col_first = spread_columns(row_first)
    updated = outer_minus(current, row_first, col_first)
    row_second = factor_rows(updated[:, :tile_size], inv_second, 1)
    col_second = spread_columns(row_second)
    result = outer_minus(updated, row_second, col_second)
    row_tiles = global_rows // tile_size
    col_tiles = global_cols // tile_size
    keep_mask = (
        (global_rows >= 2 * width)[:, None]
        & (global_cols >= 2 * width)[None, :]
        & (row_tiles[:, None] >= col_tiles[None, :])
    )
    trailing = jnp.where(keep_mask, result, jnp.zeros_like(result))
    panels = jnp.concatenate([row_first, row_second], axis=1)
    return (panels.reshape(tile_rows, 1, tile_size, 2 * width), trailing.reshape(matrix.shape))


def solution(mesh):
    placed = (P(None, "row", None, None, "col", None), P(), P())
    return jax.shard_map(
        local,
        mesh=mesh,
        in_specs=placed,
        out_specs=(P(None, "row", None, None), P(None, "row", None, None, "col", None)),
        check_vma=False,
    )
```

profile of v0, /device:TPU:0, one launch (start us, length us, event | category | flops | bytes accessed | tf_op | source)
XLA Modules:
  0.0 727.5 jit_solution(10933837619219839394)
XLA Ops:
  7.2 0.0 copy-start
  7.2 0.0 all-reduce.15.cloned.1.call-start
  7.2 26.1 %copy.13 = bf16[384,8,24,256]{3,1,2,0:T(8,128)(2,1)} copy(bf16[384,8,24,256]{3,2,1,0:T(8,128)(2,1)} %bitcast.35) | data formatting | bytes 75497472
  33.3 3.3 broadcast_select_fusion.7
  36.6 0.0 all-reduce.15.cloned.1.call-update
  36.6 0.0 all-reduce.11.cloned.1.call-start
  36.7 71.4 %all-reduce.15.cloned.1.call-done = (bf16[3072,256]{1,0:T(8,128)(2,1)}, bf16[3072,256]{1,0:T(8,128)(2,1)}) async-done(((bf16[3072,256]{1,0:T(8,128)(2,1)}, bf16[3072,256]{1,0:T(8,128)(2,1)}), (bf16[3072,256]{1,0:T(8,128)(2,1)}, bf16[3072,256]{1,0:T(8,128)(2,1)})) %all-reduce.15.cloned.1.call-update) | async-done | bytes 3145744 | tf_op jit(solution)/shard_map/psum | solution.py:9
  108.1 0.0 copy-done
  108.1 6.4 broadcast_select_fusion.3
  114.5 0.0 all-reduce.11.cloned.1.call-update
  114.5 0.0 all-reduce.13.cloned.1.call-start
  114.6 212.7 %all-reduce.11.cloned.1.call-done = (bf16[12,1,256,512]{3,2,1,0:T(8,128)(2,1)}, bf16[12,1,256,512]{3,2,1,0:T(8,128)(2,1)}) async-done(((bf16[12,1,256,512]{3,2,1,0:T(8,128)(2,1)}, bf16[12,1,256,512]{3,2,1,0:T(8,128)(2,1)}), (bf16[12,1,256,512]{3,2,1,0:T(8,128)(2,1)}, bf16[12,1,256,512]{3,2,1,0:T(8,128)(2,1)})) %all-reduce.11.cloned.1.call-update) | async-done | bytes 6291472 | tf_op jit(solution)/shard_map/psum | solution.py:9
  327.2 0.0 copy-start.2
  327.2 3.6 pad_maximum_fusion
  330.8 0.2 copy-done.2
  331.0 32.4 %subtract_convert_fusion.1 = bf16[3072,6144]{1,0:T(8,128)(2,1)} fusion(bf16[3072,6144]{1,0:T(8,128)(2,1)} %bitcast.34, bf16[3072,512]{1,0:T(8,128)(2,1)S(1)} %copy-done.2, bf16[6144,512]{1,0:T(8,128)(2,1)S(1)} %bitcast.40), kind=kOutput, calls=%fused_computation.1 | convolution fusion | flops 19383975936 | bytes 84934656 | tf_op jit(solution)/shard_map/dot_general | solution.py:13
  363.4 0.0 copy-start.3
  363.4 3.3 broadcast_select_fusion.5
  366.7 0.0 all-reduce.13.cloned.1.call-update
  366.8 0.2 all-reduce.9.cloned.1.call-start
  367.0 67.5 %all-reduce.13.cloned.1.call-done = (bf16[3072,256]{1,0:T(8,128)(2,1)}, bf16[3072,256]{1,0:T(8,128)(2,1)}) async-done(((bf16[3072,256]{1,0:T(8,128)(2,1)}, bf16[3072,256]{1,0:T(8,128)(2,1)}), (bf16[3072,256]{1,0:T(8,128)(2,1)}, bf16[3072,256]{1,0:T(8,128)(2,1)})) %all-reduce.13.cloned.1.call-update) | async-done | bytes 3145744 | tf_op jit(solution)/shard_map/psum | solution.py:9
  434.6 0.0 copy-done.3
  434.6 6.3 broadcast_select_fusion.2
  440.9 0.0 all-reduce.9.cloned.1.call-update
  441.0 6.6 pad_maximum_fusion.1
  447.6 206.1 %all-reduce.9.cloned.1.call-done = (bf16[12,1,256,512]{3,2,1,0:T(8,128)(2,1)}, bf16[12,1,256,512]{3,2,1,0:T(8,128)(2,1)}) async-done(((bf16[12,1,256,512]{3,2,1,0:T(8,128)(2,1)}, bf16[12,1,256,512]{3,2,1,0:T(8,128)(2,1)}), (bf16[12,1,256,512]{3,2,1,0:T(8,128)(2,1)}, bf16[12,1,256,512]{3,2,1,0:T(8,128)(2,1)})) %all-reduce.9.cloned.1.call-update) | async-done | bytes 6291472 | tf_op jit(solution)/shard_map/psum | solution.py:9
  653.6 6.1 pad_maximum_fusion.2
  659.7 35.9 %and_select_fusion = bf16[3072,6144]{1,0:T(8,128)(2,1)} fusion(bf16[3072,6144]{1,0:T(8,128)(2,1)} %subtract_convert_fusion.1, s32[6144]{0:T(1024)S(1)} %add_select_fusion, s32[3072]{0:T(1024)S(1)} %add_select_fusion.2, pred[6144]{0:T(1024)(128)(4,1)S(1)} %broadcast_compare_fusion, pred[3072]{0:T(1024)(128)(4,1)S(1)} %broadcast_compare_fusion.1, ...), kind=kOutput, calls=%fused_computation.2 | convolution fusion | flops 19459473408 | bytes 84980736 | tf_op jit(solution)/shard_map/dot_general | solution.py:13
  695.5 0.0 copy-start.1
  695.5 25.5 %copy.14 = bf16[384,8,24,256]{3,2,1,0:T(8,128)(2,1)} copy(bf16[384,8,24,256]{3,1,2,0:T(8,128)(2,1)} %bitcast.36) | data formatting | bytes 75497472
  721.0 0.0 copy-done.1
  (5 shorter events, 0.1 us)
Async XLA Ops:
  7.2 101.0 %copy-start = (bf16[512,512]{1,0:T(8,128)(2,1)S(1)}, bf16[512,512]{1,0:T(8,128)(2,1)}, u32[]{:S(2)}) copy-start(bf16[512,512]{1,0:T(8,128)(2,1)} %param.4) | copy-start | bytes 1572868
  7.2 100.9 %all-reduce.15.cloned.1.call-start = ((), (), s32[]{:S(2)}) async-start(), calls=%async_computation.3 | async-start | bytes 6291456 | tf_op jit(solution)/shard_map/psum | solution.py:9
  36.6 290.6 %all-reduce.11.cloned.1.call-start = ((), (), s32[]{:S(2)}) async-start(), calls=%async_computation.1 | async-start | bytes 12582912 | tf_op jit(solution)/shard_map/psum | solution.py:9
  114.5 320.0 %all-reduce.13.cloned.1.call-start = ((), (), s32[]{:S(2)}) async-start(), calls=%async_computation.2 | async-start | bytes 6291456 | tf_op jit(solution)/shard_map/psum | solution.py:9
  327.2 3.7 copy-start.2
  363.4 71.2 %copy-start.3 = (bf16[512,512]{1,0:T(8,128)(2,1)S(1)}, bf16[512,512]{1,0:T(8,128)(2,1)}, u32[]{:S(2)}) copy-start(bf16[512,512]{1,0:T(8,128)(2,1)} %param.5) | copy-start | bytes 1572868
  366.8 286.8 %all-reduce.9.cloned.1.call-start = ((), (), s32[]{:S(2)}) async-start(), calls=%async_computation | async-start | bytes 12582912 | tf_op jit(solution)/shard_map/psum | solution.py:9
  695.5 25.5 %copy-start.1 = (bf16[512,512]{1,0:T(8,128)(2,1)S(1)}, bf16[512,512]{1,0:T(8,128)(2,1)}, u32[]{:S(2)}) copy-start(bf16[512,512]{1,0:T(8,128)(2,1)} %param.4) | copy-start | bytes 1572868
Sparse Core Ops, SparseCore 0:
  36.8 71.3 all-reduce.14
  114.7 212.5 all-reduce.10
  366.9 67.6 all-reduce.12
  441.0 212.5 all-reduce.8
where the time goes:
time: 728 us
  waiting for transfers between devices  558 us (77%)
  matrix products  81 us (11%)
  local copies, waits for them, and re-layouts  51.7 us (7%)
  other arithmetic  22.9 us (3%)
  between operations  13.9 us (2%)
    psum x4, waiting for transfers between devices, from_root(): return lax.psum(kept, axis)  558 us
    dot_general x2, matrix products, outer_minus(): lax.dot_general(left_rows, right_rows, (((1,), (1,)), ((), ())), preferre...  68.3 us
    unnamed x10, local copies, waits for them, and re-layouts  51.7 us
  transfers between devices with their start and end apart: 4, of which 4 were waited for; matrix products, arithmetic and copies ran while one was open for 1% of the time, Pallas kernels for 0%

commit v1 on v0

--- a/solution.py
+++ b/solution.py
@@ -1,7 +1,15 @@
 import jax
 import jax.numpy as jnp
 from jax import lax
+from jax.experimental import pallas as pl
+from jax.experimental.pallas import tpu as pltpu
 from jax.sharding import PartitionSpec as P
+
+F32 = jnp.float32
+BF16 = jnp.bfloat16
+LANES = 128
+SUB = 8
+VMEM_LIMIT = 60 * 1024 * 1024
 
 
 def from_root(value, axis, source):
@@ -32,7 +40,7 @@
     return gathered.reshape(-1, gathered.shape[-1])
 
 
-def local(matrix, inv_first, inv_second):
+def local_any(matrix, inv_first, inv_second):
     row_count = lax.axis_size("row")
     col_count = lax.axis_size("col")
     row_id = lax.axis_index("row")
@@ -83,12 +91,240 @@
     return (panels.reshape(tile_rows, 1, tile_size, 2 * width), trailing.reshape(matrix.shape))
 
 
+def dot(left, right):
+    return lax.dot_general(left, right, (((1,), (0,)), ((), ())), preferred_element_type=F32)
+
+
+def link_kernel(ids, mine, other, inv0t, low, lowt):
+    slot, plane, core = ids[0] % 4, ids[1] // 2, ids[1] % 2
+    tile = mine.shape[1]
+
+    def piece(panel_tile, owner):
+        held = slot ^ panel_tile
+        return jnp.where(core == owner, mine[held].astype(F32), other[held].astype(F32))
+
+    @pl.when(plane == 0)
+    def _():
+        rows = [jnp.concatenate([piece(2 + i, j) for j in range(2)], axis=1) for i in range(2)]
+        block = jnp.concatenate(rows, axis=0)
+        result = dot(block.astype(BF16), inv0t[...])
+        low[...] = result.astype(BF16)
+        lowt[...] = result.T.astype(BF16)
+
+    @pl.when(plane == 1)
+    def _():
+        rows = [jnp.concatenate([piece(j, i) for i in range(2)], axis=1) for j in range(2)]
+        block = jnp.concatenate(rows, axis=0).T
+        result = dot(block.astype(BF16), inv0t[...])
+        low[...] = result.astype(BF16)
+        lowt[...] = result.T.astype(BF16)
+
+
+def rows_kernel(ids, q0, q1, q2, q3, inv0t, inv1t, lowt, out, buf):
+    tile = q0.shape[1]
+    width = 2 * tile
+    row_id, col_id = ids[0], ids[1]
+    for m, ref in enumerate((q0, q1, q2, q3)):
+        buf[:, pl.ds(pl.multiple_of((col_id ^ m) * tile, tile), tile)] = ref[0]
+    tile_row = pl.program_id(0) * 8 + row_id
+    first = dot(buf[:, :width], inv0t[...])
+    first = jnp.where(tile_row >= 2, first, 0.0).astype(BF16)
+    rest = (buf[:, width:].astype(F32) - dot(first, lowt[...])).astype(BF16)
+    second = dot(rest, inv1t[...])
+    second = jnp.where(tile_row >= 4, second, 0.0).astype(BF16)
+    out[0, :, :width] = first
+    out[0, :, width:] = second
+
+
+def update_kernel(group, ids, *refs):
+    pieces, (inv0, inv1, low, factor, matrix), rest = refs[:8], refs[8:13], refs[13:]
+    out, raw, cols, acc = rest[-4:]
+    step = pl.program_id(0)
+    tile = factor.shape[1]
+    width = 2 * tile
+    row_id, col_id = ids[0], ids[1]
+
+    @pl.when(step == 0)
+    def _():
+        for m in range(4):
+            base = pl.multiple_of(((row_id % 4) ^ m) * tile, tile)
+            for s in range(SUB):
+                raw[pl.ds(base, tile), s * tile : (s + 1) * tile] = pieces[2 * m + s % 2][s // 2]
+        for s in range(SUB):
+            tile_col = (group * SUB + s) * 4 + col_id
+            span = slice(s * tile, (s + 1) * tile)
+            first = dot(inv0[...], raw[:width, span])
+            first = jnp.where(tile_col >= 2, first, 0.0).astype(BF16)
+            cols[:width, span] = first
+            left = (raw[width:, span].astype(F32) - dot(low[...], first)).astype(BF16)
+            second = dot(inv1[...], left)
+            cols[width:, span] = jnp.where(tile_col >= 4, second, 0.0).astype(BF16)
+
+    tile_row = step * 8 + row_id
+    end = jnp.where(tile_row >= 4, (tile_row - col_id) // 4 + 1 - group * SUB, 0)
+    begin = 1 if group == 0 else 0
+
+    @pl.when(end <= begin)
+    def _():
+        out[...] = jnp.zeros_like(out)
+
+    @pl.when(end > begin)
+    def _():
+        for s in range(begin, SUB):
+
+            @pl.when(s < end)
+            def _():
+                product = dot(factor[0], cols[:, s * tile : (s + 1) * tile])
+                for part in range(tile // LANES):
+                    lanes = slice(part * LANES, (part + 1) * LANES)
+                    acc[part, pl.ds(s, tile, stride=SUB), :] = product[:, lanes]
+
+        some = 16
+        sub = lax.broadcasted_iota(jnp.int32, (some, SUB, LANES), 1)
+        keep = (sub >= begin) & (sub < end)
+
+        def finish(i, carry):
+            at = pl.multiple_of(i * some, some)
+            span = pl.ds(pl.multiple_of(at * SUB, some * SUB), some * SUB)
+            for part in range(tile // LANES):
+                lanes = slice(part * LANES, (part + 1) * LANES)
+                product = acc[part, span, :].reshape(some, SUB, LANES)
+                value = matrix[0, pl.ds(at, some), :, lanes].astype(F32) - product
+                out[0, pl.ds(at, some), :, lanes] = jnp.where(keep, value, 0.0).astype(BF16)
+            return carry
+
+        lax.fori_loop(0, tile // some, finish, 0)
+
+
+def params():
+    return pltpu.CompilerParams(vmem_limit_bytes=VMEM_LIMIT)
+
+
+def whole(array):
+    rank = array.ndim
+    return pl.BlockSpec(array.shape, lambda *_: (0,) * rank)
+
+
+def local(matrix, inv_first, inv_second):
+    row_id = lax.axis_index("row")
+    col_id = lax.axis_index("col")
+    ids = jnp.stack([row_id, col_id]).astype(jnp.int32)
+    tiles, _, tile, tile_cols, _, _ = matrix.shape
+    width = inv_first.shape[0]
+    groups = tile_cols // SUB
+    view = matrix.reshape(tiles, tile, tile_cols, tile)
+    upper = row_id >= 4
+
+    def move(value, target):
+        pairs = []
+        for r in range(8):
+            for c in range(4):
+                to = target(r, c)
+                if to is not None:
+                    pairs.append((r * 4 + c, to[0] * 4 + to[1]))
+        return lax.ppermute(value, ("row", "col"), pairs)
+
+    strip = view[:, :, 0, :]
+    swapped = jnp.swapaxes(strip, 1, 2)
+    held = jnp.swapaxes(view[0], 0, 1)
+
+    pieces = []
+    for group in range(groups):
+        lo = slice(group * SUB, (group + 1) * SUB, 2)
+        hi = slice(group * SUB + 1, (group + 1) * SUB, 2)
+        even, odd = held[lo], held[hi]
+        half = slice(group * SUB // 2, (group + 1) * SUB // 2)
+        even_up = move(even, lambda r, c: (r + 4, c) if r < 4 else None)
+        odd_up = move(swapped[half], lambda r, c: (4 + c, r - 4) if r >= 4 else None)
+        even = jnp.where(upper, even_up, even)
+        odd = jnp.where(upper, odd_up, odd)
+        across_z = lambda r, c: (r ^ 2, c)
+        across_y = lambda r, c: (r ^ 1, c)
+        even_z, even_y = move(even, across_z), move(even, across_y)
+        odd_z, odd_y = move(odd, across_z), move(odd, across_y)
+        even_zy, odd_zy = move(even_z, across_y), move(odd_y, across_z)
+        pieces.append((even, odd, even_y, odd_y, even_z, odd_z, even_zy, odd_zy))
+
+    strip_1 = move(strip, lambda r, c: (r, c ^ 1))
+    strip_2 = move(strip, lambda r, c: (r, c ^ 2))
+    strip_3 = move(strip_2, lambda r, c: (r, c ^ 1))
+
+    inv0t, inv1t = inv_first.T, inv_second.T
+    mine = jnp.stack([pieces[0][2 * m][0] for m in range(4)])
+    other = move(mine, lambda r, c: (r, c ^ 1))
+    smem = pl.BlockSpec(memory_space=pltpu.SMEM)
+    square = jax.ShapeDtypeStruct((width, width), BF16)
+    low, lowt = pl.pallas_call(
+        link_kernel,
+        in_specs=[smem, whole(mine), whole(other), whole(inv0t)],
+        out_specs=[whole(square), whole(square)],
+        out_shape=[square, square],
+        grid=(1,),
+        compiler_params=params(),
+        name="link",
+    )(ids, mine, other, inv0t)
+
+    block = pl.BlockSpec((1, tile, tile), lambda t: (t, 0, 0))
+    panels = pl.pallas_call(
+        rows_kernel,
+        grid=(tiles,),
+        in_specs=[smem, block, block, block, block, whole(inv0t), whole(inv1t), whole(lowt)],
+        out_specs=pl.BlockSpec((1, tile, 2 * width), lambda t: (t, 0, 0)),
+        out_shape=jax.ShapeDtypeStruct((tiles, tile, 2 * width), BF16),
+        scratch_shapes=[pltpu.VMEM((tile, 2 * width), BF16)],
+        compiler_params=params(),
+        name="rows",
+    )(ids, strip, strip_1, strip_2, strip_3, inv0t, inv1t, lowt)
+
+    result = None
+    for group in range(groups):
+        operands = [ids, *pieces[group], inv_first, inv_second, low, panels, view]
+        specs = [smem, *[whole(p) for p in pieces[group]], whole(inv_first), whole(inv_second), whole(low)]
+        specs.append(pl.BlockSpec((1, tile, 2 * width), lambda t: (t, 0, 0)))
+        specs.append(pl.BlockSpec((1, tile, SUB, tile), lambda t, g=group: (t, 0, g, 0)))
+        aliases = {}
+        if result is not None:
+            aliases = {len(operands): 0}
+            operands.append(result)
+            specs.append(pl.BlockSpec(memory_space=pl.ANY))
+
+        def kernel(*refs, g=group):
+            update_kernel(g, *refs)
+
+        result = pl.pallas_call(
+            kernel,
+            grid=(tiles,),
+            in_specs=specs,
+            out_specs=pl.BlockSpec((1, tile, SUB, tile), lambda t, g=group: (t, 0, g, 0)),
+            out_shape=jax.ShapeDtypeStruct(view.shape, BF16),
+            scratch_shapes=[
+                pltpu.VMEM((2 * width, SUB * tile), BF16),
+                pltpu.VMEM((2 * width, SUB * tile), BF16),
+                pltpu.VMEM((tile // LANES, tile * SUB, LANES), F32),
+            ],
+            input_output_aliases=aliases,
+            compiler_params=params(),
+            name="update_%d" % group,
+        )(*operands)
+
+    return panels.reshape(tiles, 1, tile, 2 * width), result.reshape(matrix.shape)
+
+
+def fits(mesh, matrix, inv_first):
+    tiles_match = matrix.shape[3] % SUB == 0 and matrix.shape[3] == 2 * matrix.shape[0]
+    panel_match = inv_first.shape[0] == 2 * matrix.shape[2]
+    return mesh.shape["row"] == 8 and mesh.shape["col"] == 4 and tiles_match and panel_match
+
+
 def solution(mesh):
-    placed = (P(None, "row", None, None, "col", None), P(), P())
+    def body(matrix, inv_first, inv_second):
+        plan = local if fits(mesh, matrix, inv_first) else local_any
+        return plan(matrix, inv_first, inv_second)
+
     return jax.shard_map(
-        local,
+        body,
         mesh=mesh,
-        in_specs=placed,
+        in_specs=(P(None, "row", None, None, "col", None), P(), P()),
         out_specs=(P(None, "row", None, None), P(None, "row", None, None, "col", None)),
         check_vma=False,
     )

time: 728 us -> 315 us (0.43)
  waiting for transfers between devices: 558 us -> 97 us
  Pallas kernels: 0 us -> 115 us
  matrix products: 81 us -> 0 us
  starting transfers between devices: 0.34 us -> 71.7 us
  local copies, waits for them, and re-layouts: 51.7 us -> 23 us
  other arithmetic: 22.9 us -> 2.88 us
  between operations: 13.9 us -> 0.96 us
    psum x4 -> x0, waiting for transfers between devices: 558 us -> none  [from_root(): return lax.psum(kept, axis)]
    pallas_call x0 -> x5, Pallas kernels: none -> 115 us  [the longest x3 97.5 us: local(): pl.pallas_call(kernel, grid=(tiles,), in_specs=specs, out_specs=pl.BlockS...]
    ppermute x0 -> x28, waiting for transfers between devices: none -> 97 us  [move(): return lax.ppermute(value, ('row', 'col'), pairs)]
    dot_general x4 -> x0, matrix products: 81 us -> none  [the longest x2 68.3 us: outer_minus(): lax.dot_general(left_rows, right_rows, (((1,), (1,)), ((), ())), preferre...]
    ppermute x0 -> x28, starting transfers between devices: none -> 71.7 us  [move(): return lax.ppermute(value, ('row', 'col'), pairs)]
    unnamed x10 -> x51, local copies, waits for them, and re-layouts: 51.7 us -> 10.4 us
    slice x0 -> x8, local copies, waits for them, and re-layouts: none -> 12.6 us  [the longest x1 6.88 us: local(): strip = view[:, :, 0, :]]
    another operation x2, other arithmetic: 9.62 us -> 0.71 us  [the longest x1 0.65 us: local(): ids = jnp.stack([row_id, col_id]).astype(jnp.int32)]
  transfers between devices with their start and end apart: 4 -> 28, of which waited for: 4 -> 11; matrix products, arithmetic and copies ran while one was open for 1% -> 3% of each run, Pallas kernels for 0% -> 28%
where the time goes in v1:
time: 315 us; the launch traced here: 311 us
  Pallas kernels  115 us (37%)
  waiting for transfers between devices  97 us (31%)
  starting transfers between devices  71.7 us (23%)
  local copies, waits for them, and re-layouts  23 us (7%)
    pallas_call x3, Pallas kernels, local(): pl.pallas_call(kernel, grid=(tiles,), in_specs=specs, out_specs=pl.BlockS...  97.5 us
    ppermute x28, waiting for transfers between devices, move(): return lax.ppermute(value, ('row', 'col'), pairs)  97 us
    ppermute x28, starting transfers between devices, move(): return lax.ppermute(value, ('row', 'col'), pairs)  71.7 us
    pallas_call x1, Pallas kernels, local(): pl.pallas_call(rows_kernel, grid=(tiles,), in_specs=[smem, block, block,...  14.5 us
    unnamed x51, local copies, waits for them, and re-layouts  10.4 us
    slice x1, local copies, waits for them, and re-layouts, local(): strip = view[:, :, 0, :]  6.88 us
  transfers between devices with their start and end apart: 28, of which 11 were waited for; matrix products, arithmetic and copies ran while one was open for 3% of the time, Pallas kernels for 28%

profile of v1, /device:TPU:0, one launch (start us, length us, event | category | flops | bytes accessed | tf_op | source)
XLA Modules:
  0.0 310.7 jit_solution(7072536700015111851)
XLA Ops:
  0.6 6.9 %slice.61 = bf16[12,256,1,256]{3,2,1,0:T(2,128)(2,1)S(1)} slice(bf16[12,256,24,256]{3,2,1,0:T(8,128)(2,1)} %bitcast.22), slice={[0:12], [0:256], [0:1], [0:256]} | slice | bytes 3145728 | tf_op jit(solution)/shard_map/slice | solution.py:227
  7.5 5.0 %copy.46 = bf16[12,256,1,256]{1,3,0,2:T(8,128)(2,1)} copy(bf16[12,256,1,256]{3,2,1,0:T(2,128)(2,1)S(1)} %slice.61) | data formatting | bytes 3145728
  12.5 2.3 fusion.1
  16.1 1.5 collective-permute-start.9
  17.6 2.1 slice.47
  20.4 1.3 fusion
  21.7 10.6 %collective-permute-start.16 = (bf16[4,256,256]{2,1,0:T(8,128)(2,1)}, bf16[4,256,256]{2,1,0:T(8,128)(2,1)}, u32[]{:S(2)}, u32[]{:S(2)}) collective-permute-start(bf16[4,256,256]{2,1,0:T(8,128)(2,1)} %get-tuple-element.16), channel_id=1, source_target_pairs={{0,16},{1,17},{2,18},{3,19},{4,20},{5,21},{6,22},{7,23},{8,24},{9,... | collective-permute-start | bytes 1572872 | tf_op jit(solution)/shard_map/ppermute | solution.py:225
  32.3 2.1 collective-permute-start.3
  34.4 2.1 collective-permute-start.8
  36.5 1.5 copy.50
  38.8 4.9 %collective-permute-start.1 = (bf16[12,256,256]{2,1,0:T(8,128)(2,1)}, bf16[12,256,256]{2,1,0:T(8,128)(2,1)}, u32[]{:S(2)}, u32[]{:S(2)}) collective-permute-start(bf16[12,256,256]{2,1,0:T(8,128)(2,1)} %bitcast.21.q0), channel_id=1, source_target_pairs={{0,2},{1,3},{2,0},{3,1},{4,6},{5,7},{6,4},{7,5},{8,10},{9,11},{10,... | collective-permute-start | bytes 4718600 | tf_op jit(solution)/shard_map/ppermute | solution.py:225
  43.7 10.3 %collective-permute-done.3 = bf16[4,256,256]{2,1,0:T(8,128)(2,1)} collective-permute-done((bf16[4,256,256]{2,1,0:T(8,128)(2,1)}, bf16[4,256,256]{2,1,0:T(8,128)(2,1)}, u32[]{:S(2)}, u32[]{:S(2)}) %collective-permute-start.3) | collective-permute-done | bytes 524320 | tf_op jit(solution)/shard_map/ppermute | solution.py:225
  54.0 11.2 %collective-permute-done.8 = bf16[4,256,256]{2,1,0:T(8,128)(2,1)} collective-permute-done((bf16[4,256,256]{2,1,0:T(8,128)(2,1)}, bf16[4,256,256]{2,1,0:T(8,128)(2,1)}, u32[]{:S(2)}, u32[]{:S(2)}) %collective-permute-start.8) | collective-permute-done | bytes 524320 | tf_op jit(solution)/shard_map/ppermute | solution.py:225
  65.2 2.2 slice_select_fusion
  67.5 36.6 %collective-permute-start.5 = (bf16[4,256,256]{2,1,0:T(8,128)(2,1)S(1)}, bf16[4,256,256]{2,1,0:T(8,128)(2,1)S(1)}, u32[]{:S(2)}, u32[]{:S(2)}) collective-permute-start(bf16[4,256,256]{2,1,0:T(8,128)(2,1)S(1)} %get-tuple-element.11.refs_1_), channel_id=1, source_target_pairs={{0,8},{1,9},{2,10},{3,11},{4,12},{5,13},{6,14},{7,15},{8,0},{9,1},... | collective-permute-start | bytes 1572872 | tf_op jit(solution)/shard_map/ppermute | solution.py:225
  104.5 1.6 collective-permute-start.25
  106.2 10.6 %collective-permute-done.5.refs_5_ = bf16[4,256,256]{2,1,0:T(8,128)(2,1)S(1)} collective-permute-done((bf16[4,256,256]{2,1,0:T(8,128)(2,1)S(1)}, bf16[4,256,256]{2,1,0:T(8,128)(2,1)S(1)}, u32[]{:S(2)}, u32[]{:S(2)}) %collective-permute-start.5) | collective-permute-done | bytes 524320 | tf_op jit(solution)/shard_map/ppermute | solution.py:225
  116.8 2.1 collective-permute-start.20
  119.3 10.7 %collective-permute-done.25.refs_4_ = bf16[4,256,256]{2,1,0:T(8,128)(2,1)S(1)} collective-permute-done((bf16[4,256,256]{2,1,0:T(8,128)(2,1)S(1)}, bf16[4,256,256]{2,1,0:T(8,128)(2,1)S(1)}, u32[]{:S(2)}, u32[]{:S(2)}) %collective-permute-start.25) | collective-permute-done | bytes 524320 | tf_op jit(solution)/shard_map/ppermute | solution.py:225
  130.6 1.5 collective-permute-start.6
  132.1 6.7 %collective-permute-done.20.refs_5_ = bf16[4,256,256]{2,1,0:T(8,128)(2,1)S(1)} collective-permute-done((bf16[4,256,256]{2,1,0:T(8,128)(2,1)S(1)}, bf16[4,256,256]{2,1,0:T(8,128)(2,1)S(1)}, u32[]{:S(2)}, u32[]{:S(2)}) %collective-permute-start.20) | collective-permute-done | bytes 524320 | tf_op jit(solution)/shard_map/ppermute | solution.py:225
  139.3 2.1 collective-permute-done.19.refs_4_
  141.5 11.1 %collective-permute-done.18.refs_3_ = bf16[4,256,256]{2,1,0:T(8,128)(2,1)S(1)} collective-permute-done((bf16[4,256,256]{2,1,0:T(8,128)(2,1)S(1)}, bf16[4,256,256]{2,1,0:T(8,128)(2,1)S(1)}, u32[]{:S(2)}, u32[]{:S(2)}) %collective-permute-start.18) | collective-permute-done | bytes 524320 | tf_op jit(solution)/shard_map/ppermute | solution.py:225
  152.6 10.2 %collective-permute-done.6.refs_7_ = bf16[4,256,256]{2,1,0:T(8,128)(2,1)S(1)} collective-permute-done((bf16[4,256,256]{2,1,0:T(8,128)(2,1)S(1)}, bf16[4,256,256]{2,1,0:T(8,128)(2,1)S(1)}, u32[]{:S(2)}, u32[]{:S(2)}) %collective-permute-start.6) | collective-permute-done | bytes 524320 | tf_op jit(solution)/shard_map/ppermute | solution.py:225
  165.5 12.2 %collective-permute-done.11.refs_4_ = bf16[4,256,256]{2,1,0:T(8,128)(2,1)} collective-permute-done((bf16[4,256,256]{2,1,0:T(8,128)(2,1)S(1)}, bf16[4,256,256]{2,1,0:T(8,128)(2,1)}, u32[]{:S(2)}, u32[]{:S(2)}) %collective-permute-start.11) | collective-permute-done | bytes 524320 | tf_op jit(solution)/shard_map/ppermute | solution.py:225
  178.1 10.8 %collective-permute-done.22.refs_7_ = bf16[4,256,256]{2,1,0:T(8,128)(2,1)S(1)} collective-permute-done((bf16[4,256,256]{2,1,0:T(8,128)(2,1)S(1)}, bf16[4,256,256]{2,1,0:T(8,128)(2,1)S(1)}, u32[]{:S(2)}, u32[]{:S(2)}) %collective-permute-start.22) | collective-permute-done | bytes 524320 | tf_op jit(solution)/shard_map/ppermute | solution.py:225
  189.2 1.7 collective-permute-start.13
  195.5 3.1 link.1
  198.6 14.5 %rows.1.refs_12_ = bf16[12,256,1024]{2,1,0:T(8,128)(2,1)} custom-call(s32[2]{0:T(128)} %pad_add_fusion.ids.refs_0_, bf16[12,256,256]{2,1,0:T(8,128)(2,1)} %bitcast.21.q0, bf16[12,256,256]{2,1,0:T(8,128)(2,1)} %copy-done.10, bf16[12,256,256]{2,1,0:T(8,128)(2,1)} %collective-permute-done.1.q2, bf16[12,256,256]{2,1,0:T(8,128)(2,1)} %collective-permute-done.2.q3, ...), custom_call_target="tpu_custom_call" | custom-call | tf_op jit(solution)/shard_map/rows/pallas_call | solution.py:268
  213.1 37.3 %update_0.1.refs_14_ = bf16[12,256,24,256]{3,2,1,0:T(8,128)(2,1)} custom-call(s32[2]{0:T(128)} %pad_add_fusion.ids.refs_0_, bf16[4,256,256]{2,1,0:T(8,128)(2,1)} %copy-done.3, bf16[4,256,256]{2,1,0:T(8,128)(2,1)} %copy-done.8, bf16[4,256,256]{2,1,0:T(8,128)(2,1)} %copy-done.12, bf16[4,256,256]{2,1,0:T(8,128)(2,1)} %copy-done.14, ...), custom_call_target="tpu_custom_call" | custom-call | tf_op jit(solution)/shard_map/update_0/pallas_call | solution.py:294
  250.4 33.7 %update_1.1.refs_14_ = bf16[12,256,24,256]{3,2,1,0:T(8,128)(2,1)} custom-call(s32[2]{0:T(128)} %pad_add_fusion.ids.refs_0_, bf16[4,256,256]{2,1,0:T(8,128)(2,1)} %copy-done.6, bf16[4,256,256]{2,1,0:T(8,128)(2,1)} %copy-done.7, bf16[4,256,256]{2,1,0:T(8,128)(2,1)} %copy-done.16, ...), custom_call_target="tpu_custom_call", output_to_operand_aliasing={{}: (14, {})} | custom-call | tf_op jit(solution)/shard_map/update_1/pallas_call | solution.py:294
  284.1 26.5 %update_2.1 = bf16[12,256,24,256]{3,2,1,0:T(8,128)(2,1)} custom-call(s32[2]{0:T(128)} %pad_add_fusion.ids.refs_0_, bf16[4,256,256]{2,1,0:T(8,128)(2,1)} %copy-done.4, bf16[4,256,256]{2,1,0:T(8,128)(2,1)} %copy-done.5, bf16[4,256,256]{2,1,0:T(8,128)(2,1)} %collective-permute-done.10.refs_3_, ...), custom_call_target="tpu_custom_call", output_to_operand_aliasing={{}: (14, {})} | custom-call | tf_op jit(solution)/shard_map/update_2/pallas_call | solution.py:294
  (91 shorter events, 12.9 us)
Async XLA Ops:
  14.7 19.7 %collective-permute-start.17 = (bf16[4,256,256]{2,1,0:T(8,128)(2,1)S(1)}, bf16[4,256,256]{2,1,0:T(8,128)(2,1)S(1)}, u32[]{:S(2)}, u32[]{:S(2)}) collective-permute-start(bf16[4,256,256]{2,1,0:T(8,128)(2,1)S(1)} %get-tuple-element.20), channel_id=1, source_target_pairs={{16,16},{17,20},{18,24},{19,28},{20,17},{21,21},{22,25},{23,29},{2... | collective-permute-start | bytes 1572872 | tf_op jit(solution)/shard_map/ppermute | solution.py:225
  15.4 22.6 %collective-permute-start.24 = (bf16[4,256,256]{2,1,0:T(8,128)(2,1)S(1)}, bf16[4,256,256]{2,1,0:T(8,128)(2,1)S(1)}, u32[]{:S(2)}, u32[]{:S(2)}) collective-permute-start(bf16[4,256,256]{2,1,0:T(8,128)(2,1)S(1)} %get-tuple-element.19), channel_id=1, source_target_pairs={{16,16},{17,20},{18,24},{19,28},{20,17},{21,21},{22,25},{23,29},{2... | collective-permute-start | bytes 1572872 | tf_op jit(solution)/shard_map/ppermute | solution.py:225
  16.1 27.6 %collective-permute-start.9 = (bf16[4,256,256]{2,1,0:T(8,128)(2,1)}, bf16[4,256,256]{2,1,0:T(8,128)(2,1)}, u32[]{:S(2)}, u32[]{:S(2)}) collective-permute-start(bf16[4,256,256]{2,1,0:T(8,128)(2,1)} %get-tuple-element.21), channel_id=1, source_target_pairs={{16,16},{17,20},{18,24},{19,28},{20,17},{21,21},{22,25},{23,29},{2... | collective-permute-start | bytes 1572872 | tf_op jit(solution)/shard_map/ppermute | solution.py:225
  21.7 22.0 %collective-permute-start.16 = (bf16[4,256,256]{2,1,0:T(8,128)(2,1)}, bf16[4,256,256]{2,1,0:T(8,128)(2,1)}, u32[]{:S(2)}, u32[]{:S(2)}) collective-permute-start(bf16[4,256,256]{2,1,0:T(8,128)(2,1)} %get-tuple-element.16), channel_id=1, source_target_pairs={{0,16},{1,17},{2,18},{3,19},{4,20},{5,21},{6,22},{7,23},{8,24},{9,... | collective-permute-start | bytes 1572872 | tf_op jit(solution)/shard_map/ppermute | solution.py:225
  32.3 21.7 %collective-permute-start.3 = (bf16[4,256,256]{2,1,0:T(8,128)(2,1)}, bf16[4,256,256]{2,1,0:T(8,128)(2,1)}, u32[]{:S(2)}, u32[]{:S(2)}) collective-permute-start(bf16[4,256,256]{2,1,0:T(8,128)(2,1)} %get-tuple-element.18), channel_id=1, source_target_pairs={{0,16},{1,17},{2,18},{3,19},{4,20},{5,21},{6,22},{7,23},{8,24},{9,... | collective-permute-start | bytes 1572872 | tf_op jit(solution)/shard_map/ppermute | solution.py:225
  34.4 30.8 %collective-permute-start.8 = (bf16[4,256,256]{2,1,0:T(8,128)(2,1)}, bf16[4,256,256]{2,1,0:T(8,128)(2,1)}, u32[]{:S(2)}, u32[]{:S(2)}) collective-permute-start(bf16[4,256,256]{2,1,0:T(8,128)(2,1)} %get-tuple-element.17), channel_id=1, source_target_pairs={{0,16},{1,17},{2,18},{3,19},{4,20},{5,21},{6,22},{7,23},{8,24},{9,... | collective-permute-start | bytes 1572872 | tf_op jit(solution)/shard_map/ppermute | solution.py:225
  38.8 100.0 %collective-permute-start.1 = (bf16[12,256,256]{2,1,0:T(8,128)(2,1)}, bf16[12,256,256]{2,1,0:T(8,128)(2,1)}, u32[]{:S(2)}, u32[]{:S(2)}) collective-permute-start(bf16[12,256,256]{2,1,0:T(8,128)(2,1)} %bitcast.21.q0), channel_id=1, source_target_pairs={{0,2},{1,3},{2,0},{3,1},{4,6},{5,7},{6,4},{7,5},{8,10},{9,11},{10,... | collective-permute-start | bytes 4718600 | tf_op jit(solution)/shard_map/ppermute | solution.py:225
  43.7 149.1 %copy-start.1 = (bf16[512,512]{1,0:T(8,128)(2,1)S(1)}, bf16[512,512]{1,0:T(8,128)(2,1)}, u32[]{:S(2)}) copy-start(bf16[512,512]{1,0:T(8,128)(2,1)} %refs_9_.5) | copy-start | bytes 1572868
  67.4 145.7 %copy-start.3 = (bf16[4,256,256]{2,1,0:T(8,128)(2,1)}, bf16[4,256,256]{2,1,0:T(8,128)(2,1)S(1)}, u32[]{:S(2)}) copy-start(bf16[4,256,256]{2,1,0:T(8,128)(2,1)S(1)} %get-tuple-element.11.refs_1_) | copy-start | bytes 1572868
  67.4 145.7 %copy-start.4 = (bf16[4,256,256]{2,1,0:T(8,128)(2,1)}, bf16[4,256,256]{2,1,0:T(8,128)(2,1)S(1)}, u32[]{:S(2)}) copy-start(bf16[4,256,256]{2,1,0:T(8,128)(2,1)S(1)} %get-tuple-element.12.refs_1_) | copy-start | bytes 1572868
  67.4 145.7 %copy-start.5 = (bf16[4,256,256]{2,1,0:T(8,128)(2,1)}, bf16[4,256,256]{2,1,0:T(8,128)(2,1)S(1)}, u32[]{:S(2)}) copy-start(bf16[4,256,256]{2,1,0:T(8,128)(2,1)S(1)} %get-tuple-element.15.refs_2_) | copy-start | bytes 1572868
  67.5 49.3 %collective-permute-start.5 = (bf16[4,256,256]{2,1,0:T(8,128)(2,1)S(1)}, bf16[4,256,256]{2,1,0:T(8,128)(2,1)S(1)}, u32[]{:S(2)}, u32[]{:S(2)}) collective-permute-start(bf16[4,256,256]{2,1,0:T(8,128)(2,1)S(1)} %get-tuple-element.11.refs_1_), channel_id=1, source_target_pairs={{0,8},{1,9},{2,10},{3,11},{4,12},{5,13},{6,14},{7,15},{8,0},{9,1},... | collective-permute-start | bytes 1572872 | tf_op jit(solution)/shard_map/ppermute | solution.py:225
  104.0 14.8 %collective-permute-start.4 = (bf16[4,256,256]{2,1,0:T(8,128)(2,1)S(1)}, bf16[4,256,256]{2,1,0:T(8,128)(2,1)S(1)}, u32[]{:S(2)}, u32[]{:S(2)}) collective-permute-start(bf16[4,256,256]{2,1,0:T(8,128)(2,1)S(1)} %get-tuple-element.11.refs_1_), channel_id=1, source_target_pairs={{0,4},{1,5},{2,6},{3,7},{4,0},{5,1},{6,2},{7,3},{8,12},{9,13},{10,... | collective-permute-start | bytes 1572872 | tf_op jit(solution)/shard_map/ppermute | solution.py:225
  104.5 25.6 %collective-permute-start.25 = (bf16[4,256,256]{2,1,0:T(8,128)(2,1)S(1)}, bf16[4,256,256]{2,1,0:T(8,128)(2,1)S(1)}, u32[]{:S(2)}, u32[]{:S(2)}) collective-permute-start(bf16[4,256,256]{2,1,0:T(8,128)(2,1)S(1)} %get-tuple-element.10.refs_2_), channel_id=1, source_target_pairs={{0,4},{1,5},{2,6},{3,7},{4,0},{5,1},{6,2},{7,3},{8,12},{9,13},{10,... | collective-permute-start | bytes 1572872 | tf_op jit(solution)/shard_map/ppermute | solution.py:225
  106.1 24.5 %collective-permute-start.26 = (bf16[4,256,256]{2,1,0:T(8,128)(2,1)S(1)}, bf16[4,256,256]{2,1,0:T(8,128)(2,1)}, u32[]{:S(2)}, u32[]{:S(2)}) collective-permute-start(bf16[4,256,256]{2,1,0:T(8,128)(2,1)S(1)} %get-tuple-element.10.refs_2_), channel_id=1, source_target_pairs={{0,8},{1,9},{2,10},{3,11},{4,12},{5,13},{6,14},{7,15},{8,0},{9,1},... | collective-permute-start | bytes 1572872 | tf_op jit(solution)/shard_map/ppermute | solution.py:225
  116.8 22.1 %collective-permute-start.20 = (bf16[4,256,256]{2,1,0:T(8,128)(2,1)S(1)}, bf16[4,256,256]{2,1,0:T(8,128)(2,1)S(1)}, u32[]{:S(2)}, u32[]{:S(2)}) collective-permute-start(bf16[4,256,256]{2,1,0:T(8,128)(2,1)S(1)} %get-tuple-element.13.refs_1_), channel_id=1, source_target_pairs={{0,8},{1,9},{2,10},{3,11},{4,12},{5,13},{6,14},{7,15},{8,0},{9,1},... | collective-permute-start | bytes 1572872 | tf_op jit(solution)/shard_map/ppermute | solution.py:225
  118.8 22.6 %collective-permute-start.19 = (bf16[4,256,256]{2,1,0:T(8,128)(2,1)S(1)}, bf16[4,256,256]{2,1,0:T(8,128)(2,1)}, u32[]{:S(2)}, u32[]{:S(2)}) collective-permute-start(bf16[4,256,256]{2,1,0:T(8,128)(2,1)S(1)} %get-tuple-element.14.refs_2_), channel_id=1, source_target_pairs={{0,4},{1,5},{2,6},{3,7},{4,0},{5,1},{6,2},{7,3},{8,12},{9,13},{10,... | collective-permute-start | bytes 1572872 | tf_op jit(solution)/shard_map/ppermute | solution.py:225
  130.1 22.5 %collective-permute-start.18 = (bf16[4,256,256]{2,1,0:T(8,128)(2,1)S(1)}, bf16[4,256,256]{2,1,0:T(8,128)(2,1)S(1)}, u32[]{:S(2)}, u32[]{:S(2)}) collective-permute-start(bf16[4,256,256]{2,1,0:T(8,128)(2,1)S(1)} %get-tuple-element.13.refs_1_), channel_id=1, source_target_pairs={{0,4},{1,5},{2,6},{3,7},{4,0},{5,1},{6,2},{7,3},{8,12},{9,13},{10,... | collective-permute-start | bytes 1572872 | tf_op jit(solution)/shard_map/ppermute | solution.py:225
  130.6 32.2 %collective-permute-start.6 = (bf16[4,256,256]{2,1,0:T(8,128)(2,1)S(1)}, bf16[4,256,256]{2,1,0:T(8,128)(2,1)S(1)}, u32[]{:S(2)}, u32[]{:S(2)}) collective-permute-start(bf16[4,256,256]{2,1,0:T(8,128)(2,1)S(1)} %collective-permute-done.5.refs_5_), channel_id=1, source_target_pairs={{0,4},{1,5},{2,6},{3,7},{4,0},{5,1},{6,2},{7,3},{8,12},{9,13},{10,... | collective-permute-start | bytes 1572872 | tf_op jit(solution)/shard_map/ppermute | solution.py:225
  138.8 50.4 %collective-permute-start = (bf16[12,256,256]{2,1,0:T(8,128)(2,1)}, bf16[12,256,256]{2,1,0:T(8,128)(2,1)S(1)}, u32[]{:S(2)}, u32[]{:S(2)}) collective-permute-start(bf16[12,256,256]{2,1,0:T(8,128)(2,1)} %bitcast.21.q0), channel_id=1, source_target_pairs={{0,1},{1,0},{2,3},{3,2},{4,5},{5,4},{6,7},{7,6},{8,9},{9,8},{10,11... | collective-permute-start | bytes 4718600 | tf_op jit(solution)/shard_map/ppermute | solution.py:225
  138.8 52.5 %collective-permute-start.2 = (bf16[12,256,256]{2,1,0:T(8,128)(2,1)}, bf16[12,256,256]{2,1,0:T(8,128)(2,1)}, u32[]{:S(2)}, u32[]{:S(2)}) collective-permute-start(bf16[12,256,256]{2,1,0:T(8,128)(2,1)} %collective-permute-done.1.q2), channel_id=1, source_target_pairs={{0,1},{1,0},{2,3},{3,2},{4,5},{5,4},{6,7},{7,6},{8,9},{9,8},{10,11... | collective-permute-start | bytes 4718600 | tf_op jit(solution)/shard_map/ppermute | solution.py:225
  141.4 21.7 %collective-permute-start.21 = (bf16[4,256,256]{2,1,0:T(8,128)(2,1)S(1)}, bf16[4,256,256]{2,1,0:T(8,128)(2,1)S(1)}, u32[]{:S(2)}, u32[]{:S(2)}) collective-permute-start(bf16[4,256,256]{2,1,0:T(8,128)(2,1)S(1)} %get-tuple-element.14.refs_2_), channel_id=1, source_target_pairs={{0,8},{1,9},{2,10},{3,11},{4,12},{5,13},{6,14},{7,15},{8,0},{9,1},... | collective-permute-start | bytes 1572872 | tf_op jit(solution)/shard_map/ppermute | solution.py:225
  152.6 12.1 %collective-permute-start.12 = (bf16[4,256,256]{2,1,0:T(8,128)(2,1)S(1)}, bf16[4,256,256]{2,1,0:T(8,128)(2,1)}, u32[]{:S(2)}, u32[]{:S(2)}) collective-permute-start(bf16[4,256,256]{2,1,0:T(8,128)(2,1)S(1)} %get-tuple-element.12.refs_1_), channel_id=1, source_target_pairs={{0,8},{1,9},{2,10},{3,11},{4,12},{5,13},{6,14},{7,15},{8,0},{9,1},... | collective-permute-start | bytes 1572872 | tf_op jit(solution)/shard_map/ppermute | solution.py:225
  162.8 15.0 %collective-permute-start.11 = (bf16[4,256,256]{2,1,0:T(8,128)(2,1)S(1)}, bf16[4,256,256]{2,1,0:T(8,128)(2,1)}, u32[]{:S(2)}, u32[]{:S(2)}) collective-permute-start(bf16[4,256,256]{2,1,0:T(8,128)(2,1)S(1)} %get-tuple-element.15.refs_2_), channel_id=1, source_target_pairs={{0,4},{1,5},{2,6},{3,7},{4,0},{5,1},{6,2},{7,3},{8,12},{9,13},{10,... | collective-permute-start | bytes 1572872 | tf_op jit(solution)/shard_map/ppermute | solution.py:225
  163.1 14.6 %collective-permute-start.27 = (bf16[4,256,256]{2,1,0:T(8,128)(2,1)S(1)}, bf16[4,256,256]{2,1,0:T(8,128)(2,1)S(1)}, u32[]{:S(2)}, u32[]{:S(2)}) collective-permute-start(bf16[4,256,256]{2,1,0:T(8,128)(2,1)S(1)} %collective-permute-done.25.refs_4_), channel_id=1, source_target_pairs={{0,8},{1,9},{2,10},{3,11},{4,12},{5,13},{6,14},{7,15},{8,0},{9,1},... | collective-permute-start | bytes 1572872 | tf_op jit(solution)/shard_map/ppermute | solution.py:225
  164.7 24.2 %collective-permute-start.22 = (bf16[4,256,256]{2,1,0:T(8,128)(2,1)S(1)}, bf16[4,256,256]{2,1,0:T(8,128)(2,1)S(1)}, u32[]{:S(2)}, u32[]{:S(2)}) collective-permute-start(bf16[4,256,256]{2,1,0:T(8,128)(2,1)S(1)} %collective-permute-done.20.refs_5_), channel_id=1, source_target_pairs={{0,4},{1,5},{2,6},{3,7},{4,0},{5,1},{6,2},{7,3},{8,12},{9,13},{10,... | collective-permute-start | bytes 1572872 | tf_op jit(solution)/shard_map/ppermute | solution.py:225
  177.7 13.3 %collective-permute-start.7 = (bf16[4,256,256]{2,1,0:T(8,128)(2,1)S(1)}, bf16[4,256,256]{2,1,0:T(8,128)(2,1)S(1)}, u32[]{:S(2)}, u32[]{:S(2)}) collective-permute-start(bf16[4,256,256]{2,1,0:T(8,128)(2,1)S(1)} %pad_maximum_fusion.mine), channel_id=1, source_target_pairs={{0,1},{1,0},{2,3},{3,2},{4,5},{5,4},{6,7},{7,6},{8,9},{9,8},{10,11... | collective-permute-start | bytes 1572872 | tf_op jit(solution)/shard_map/ppermute | solution.py:225
  177.7 106.3 %collective-permute-start.10 = (bf16[4,256,256]{2,1,0:T(8,128)(2,1)S(1)}, bf16[4,256,256]{2,1,0:T(8,128)(2,1)}, u32[]{:S(2)}, u32[]{:S(2)}) collective-permute-start(bf16[4,256,256]{2,1,0:T(8,128)(2,1)S(1)} %get-tuple-element.12.refs_1_), channel_id=1, source_target_pairs={{0,4},{1,5},{2,6},{3,7},{4,0},{5,1},{6,2},{7,3},{8,12},{9,13},{10,... | collective-permute-start | bytes 1572872 | tf_op jit(solution)/shard_map/ppermute | solution.py:225
  188.9 61.5 %collective-permute-start.23 = (bf16[4,256,256]{2,1,0:T(8,128)(2,1)}, bf16[4,256,256]{2,1,0:T(8,128)(2,1)}, u32[]{:S(2)}, u32[]{:S(2)}) collective-permute-start(bf16[4,256,256]{2,1,0:T(8,128)(2,1)} %collective-permute-done.19.refs_4_), channel_id=1, source_target_pairs={{0,8},{1,9},{2,10},{3,11},{4,12},{5,13},{6,14},{7,15},{8,0},{9,1},... | collective-permute-start | bytes 1572872 | tf_op jit(solution)/shard_map/ppermute | solution.py:225
  189.2 94.9 %collective-permute-start.13 = (bf16[4,256,256]{2,1,0:T(8,128)(2,1)S(1)}, bf16[4,256,256]{2,1,0:T(8,128)(2,1)}, u32[]{:S(2)}, u32[]{:S(2)}) collective-permute-start(bf16[4,256,256]{2,1,0:T(8,128)(2,1)S(1)} %get-tuple-element.15.refs_2_), channel_id=1, source_target_pairs={{0,8},{1,9},{2,10},{3,11},{4,12},{5,13},{6,14},{7,15},{8,0},{9,1},... | collective-permute-start | bytes 1572872 | tf_op jit(solution)/shard_map/ppermute | solution.py:225
  191.0 93.1 %collective-permute-start.14 = (bf16[4,256,256]{2,1,0:T(8,128)(2,1)}, bf16[4,256,256]{2,1,0:T(8,128)(2,1)}, u32[]{:S(2)}, u32[]{:S(2)}) collective-permute-start(bf16[4,256,256]{2,1,0:T(8,128)(2,1)} %collective-permute-done.12.refs_5_), channel_id=1, source_target_pairs={{0,4},{1,5},{2,6},{3,7},{4,0},{5,1},{6,2},{7,3},{8,12},{9,13},{10,... | collective-permute-start | bytes 1572872 | tf_op jit(solution)/shard_map/ppermute | solution.py:225
  191.8 92.3 %collective-permute-start.15 = (bf16[4,256,256]{2,1,0:T(8,128)(2,1)}, bf16[4,256,256]{2,1,0:T(8,128)(2,1)}, u32[]{:S(2)}, u32[]{:S(2)}) collective-permute-start(bf16[4,256,256]{2,1,0:T(8,128)(2,1)} %collective-permute-done.11.refs_4_), channel_id=1, source_target_pairs={{0,8},{1,9},{2,10},{3,11},{4,12},{5,13},{6,14},{7,15},{8,0},{9,1},... | collective-permute-start | bytes 1572872 | tf_op jit(solution)/shard_map/ppermute | solution.py:225
  (19 other events, 831.5 us)

commit v2 on v0

--- a/solution.py
+++ b/solution.py
@@ -1,7 +1,15 @@
 import jax
 import jax.numpy as jnp
 from jax import lax
+from jax.experimental import pallas as pl
+from jax.experimental.pallas import tpu as pltpu
 from jax.sharding import PartitionSpec as P
+
+F32 = jnp.float32
+BF16 = jnp.bfloat16
+LANES = 128
+SUB = 8
+VMEM_LIMIT = 60 * 1024 * 1024
 
 
 def from_root(value, axis, source):
@@ -32,7 +40,7 @@
     return gathered.reshape(-1, gathered.shape[-1])
 
 
-def local(matrix, inv_first, inv_second):
+def local_any(matrix, inv_first, inv_second):
     row_count = lax.axis_size("row")
     col_count = lax.axis_size("col")
     row_id = lax.axis_index("row")
@@ -83,12 +91,368 @@
     return (panels.reshape(tile_rows, 1, tile_size, 2 * width), trailing.reshape(matrix.shape))
 
 
+def dot(left, right):
+    return lax.dot_general(left, right, (((1,), (0,)), ((), ())), preferred_element_type=F32)
+
+
+def link_kernel(ids, mine, other, inv0t, low, lowt):
+    slot, plane, core = ids[0] % 4, ids[1] // 2, ids[1] % 2
+    tile = mine.shape[1]
+
+    def piece(panel_tile, owner):
+        held = slot ^ panel_tile
+        return jnp.where(core == owner, mine[held].astype(F32), other[held].astype(F32))
+
+    @pl.when(plane == 0)
+    def _():
+        rows = [jnp.concatenate([piece(2 + i, j) for j in range(2)], axis=1) for i in range(2)]
+        block = jnp.concatenate(rows, axis=0)
+        result = dot(block.astype(BF16), inv0t[...])
+        low[...] = result.astype(BF16)
+        lowt[...] = result.T.astype(BF16)
+
+    @pl.when(plane == 1)
+    def _():
+        rows = [jnp.concatenate([piece(j, i) for i in range(2)], axis=1) for j in range(2)]
+        block = jnp.concatenate(rows, axis=0).T
+        result = dot(block.astype(BF16), inv0t[...])
+        low[...] = result.astype(BF16)
+        lowt[...] = result.T.astype(BF16)
+
+
+def rows_kernel(ids, strips, inv0t, inv1t, lowt, out, buf):
+    _, count, tile, _ = strips.shape
+    width = 2 * tile
+    row_id = ids[0]
+    for k in range(4):
+        for i in range(count):
+            buf[i * tile : (i + 1) * tile, k * tile : (k + 1) * tile] = strips[k, i]
+    local = lax.broadcasted_iota(jnp.int32, (count * tile, 1), 0) // tile
+    tile_row = (pl.program_id(0) * count + local) * 8 + row_id
+    first = dot(buf[:, :width], inv0t[...])
+    first = jnp.where(tile_row >= 2, first, 0.0).astype(BF16)
+    rest = (buf[:, width:].astype(F32) - dot(first, lowt[...])).astype(BF16)
+    second = dot(rest, inv1t[...])
+    second = jnp.where(tile_row >= 4, second, 0.0).astype(BF16)
+    for i in range(count):
+        out[i, :, :width] = first[i * tile : (i + 1) * tile]
+        out[i, :, width:] = second[i * tile : (i + 1) * tile]
+
+
+def cols_kernel(start, stride, ids, p0, p1, p2, p3, inv0, inv1, low, out, raw):
+    count, tile, _ = p0.shape
+    width = 2 * tile
+    row_id, col_id = ids[0], ids[1]
+    for m, ref in enumerate((p0, p1, p2, p3)):
+        base = pl.multiple_of(((row_id % 4) ^ m) * tile, tile)
+        for i in range(count):
+            raw[pl.ds(base, tile), i * tile : (i + 1) * tile] = ref[i]
+    local = lax.broadcasted_iota(jnp.int32, (1, count * tile), 1) // tile
+    tile_col = (start + (pl.program_id(0) * count + local) * stride) * 4 + col_id
+    first = dot(inv0[...], raw[:width])
+    first = jnp.where(tile_col >= 2, first, 0.0).astype(BF16)
+    rest = (raw[width:].astype(F32) - dot(low[...], first)).astype(BF16)
+    second = dot(inv1[...], rest)
+    second = jnp.where(tile_col >= 4, second, 0.0).astype(BF16)
+    for i in range(count):
+        out[i, :width] = first[:, i * tile : (i + 1) * tile]
+        out[i, width:] = second[:, i * tile : (i + 1) * tile]
+
+
+def zeros_kernel(_, out):
+    out[...] = jnp.zeros_like(out)
+
+
+def update_kernel(group, start, ids, even, odd, factor, matrix, _, out, acc):
+    tile = factor.shape[1]
+    row_id, col_id = ids[0], ids[1]
+    tile_row = (start + pl.program_id(0)) * 8 + row_id
+    end = jnp.where(tile_row >= 4, (tile_row - col_id) // 4 + 1 - group * SUB, 0)
+    begin = 1 if group == 0 else 0
+    held = [(odd if s % 2 else even, s // 2) for s in range(SUB)]
+
+    @pl.when(end <= begin)
+    def _():
+        out[...] = jnp.zeros_like(out)
+
+    @pl.when(end > begin)
+    def _():
+        def fill(chosen):
+            for s in chosen:
+                ref, at = held[s]
+                product = dot(factor[0], ref[at])
+                for part in range(tile // LANES):
+                    lanes = slice(part * LANES, (part + 1) * LANES)
+                    acc[part, pl.ds(s, tile, stride=SUB), :] = product[:, lanes]
+
+        @pl.when(end >= SUB)
+        def _():
+            fill(range(begin, SUB))
+
+        for pair in range(0, len(held), 2):
+
+            @pl.when((end < SUB) & (pair < end))
+            def _(pair=pair):
+                fill(range(max(pair, begin), pair + 2))
+
+        some = 32
+        sub = lax.broadcasted_iota(jnp.int32, (some, SUB, LANES), 1)
+        keep = (sub >= begin) & (sub < end)
+
+        def finish(i, carry):
+            at = pl.multiple_of(i * some, some)
+            span = pl.ds(pl.multiple_of(at * SUB, some * SUB), some * SUB)
+            for part in range(tile // LANES):
+                lanes = slice(part * LANES, (part + 1) * LANES)
+                product = acc[part, span, :].reshape(some, SUB, LANES)
+                value = matrix[0, pl.ds(at, some), :, lanes].astype(F32) - product
+                out[0, pl.ds(at, some), :, lanes] = jnp.where(keep, value, 0.0).astype(BF16)
+            return carry
+
+        lax.fori_loop(0, tile // some, finish, 0)
+
+
+def params():
+    return pltpu.CompilerParams(vmem_limit_bytes=VMEM_LIMIT)
+
+
+def whole(array):
+    rank = array.ndim
+    return pl.BlockSpec(array.shape, lambda *_: (0,) * rank)
+
+
+def local(matrix, inv_first, inv_second):
+    row_id = lax.axis_index("row")
+    col_id = lax.axis_index("col")
+    ids = jnp.stack([row_id, col_id]).astype(jnp.int32)
+    tiles, _, tile, tile_cols, _, _ = matrix.shape
+    width = inv_first.shape[0]
+    groups = tile_cols // SUB
+    ratio = tiles // groups
+    view = matrix.reshape(tiles, tile, tile_cols, tile)
+    upper = row_id >= 4
+    smem = pl.BlockSpec(memory_space=pltpu.SMEM)
+    inv0t, inv1t = inv_first.T, inv_second.T
+
+    def together(*values):
+        return lax.optimization_barrier(values)
+
+    def move(value, target):
+        pairs = []
+        for r in range(8):
+            for c in range(4):
+                to = target(r, c)
+                if to is not None:
+                    pairs.append((r * 4 + c, to[0] * 4 + to[1]))
+        return lax.ppermute(value, ("row", "col"), pairs)
+
+    def across_z(value):
+        return move(value, lambda r, c: (r ^ 2, c))
+
+    def across_y(value):
+        return move(value, lambda r, c: (r ^ 1, c))
+
+    def across_core(value):
+        return move(value, lambda r, c: (r, c ^ 1))
+
+    def lift(value):
+        return move(value, lambda r, c: (r + 4, c) if r < 4 else None)
+
+    def factor_link(mine, other):
+        square = jax.ShapeDtypeStruct((width, width), BF16)
+        return pl.pallas_call(
+            link_kernel,
+            in_specs=[smem, whole(mine), whole(other), whole(inv0t)],
+            out_specs=[whole(square), whole(square)],
+            out_shape=[square, square],
+            grid=(1,),
+            compiler_params=params(),
+            name="link",
+        )(ids, mine, other, inv0t)
+
+    def factor_rows(strips, lowt):
+        count = 2
+        block = pl.BlockSpec((4, count, tile, tile), lambda t: (0, t, 0, 0))
+        return pl.pallas_call(
+            rows_kernel,
+            grid=(tiles // count,),
+            in_specs=[smem, block, whole(inv0t), whole(inv1t), whole(lowt)],
+            out_specs=pl.BlockSpec((count, tile, 2 * width), lambda t: (t, 0, 0)),
+            out_shape=jax.ShapeDtypeStruct((tiles, tile, 2 * width), BF16),
+            scratch_shapes=[pltpu.VMEM((count * tile, 2 * width), BF16)],
+            compiler_params=params(),
+            cost_estimate=cost(tiles * 6 * tile * width * width, 24 * tiles * tile * tile),
+            name="rows",
+        )(ids, strips, inv0t, inv1t, lowt)
+
+    def factor_cols(start, pieces, low):
+        total = pieces[0].shape[0]
+        count = 2
+        block = pl.BlockSpec((count, tile, tile), lambda s: (s, 0, 0))
+
+        def kernel(*refs):
+            cols_kernel(start, 2, *refs)
+
+        return pl.pallas_call(
+            kernel,
+            grid=(total // count,),
+            in_specs=[smem, *[block] * 4, whole(inv_first), whole(inv_second), whole(low)],
+            out_specs=pl.BlockSpec((count, 2 * width, tile), lambda s: (s, 0, 0)),
+            out_shape=jax.ShapeDtypeStruct((total, 2 * width, tile), BF16),
+            scratch_shapes=[pltpu.VMEM((2 * width, count * tile), BF16)],
+            compiler_params=params(),
+            cost_estimate=cost(total * 6 * tile * width * width, 24 * total * tile * tile),
+            name="cols_%d" % start,
+        )(ids, *pieces, inv_first, inv_second, low)
+
+    def cost(flops, size):
+        return pl.CostEstimate(flops=flops, bytes_accessed=size, transcendentals=0)
+
+    def clear(gate):
+        def place(i):
+            group, first = 1, 0
+            for g in range(1, groups):
+                begin = ratio * g * (g - 1) // 2
+                group = jnp.where(i >= begin, g, group)
+                first = jnp.where(i >= begin, begin, first)
+            return (i - first, 0, group, 0)
+
+        return pl.pallas_call(
+            zeros_kernel,
+            grid=(ratio * groups * (groups - 1) // 2,),
+            in_specs=[smem],
+            out_specs=pl.BlockSpec((1, tile, SUB, tile), place),
+            out_shape=jax.ShapeDtypeStruct(view.shape, BF16),
+            compiler_params=params(),
+            cost_estimate=cost(0, tiles * tile * SUB * tile * 2),
+            name="clear",
+        )(together(ids, gate)[0])
+
+    def update(result, group, start, stop, cols, panels):
+        grid_block = pl.BlockSpec((1, tile, SUB, tile), lambda t: (t + start, 0, group, 0))
+
+        def kernel(*refs):
+            update_kernel(group, start, *refs)
+
+        return pl.pallas_call(
+            kernel,
+            grid=(stop - start,),
+            in_specs=[
+                smem,
+                *[whole(part) for part in cols],
+                pl.BlockSpec((1, tile, 2 * width), lambda t: (t + start, 0, 0)),
+                grid_block,
+                pl.BlockSpec(memory_space=pl.ANY),
+            ],
+            out_specs=grid_block,
+            out_shape=jax.ShapeDtypeStruct(view.shape, BF16),
+            scratch_shapes=[pltpu.VMEM((tile // LANES, tile * SUB, LANES), F32)],
+            input_output_aliases={len(cols) + 3: 0},
+            compiler_params=params(),
+            cost_estimate=cost(
+                (stop - start) * 2 * tile * tile * 2 * width * SUB,
+                (stop - start) * 6 * tile * tile * SUB,
+            ),
+            name="update_%d_%d" % (group, start),
+        )(ids, *cols, panels, view, result)
+
+    def cross(value):
+        return move(value, lambda r, c: (4 + c, r - 4) if r >= 4 else None)
+
+    count = 2 * groups
+    half = SUB // 2
+    held = jnp.swapaxes(view[0], 0, 1)
+    own = [held[i // 2 * SUB + i % 2 : (i // 2 + 1) * SUB : 2] for i in range(count)]
+    up, base, ez, ey, ed, cols = ([None] * count for _ in range(6))
+
+    def begin(i, token):
+        got, token = together(up[i], token)
+        base[i] = jnp.where(upper, got, own[i])
+        ez[i], ey[i] = across_z(base[i]), across_y(base[i])
+        return token
+
+    def raise_after(i, gate):
+        source, gate = together(own[i], gate)
+        up[i] = lift(source)
+        return gate
+
+    def cross_after(i, gate):
+        source, gate = together(swapped[i // 2 * half : (i // 2 + 1) * half], gate)
+        up[i] = cross(source)
+        return gate
+
+    def forward(i, token):
+        ez[i], token = together(ez[i], token)
+        ed[i] = across_y(ez[i])
+        return token
+
+    def make_cols(i, gate):
+        parts = together(base[i], ey[i], ez[i], ed[i], gate)
+        cols[i] = factor_cols(i // 2 * SUB + i % 2, parts[:4], low)
+
+    up[0] = lift(own[0])
+    source, own[0] = together(view, own[0])
+    strip = source[:, :, 0, :]
+    swapped = jnp.swapaxes(strip, 1, 2)
+    strips = lax.all_gather(strip, "col")
+    up[1] = cross(swapped[:half])
+    up[0] = raise_after(2, up[0])
+    begin(0, ids)
+    up[1] = cross_after(3, up[1])
+    result = clear(base[0])
+    ey[0] = forward(0, ey[0])
+    up[2] = raise_after(4, up[2])
+    begin(1, base[0])
+    up[3] = cross_after(5, up[3])
+    mine = jnp.stack([p[0] for p in (base[0], ey[0], ez[0], ed[0])])
+    other = across_core(mine)
+    base[1] = begin(2, base[1])
+    base[2] = forward(1, base[2])
+    low, lowt = factor_link(mine, other)
+    low = begin(3, low)
+    make_cols(0, base[3])
+    cols[0] = forward(2, cols[0])
+    make_cols(1, ez[2])
+    cols[1] = begin(4, cols[1])
+    lowt, base[4] = together(lowt, base[4])
+    panels = factor_rows(strips, lowt)
+    panels = forward(3, panels)
+    result, ez[3] = together(result, ez[3])
+    middle = tiles // 2
+    result = update(result, 0, 0, middle, cols[0:2], panels)
+    result = begin(5, result)
+    base[5] = forward(4, base[5])
+    make_cols(2, base[5])
+    result, cols[2] = together(result, cols[2])
+    result = update(result, 0, middle, tiles, cols[0:2], panels)
+    ey[5], result = together(ey[5], result)
+    ed[5] = across_z(ey[5])
+    make_cols(3, ey[5])
+    result, cols[3] = together(result, cols[3])
+    result = update(result, 1, ratio, tiles, cols[2:4], panels)
+    ed[4], result = together(ed[4], result)
+    make_cols(4, base[5])
+    ed[5], cols[4] = together(ed[5], cols[4])
+    make_cols(5, base[5])
+    result = update(result, 2, 2 * ratio, tiles, cols[4:6], panels)
+    return panels.reshape(tiles, 1, tile, 2 * width), result.reshape(matrix.shape)
+
+
+def fits(mesh, matrix, inv_first):
+    tiles_match = matrix.shape[3] == 3 * SUB and matrix.shape[0] == 12
+    panel_match = inv_first.shape[0] == 2 * matrix.shape[2]
+    return mesh.shape["row"] == 8 and mesh.shape["col"] == 4 and tiles_match and panel_match
+
+
 def solution(mesh):
-    placed = (P(None, "row", None, None, "col", None), P(), P())
+    def body(matrix, inv_first, inv_second):
+        plan = local if fits(mesh, matrix, inv_first) else local_any
+        return plan(matrix, inv_first, inv_second)
+
     return jax.shard_map(
-        local,
+        body,
         mesh=mesh,
-        in_specs=placed,
+        in_specs=(P(None, "row", None, None, "col", None), P(), P()),
         out_specs=(P(None, "row", None, None), P(None, "row", None, None, "col", None)),
         check_vma=False,
     )

time: 728 us -> 270 us (0.37)
  waiting for transfers between devices: 558 us -> 30.1 us
  Pallas kernels: 0 us -> 105 us
  matrix products: 81 us -> 0 us
  starting transfers between devices: 0.34 us -> 78 us
  local copies, waits for them, and re-layouts: 51.7 us -> 30.5 us
  other arithmetic: 22.9 us -> 7.39 us
    psum x4 -> x0, waiting for transfers between devices: 558 us -> none  [from_root(): return lax.psum(kept, axis)]
    pallas_call x0 -> x13, Pallas kernels: none -> 105 us  [the longest x4 53.4 us: update(): pl.pallas_call(kernel, grid=(stop - start,), in_specs=[smem, *[whole(part...]
    dot_general x4 -> x0, matrix products: 81 us -> none  [the longest x2 68.3 us: outer_minus(): lax.dot_general(left_rows, right_rows, (((1,), (1,)), ((), ())), preferre...]
    ppermute x0 -> x25, starting transfers between devices: none -> 78 us  [move(): return lax.ppermute(value, ('row', 'col'), pairs)]
    unnamed x10 -> x21, local copies, waits for them, and re-layouts: 51.7 us -> 8.89 us
    ppermute x0 -> x25, waiting for transfers between devices: none -> 30.1 us  [move(): return lax.ppermute(value, ('row', 'col'), pairs)]
    slice x0 -> x10, local copies, waits for them, and re-layouts: none -> 16.7 us  [the longest x2 8.35 us: local(): strip = source[:, :, 0, :]]
    another operation x2, other arithmetic: 9.62 us -> 1.65 us  [the longest x1 0.98 us: local(): mine = jnp.stack([p[0] for p in (base[0], ey[0], ez[0], ed[0])])]
  transfers between devices with their start and end apart: 4 -> 26, of which waited for: 4 -> 8; matrix products, arithmetic and copies ran while one was open for 1% -> 8% of each run, Pallas kernels for 0% -> 34%
where the time goes in v2:
time: 270 us; the launch traced here: 265 us
  Pallas kernels  105 us (39%)
  starting transfers between devices  78 us (29%)
  local copies, waits for them, and re-layouts  30.5 us (11%)
  waiting for transfers between devices  30.1 us (11%)
  between operations  14.2 us (5%)
  other arithmetic  7.39 us (3%)
    ppermute x25, starting transfers between devices, move(): return lax.ppermute(value, ('row', 'col'), pairs)  78 us
    pallas_call x4, Pallas kernels, update(): pl.pallas_call(kernel, grid=(stop - start,), in_specs=[smem, *[whole(part...  53.4 us
    pallas_call x6, Pallas kernels, factor_cols(): pl.pallas_call(kernel, grid=(total // count,), in_specs=[smem, *[block] *...  31.4 us
    ppermute x25, waiting for transfers between devices, move(): return lax.ppermute(value, ('row', 'col'), pairs)  30.1 us
    pallas_call x1, Pallas kernels, factor_rows(): pl.pallas_call(rows_kernel, grid=(tiles // count,), in_specs=[smem, block...  10.1 us
    unnamed x21, local copies, waits for them, and re-layouts  8.89 us
    slice x2, local copies, waits for them, and re-layouts, local(): strip = source[:, :, 0, :]  8.35 us
    pallas_call x1, Pallas kernels, clear(): pl.pallas_call(zeros_kernel, grid=(ratio * groups * (groups - 1) // 2,),...  7.26 us
  transfers between devices with their start and end apart: 26, of which 8 were waited for; matrix products, arithmetic and copies ran while one was open for 8% of the time, Pallas kernels for 34%

profile of v2, /device:TPU:0, one launch (start us, length us, event | category | flops | bytes accessed | tf_op | source)
XLA Modules:
  0.0 265.3 jit_solution(8938319955235854469)
XLA Ops:
  11.8 6.9 %slice.48 = bf16[12,256,1,256]{3,2,1,0:T(2,128)(2,1)S(1)} slice(bf16[12,256,24,256]{3,2,1,0:T(8,128)(2,1)} %bitcast.21), slice={[0:12], [0:256], [0:1], [0:256]} | slice | bytes 3145728 | tf_op jit(solution)/shard_map/slice | solution.py:395
  20.2 6.8 %collective-permute-start.2 = (bf16[4,256,256]{2,1,0:T(8,128)(2,1)}, bf16[4,256,256]{2,1,0:T(8,128)(2,1)}, u32[]{:S(2)}, u32[]{:S(2)}) collective-permute-start(bf16[4,256,256]{2,1,0:T(8,128)(2,1)} %get-tuple-element.78), channel_id=1, source_target_pairs={{0,16},{1,17},{2,18},{3,19},{4,20},{5,21},{6,22},{7,23},{8,24},{9,... | collective-permute-start | bytes 1572872 | tf_op jit(solution)/shard_map/ppermute | solution.py:247
  27.6 10.1 %collective-permute-done.2 = bf16[4,256,256]{2,1,0:T(8,128)(2,1)} collective-permute-done((bf16[4,256,256]{2,1,0:T(8,128)(2,1)}, bf16[4,256,256]{2,1,0:T(8,128)(2,1)}, u32[]{:S(2)}, u32[]{:S(2)}) %collective-permute-start.2) | collective-permute-done | bytes 524320 | tf_op jit(solution)/shard_map/ppermute | solution.py:247
  39.6 12.7 %collective-permute-start.3 = (bf16[4,256,256]{2,1,0:T(8,128)(2,1)}, bf16[4,256,256]{2,1,0:T(8,128)(2,1)}, u32[]{:S(2)}, u32[]{:S(2)}) collective-permute-start(bf16[4,256,256]{2,1,0:T(8,128)(2,1)} %broadcast_select_fusion.2.refs_1_), channel_id=1, source_target_pairs={{0,8},{1,9},{2,10},{3,11},{4,12},{5,13},{6,14},{7,15},{8,0},{9,1},... | collective-permute-start | bytes 1572872 | tf_op jit(solution)/shard_map/ppermute | solution.py:247
  53.7 4.9 %copy.53 = bf16[12,256,1,256]{1,3,0,2:T(8,128)(2,1)} copy(bf16[12,256,1,256]{3,2,1,0:T(2,128)(2,1)S(1)} %slice.48) | data formatting | bytes 3145728 | tf_op jit(solution)/shard_map/squeeze | solution.py:395
  58.7 2.6 fusion.1
  62.0 2.7 %collective-permute-done.3.refs_3_ = bf16[4,256,256]{2,1,0:T(8,128)(2,1)} collective-permute-done((bf16[4,256,256]{2,1,0:T(8,128)(2,1)}, bf16[4,256,256]{2,1,0:T(8,128)(2,1)}, u32[]{:S(2)}, u32[]{:S(2)}) %collective-permute-start.3) | collective-permute-done | bytes 524320 | tf_op jit(solution)/shard_map/ppermute | solution.py:247
  68.5 6.8 %collective-permute-start.8 = (bf16[4,256,256]{2,1,0:T(8,128)(2,1)}, bf16[4,256,256]{2,1,0:T(8,128)(2,1)}, u32[]{:S(2)}, u32[]{:S(2)}) collective-permute-start(bf16[4,256,256]{2,1,0:T(8,128)(2,1)} %get-tuple-element.84), channel_id=1, source_target_pairs={{0,16},{1,17},{2,18},{3,19},{4,20},{5,21},{6,22},{7,23},{8,24},{9,... | collective-permute-start | bytes 1572872 | tf_op jit(solution)/shard_map/ppermute | solution.py:247
  80.0 5.3 %collective-permute-start.6 = (bf16[4,256,256]{2,1,0:T(8,128)(2,1)}, bf16[4,256,256]{2,1,0:T(8,128)(2,1)}, u32[]{:S(2)}, u32[]{:S(2)}) collective-permute-start(bf16[4,256,256]{2,1,0:T(8,128)(2,1)} %pad_maximum_fusion.mine), channel_id=1, source_target_pairs={{0,1},{1,0},{2,3},{3,2},{4,5},{5,4},{6,7},{7,6},{8,9},{9,8},{10,11... | collective-permute-start | bytes 1572872 | tf_op jit(solution)/shard_map/ppermute | solution.py:247
  86.4 15.2 %collective-permute-start.11 = (bf16[4,256,256]{2,1,0:T(8,128)(2,1)}, bf16[4,256,256]{2,1,0:T(8,128)(2,1)}, u32[]{:S(2)}, u32[]{:S(2)}) collective-permute-start(bf16[4,256,256]{2,1,0:T(8,128)(2,1)} %get-tuple-element.98.refs_1_), channel_id=1, source_target_pairs={{0,8},{1,9},{2,10},{3,11},{4,12},{5,13},{6,14},{7,15},{8,0},{9,1},... | collective-permute-start | bytes 1572872 | tf_op jit(solution)/shard_map/ppermute | solution.py:247
  101.6 2.0 copy.48
  103.7 2.9 %link.1 = (bf16[512,512]{1,0:T(8,128)(2,1)}, bf16[512,512]{1,0:T(8,128)(2,1)}) custom-call(s32[2]{0:T(128)} %pad_add_fusion.ids.refs_0_._, bf16[4,256,256]{2,1,0:T(8,128)(2,1)} %pad_maximum_fusion.mine, bf16[4,256,256]{2,1,0:T(8,128)(2,1)} %collective-permute-done.6.other, bf16[512,512]{1,0:T(8,128)(2,1)} %bitcast.33), custom_call_target="tpu_custom_call" | custom-call | tf_op jit(solution)/shard_map/link/pallas_call | solution.py:263
  107.7 3.8 %collective-permute-start.13 = (bf16[4,256,256]{2,1,0:T(8,128)(2,1)}, bf16[4,256,256]{2,1,0:T(8,128)(2,1)}, u32[]{:S(2)}, u32[]{:S(2)}) collective-permute-start(bf16[4,256,256]{2,1,0:T(8,128)(2,1)} %get-tuple-element.115.refs_1_), channel_id=1, source_target_pairs={{0,8},{1,9},{2,10},{3,11},{4,12},{5,13},{6,14},{7,15},{8,0},{9,1},... | collective-permute-start | bytes 1572872 | tf_op jit(solution)/shard_map/ppermute | solution.py:247
  111.4 3.2 %collective-permute-done.11.refs_3_ = bf16[4,256,256]{2,1,0:T(8,128)(2,1)} collective-permute-done((bf16[4,256,256]{2,1,0:T(8,128)(2,1)}, bf16[4,256,256]{2,1,0:T(8,128)(2,1)}, u32[]{:S(2)}, u32[]{:S(2)}) %collective-permute-start.11) | collective-permute-done | bytes 524320 | tf_op jit(solution)/shard_map/ppermute | solution.py:247
  115.2 9.1 %collective-permute-start.9 = (bf16[4,256,256]{2,1,0:T(8,128)(2,1)}, bf16[4,256,256]{2,1,0:T(8,128)(2,1)}, u32[]{:S(2)}, u32[]{:S(2)}) collective-permute-start(bf16[4,256,256]{2,1,0:T(8,128)(2,1)} %get-tuple-element.85), channel_id=1, source_target_pairs={{0,16},{1,17},{2,18},{3,19},{4,20},{5,21},{6,22},{7,23},{8,24},{9,... | collective-permute-start | bytes 1572872 | tf_op jit(solution)/shard_map/ppermute | solution.py:247
  124.3 2.1 copy.50
  126.4 7.3 %clear.1.refs_5_ = bf16[12,256,24,256]{3,2,1,0:T(8,128)(2,1)} custom-call(s32[2]{0:T(128)} %pad_add_fusion.ids.refs_0_._), custom_call_target="tpu_custom_call" | custom-call | bytes 12582912 | tf_op jit(solution)/shard_map/clear/pallas_call | solution.py:320
  135.1 5.3 %cols_0.1.refs_1_ = bf16[4,1024,256]{2,1,0:T(8,128)(2,1)} custom-call(s32[2]{0:T(128)} %pad_add_fusion.ids.refs_0_._, bf16[4,256,256]{2,1,0:T(8,128)(2,1)} %broadcast_select_fusion.2.refs_1_, bf16[4,256,256]{2,1,0:T(8,128)(2,1)} %collective-permute-done.4.refs_2_, bf16[4,256,256]{2,1,0:T(8,128)(2,1)} %collective-permute-done.3.refs_3_, ...), custom_call_target="tpu_custom_call" | custom-call | flops 1610612736 | bytes 6291456 | tf_op jit(solution)/shard_map/cols_0/pallas_call | solution.py:296
  141.0 2.0 collective-permute-start.16
  143.1 5.2 %cols_1.1.refs_2_ = bf16[4,1024,256]{2,1,0:T(8,128)(2,1)} custom-call(s32[2]{0:T(128)} %pad_add_fusion.ids.refs_0_._, bf16[4,256,256]{2,1,0:T(8,128)(2,1)} %get-tuple-element.98.refs_1_, bf16[4,256,256]{2,1,0:T(8,128)(2,1)} %collective-permute-done.10.refs_2_, bf16[4,256,256]{2,1,0:T(8,128)(2,1)} %collective-permute-done.11.refs_3_, ...), custom_call_target="tpu_custom_call" | custom-call | flops 1610612736 | bytes 6291456 | tf_op jit(solution)/shard_map/cols_1/pallas_call | solution.py:296
  151.2 10.1 %rows.1.refs_3_ = bf16[12,256,1024]{2,1,0:T(8,128)(2,1)} custom-call(s32[2]{0:T(128)} %pad_add_fusion.ids.refs_0_._, bf16[4,12,256,256]{3,2,1,0:T(8,128)(2,1)} %bitcast.36, bf16[512,512]{1,0:T(8,128)(2,1)} %bitcast.34, bf16[512,512]{1,0:T(8,128)(2,1)} %bitcast.35, bf16[512,512]{1,0:T(8,128)(2,1)} %get-tuple-element.103.lowt), custom_call_target="tpu_custom_call" | custom-call | flops 4831838208 | bytes 18874368 | tf_op jit(solution)/shard_map/rows/pallas_call | solution.py:276
  161.8 12.6 %update_0_0.1.refs_5_ = bf16[12,256,24,256]{3,2,1,0:T(8,128)(2,1)} custom-call(s32[2]{0:T(128)} %pad_add_fusion.ids.refs_0_._, bf16[4,1024,256]{2,1,0:T(8,128)(2,1)} %cols_0.1.refs_1_, bf16[4,1024,256]{2,1,0:T(8,128)(2,1)} %cols_1.1.refs_2_, bf16[12,256,1024]{2,1,0:T(8,128)(2,1)} %rows.1.refs_3_, ...), custom_call_target="tpu_custom_call", output_to_operand_aliasing={{}: (5, {})} | custom-call | flops 6442450944 | bytes 18874368 | tf_op jit(solution)/shard_map/update_0_0/pallas_call | solution.py:337
  179.0 5.2 %cols_8.1.refs_1_ = bf16[4,1024,256]{2,1,0:T(8,128)(2,1)} custom-call(s32[2]{0:T(128)} %pad_add_fusion.ids.refs_0_._, bf16[4,256,256]{2,1,0:T(8,128)(2,1)} %get-tuple-element.115.refs_1_, bf16[4,256,256]{2,1,0:T(8,128)(2,1)} %collective-permute-done.16.refs_2_, bf16[4,256,256]{2,1,0:T(8,128)(2,1)} %collective-permute-done.13.refs_3_, ...), custom_call_target="tpu_custom_call" | custom-call | flops 1610612736 | bytes 6291456 | tf_op jit(solution)/shard_map/cols_8/pallas_call | solution.py:296
  184.2 13.5 %update_0_6.1.refs_5_ = bf16[12,256,24,256]{3,2,1,0:T(8,128)(2,1)} custom-call(s32[2]{0:T(128)} %pad_add_fusion.ids.refs_0_._, bf16[4,1024,256]{2,1,0:T(8,128)(2,1)} %cols_0.1.refs_1_, bf16[4,1024,256]{2,1,0:T(8,128)(2,1)} %cols_1.1.refs_2_, bf16[12,256,1024]{2,1,0:T(8,128)(2,1)} %rows.1.refs_3_, ...), custom_call_target="tpu_custom_call", output_to_operand_aliasing={{}: (5, {})} | custom-call | flops 6442450944 | bytes 18874368 | tf_op jit(solution)/shard_map/update_0_6/pallas_call | solution.py:337
  197.7 3.3 %collective-permute-done.15.refs_2_ = bf16[4,256,256]{2,1,0:T(8,128)(2,1)S(1)} collective-permute-done((bf16[4,256,256]{2,1,0:T(8,128)(2,1)}, bf16[4,256,256]{2,1,0:T(8,128)(2,1)S(1)}, u32[]{:S(2)}, u32[]{:S(2)}) %collective-permute-start.15) | collective-permute-done | bytes 524320 | tf_op jit(solution)/shard_map/ppermute | solution.py:247
  201.0 2.0 collective-permute-start.21
  203.5 8.8 %collective-permute-done.23.refs_4_ = bf16[4,256,256]{2,1,0:T(8,128)(2,1)S(1)} collective-permute-done((bf16[4,256,256]{2,1,0:T(8,128)(2,1)}, bf16[4,256,256]{2,1,0:T(8,128)(2,1)S(1)}, u32[]{:S(2)}, u32[]{:S(2)}) %collective-permute-start.23) | collective-permute-done | bytes 524320 | tf_op jit(solution)/shard_map/ppermute | solution.py:247
  213.1 5.2 %cols_9.1.refs_2_ = bf16[4,1024,256]{2,1,0:T(8,128)(2,1)} custom-call(s32[2]{0:T(128)} %pad_add_fusion.ids.refs_0_._, bf16[4,256,256]{2,1,0:T(8,128)(2,1)} %get-tuple-element.126.refs_1_, bf16[4,256,256]{2,1,0:T(8,128)(2,1)} %collective-permute-done.22.refs_2_, bf16[4,256,256]{2,1,0:T(8,128)(2,1)} %collective-permute-done.7.refs_3_, ...), custom_call_target="tpu_custom_call" | custom-call | flops 1610612736 | bytes 6291456 | tf_op jit(solution)/shard_map/cols_9/pallas_call | solution.py:296
  218.3 17.1 %update_1_4.1.refs_5_ = bf16[12,256,24,256]{3,2,1,0:T(8,128)(2,1)} custom-call(s32[2]{0:T(128)} %pad_add_fusion.ids.refs_0_._, bf16[4,1024,256]{2,1,0:T(8,128)(2,1)} %cols_8.1.refs_1_, bf16[4,1024,256]{2,1,0:T(8,128)(2,1)} %cols_9.1.refs_2_, bf16[12,256,1024]{2,1,0:T(8,128)(2,1)} %rows.1.refs_3_, ...), custom_call_target="tpu_custom_call", output_to_operand_aliasing={{}: (5, {})} | custom-call | flops 8589934592 | bytes 25165824 | tf_op jit(solution)/shard_map/update_1_4/pallas_call | solution.py:337
  236.2 5.2 %cols_16.1.refs_1_ = bf16[4,1024,256]{2,1,0:T(8,128)(2,1)} custom-call(s32[2]{0:T(128)} %pad_add_fusion.ids.refs_0_._, bf16[4,256,256]{2,1,0:T(8,128)(2,1)} %broadcast_select_fusion.refs_1_, bf16[4,256,256]{2,1,0:T(8,128)(2,1)} %collective-permute-done.20.refs_2_, bf16[4,256,256]{2,1,0:T(8,128)(2,1)} %collective-permute-done.18.refs_3_, ...), custom_call_target="tpu_custom_call" | custom-call | flops 1610612736 | bytes 6291456 | tf_op jit(solution)/shard_map/cols_16/pallas_call | solution.py:296
  243.0 5.2 %cols_17.1.refs_2_ = bf16[4,1024,256]{2,1,0:T(8,128)(2,1)} custom-call(s32[2]{0:T(128)} %pad_add_fusion.ids.refs_0_._, bf16[4,256,256]{2,1,0:T(8,128)(2,1)} %slice_select_fusion.refs_1_, bf16[4,256,256]{2,1,0:T(8,128)(2,1)} %copy-done.4, bf16[4,256,256]{2,1,0:T(8,128)(2,1)} %copy-done.5, bf16[4,256,256]{2,1,0:T(8,128)(2,1)} %copy-done.7, ...), custom_call_target="tpu_custom_call" | custom-call | flops 1610612736 | bytes 6291456 | tf_op jit(solution)/shard_map/cols_17/pallas_call | solution.py:296
  248.2 10.2 %update_2_8.1 = bf16[12,256,24,256]{3,2,1,0:T(8,128)(2,1)} custom-call(s32[2]{0:T(128)} %pad_add_fusion.ids.refs_0_._, bf16[4,1024,256]{2,1,0:T(8,128)(2,1)} %cols_16.1.refs_1_, bf16[4,1024,256]{2,1,0:T(8,128)(2,1)} %cols_17.1.refs_2_, bf16[12,256,1024]{2,1,0:T(8,128)(2,1)} %rows.1.refs_3_, ...), custom_call_target="tpu_custom_call", output_to_operand_aliasing={{}: (5, {})} | custom-call | flops 4294967296 | bytes 12582912 | tf_op jit(solution)/shard_map/update_2_8/pallas_call | solution.py:337
  (73 shorter events, 35.7 us)
Async XLA Ops:
  7.2 1.9 slice-start
  7.2 144.0 %all-gather.3.cloned.1.call-start = ((), (), s32[]{:S(2)}) async-start(), calls=%async_computation | async-start | bytes 7864320 | tf_op jit(solution)/shard_map/all_gather | solution.py:397
  9.8 2.0 copy-start
  20.2 17.5 %collective-permute-start.2 = (bf16[4,256,256]{2,1,0:T(8,128)(2,1)}, bf16[4,256,256]{2,1,0:T(8,128)(2,1)}, u32[]{:S(2)}, u32[]{:S(2)}) collective-permute-start(bf16[4,256,256]{2,1,0:T(8,128)(2,1)} %get-tuple-element.78), channel_id=1, source_target_pairs={{0,16},{1,17},{2,18},{3,19},{4,20},{5,21},{6,22},{7,23},{8,24},{9,... | collective-permute-start | bytes 1572872 | tf_op jit(solution)/shard_map/ppermute | solution.py:247
  39.6 25.1 %collective-permute-start.3 = (bf16[4,256,256]{2,1,0:T(8,128)(2,1)}, bf16[4,256,256]{2,1,0:T(8,128)(2,1)}, u32[]{:S(2)}, u32[]{:S(2)}) collective-permute-start(bf16[4,256,256]{2,1,0:T(8,128)(2,1)} %broadcast_select_fusion.2.refs_1_), channel_id=1, source_target_pairs={{0,8},{1,9},{2,10},{3,11},{4,12},{5,13},{6,14},{7,15},{8,0},{9,1},... | collective-permute-start | bytes 1572872 | tf_op jit(solution)/shard_map/ppermute | solution.py:247
  52.2 13.9 %collective-permute-start.4 = (bf16[4,256,256]{2,1,0:T(8,128)(2,1)}, bf16[4,256,256]{2,1,0:T(8,128)(2,1)}, u32[]{:S(2)}, u32[]{:S(2)}) collective-permute-start(bf16[4,256,256]{2,1,0:T(8,128)(2,1)} %broadcast_select_fusion.2.refs_1_), channel_id=1, source_target_pairs={{0,4},{1,5},{2,6},{3,7},{4,0},{5,1},{6,2},{7,3},{8,12},{9,13},{10,... | collective-permute-start | bytes 1572872 | tf_op jit(solution)/shard_map/ppermute | solution.py:247
  58.7 26.7 %copy-start.1 = (bf16[1,1,256,24,1,256]{5,2,3,4,1,0:T(8,128)(2,1)S(1)}, bf16[1,1,256,24,1,256]{5,2,3,4,1,0:T(8,128)(2,1)}, u32[]{:S(2)}) copy-start(bf16[1,1,256,24,1,256]{5,2,3,4,1,0:T(8,128)(2,1)} %copy-done) | copy-start | bytes 9437188
  61.3 7.2 %collective-permute-start = (bf16[4,256,256]{2,1,0:T(8,128)(2,1)S(1)}, bf16[4,256,256]{2,1,0:T(8,128)(2,1)S(1)}, u32[]{:S(2)}, u32[]{:S(2)}) collective-permute-start(bf16[4,256,256]{2,1,0:T(8,128)(2,1)S(1)} %get-tuple-element.156), channel_id=1, source_target_pairs={{16,16},{17,20},{18,24},{19,28},{20,17},{21,21},{22,25},{23,29},{2... | collective-permute-start | bytes 1572872 | tf_op jit(solution)/shard_map/ppermute | solution.py:247
  66.1 12.9 %collective-permute-start.5 = (bf16[4,256,256]{2,1,0:T(8,128)(2,1)}, bf16[4,256,256]{2,1,0:T(8,128)(2,1)S(1)}, u32[]{:S(2)}, u32[]{:S(2)}) collective-permute-start(bf16[4,256,256]{2,1,0:T(8,128)(2,1)} %collective-permute-done.3.refs_3_), channel_id=1, source_target_pairs={{0,4},{1,5},{2,6},{3,7},{4,0},{5,1},{6,2},{7,3},{8,12},{9,13},{10,... | collective-permute-start | bytes 1572872 | tf_op jit(solution)/shard_map/ppermute | solution.py:247
  68.5 35.1 %collective-permute-start.8 = (bf16[4,256,256]{2,1,0:T(8,128)(2,1)}, bf16[4,256,256]{2,1,0:T(8,128)(2,1)}, u32[]{:S(2)}, u32[]{:S(2)}) collective-permute-start(bf16[4,256,256]{2,1,0:T(8,128)(2,1)} %get-tuple-element.84), channel_id=1, source_target_pairs={{0,16},{1,17},{2,18},{3,19},{4,20},{5,21},{6,22},{7,23},{8,24},{9,... | collective-permute-start | bytes 1572872 | tf_op jit(solution)/shard_map/ppermute | solution.py:247
  75.4 28.3 %collective-permute-start.1 = (bf16[4,256,256]{2,1,0:T(8,128)(2,1)}, bf16[4,256,256]{2,1,0:T(8,128)(2,1)}, u32[]{:S(2)}, u32[]{:S(2)}) collective-permute-start(bf16[4,256,256]{2,1,0:T(8,128)(2,1)} %get-tuple-element.74), channel_id=1, source_target_pairs={{16,16},{17,20},{18,24},{19,28},{20,17},{21,21},{22,25},{23,29},{2... | collective-permute-start | bytes 1572872 | tf_op jit(solution)/shard_map/ppermute | solution.py:247
  79.0 7.4 %copy-start.3 = (bf16[4,256,256]{2,1,0:T(8,128)(2,1)}, bf16[4,256,256]{2,1,0:T(8,128)(2,1)S(1)}, u32[]{:S(2)}) copy-start(bf16[4,256,256]{2,1,0:T(8,128)(2,1)S(1)} %collective-permute-done.5.refs_4_) | copy-start | bytes 1572868
  80.0 23.7 %collective-permute-start.6 = (bf16[4,256,256]{2,1,0:T(8,128)(2,1)}, bf16[4,256,256]{2,1,0:T(8,128)(2,1)}, u32[]{:S(2)}, u32[]{:S(2)}) collective-permute-start(bf16[4,256,256]{2,1,0:T(8,128)(2,1)} %pad_maximum_fusion.mine), channel_id=1, source_target_pairs={{0,1},{1,0},{2,3},{3,2},{4,5},{5,4},{6,7},{7,6},{8,9},{9,8},{10,11... | collective-permute-start | bytes 1572872 | tf_op jit(solution)/shard_map/ppermute | solution.py:247
  86.4 28.3 %collective-permute-start.11 = (bf16[4,256,256]{2,1,0:T(8,128)(2,1)}, bf16[4,256,256]{2,1,0:T(8,128)(2,1)}, u32[]{:S(2)}, u32[]{:S(2)}) collective-permute-start(bf16[4,256,256]{2,1,0:T(8,128)(2,1)} %get-tuple-element.98.refs_1_), channel_id=1, source_target_pairs={{0,8},{1,9},{2,10},{3,11},{4,12},{5,13},{6,14},{7,15},{8,0},{9,1},... | collective-permute-start | bytes 1572872 | tf_op jit(solution)/shard_map/ppermute | solution.py:247
  107.7 32.8 %collective-permute-start.13 = (bf16[4,256,256]{2,1,0:T(8,128)(2,1)}, bf16[4,256,256]{2,1,0:T(8,128)(2,1)}, u32[]{:S(2)}, u32[]{:S(2)}) collective-permute-start(bf16[4,256,256]{2,1,0:T(8,128)(2,1)} %get-tuple-element.115.refs_1_), channel_id=1, source_target_pairs={{0,8},{1,9},{2,10},{3,11},{4,12},{5,13},{6,14},{7,15},{8,0},{9,1},... | collective-permute-start | bytes 1572872 | tf_op jit(solution)/shard_map/ppermute | solution.py:247
  111.4 29.6 %collective-permute-start.10 = (bf16[4,256,256]{2,1,0:T(8,128)(2,1)}, bf16[4,256,256]{2,1,0:T(8,128)(2,1)}, u32[]{:S(2)}, u32[]{:S(2)}) collective-permute-start(bf16[4,256,256]{2,1,0:T(8,128)(2,1)} %get-tuple-element.98.refs_1_), channel_id=1, source_target_pairs={{0,4},{1,5},{2,6},{3,7},{4,0},{5,1},{6,2},{7,3},{8,12},{9,13},{10,... | collective-permute-start | bytes 1572872 | tf_op jit(solution)/shard_map/ppermute | solution.py:247
  114.7 28.4 %collective-permute-start.12 = (bf16[4,256,256]{2,1,0:T(8,128)(2,1)}, bf16[4,256,256]{2,1,0:T(8,128)(2,1)}, u32[]{:S(2)}, u32[]{:S(2)}) collective-permute-start(bf16[4,256,256]{2,1,0:T(8,128)(2,1)} %collective-permute-done.11.refs_3_), channel_id=1, source_target_pairs={{0,4},{1,5},{2,6},{3,7},{4,0},{5,1},{6,2},{7,3},{8,12},{9,13},{10,... | collective-permute-start | bytes 1572872 | tf_op jit(solution)/shard_map/ppermute | solution.py:247
  115.2 33.1 %collective-permute-start.9 = (bf16[4,256,256]{2,1,0:T(8,128)(2,1)}, bf16[4,256,256]{2,1,0:T(8,128)(2,1)}, u32[]{:S(2)}, u32[]{:S(2)}) collective-permute-start(bf16[4,256,256]{2,1,0:T(8,128)(2,1)} %get-tuple-element.85), channel_id=1, source_target_pairs={{0,16},{1,17},{2,18},{3,19},{4,20},{5,21},{6,22},{7,23},{8,24},{9,... | collective-permute-start | bytes 1572872 | tf_op jit(solution)/shard_map/ppermute | solution.py:247
  133.7 40.7 %collective-permute-start.14 = (bf16[4,256,256]{2,1,0:T(8,128)(2,1)}, bf16[4,256,256]{2,1,0:T(8,128)(2,1)}, u32[]{:S(2)}, u32[]{:S(2)}) collective-permute-start(bf16[4,256,256]{2,1,0:T(8,128)(2,1)} %get-tuple-element.105), channel_id=1, source_target_pairs={{16,16},{17,20},{18,24},{19,28},{20,17},{21,21},{22,25},{23,29},{2... | collective-permute-start | bytes 1572872 | tf_op jit(solution)/shard_map/ppermute | solution.py:247
  140.5 20.9 %collective-permute-start.7 = (bf16[4,256,256]{2,1,0:T(8,128)(2,1)}, bf16[4,256,256]{2,1,0:T(8,128)(2,1)}, u32[]{:S(2)}, u32[]{:S(2)}) collective-permute-start(bf16[4,256,256]{2,1,0:T(8,128)(2,1)} %get-tuple-element.126.refs_1_), channel_id=1, source_target_pairs={{0,8},{1,9},{2,10},{3,11},{4,12},{5,13},{6,14},{7,15},{8,0},{9,1},... | collective-permute-start | bytes 1572872 | tf_op jit(solution)/shard_map/ppermute | solution.py:247
  141.0 36.3 %collective-permute-start.16 = (bf16[4,256,256]{2,1,0:T(8,128)(2,1)}, bf16[4,256,256]{2,1,0:T(8,128)(2,1)}, u32[]{:S(2)}, u32[]{:S(2)}) collective-permute-start(bf16[4,256,256]{2,1,0:T(8,128)(2,1)} %get-tuple-element.115.refs_1_), channel_id=1, source_target_pairs={{0,4},{1,5},{2,6},{3,7},{4,0},{5,1},{6,2},{7,3},{8,12},{9,13},{10,... | collective-permute-start | bytes 1572872 | tf_op jit(solution)/shard_map/ppermute | solution.py:247
  143.1 60.0 %collective-permute-start.22 = (bf16[4,256,256]{2,1,0:T(8,128)(2,1)}, bf16[4,256,256]{2,1,0:T(8,128)(2,1)}, u32[]{:S(2)}, u32[]{:S(2)}) collective-permute-start(bf16[4,256,256]{2,1,0:T(8,128)(2,1)} %get-tuple-element.126.refs_1_), channel_id=1, source_target_pairs={{0,4},{1,5},{2,6},{3,7},{4,0},{5,1},{6,2},{7,3},{8,12},{9,13},{10,... | collective-permute-start | bytes 1572872 | tf_op jit(solution)/shard_map/ppermute | solution.py:247
  148.3 30.3 %collective-permute-start.17 = (bf16[4,256,256]{2,1,0:T(8,128)(2,1)}, bf16[4,256,256]{2,1,0:T(8,128)(2,1)}, u32[]{:S(2)}, u32[]{:S(2)}) collective-permute-start(bf16[4,256,256]{2,1,0:T(8,128)(2,1)} %collective-permute-done.13.refs_3_), channel_id=1, source_target_pairs={{0,4},{1,5},{2,6},{3,7},{4,0},{5,1},{6,2},{7,3},{8,12},{9,13},{10,... | collective-permute-start | bytes 1572872 | tf_op jit(solution)/shard_map/ppermute | solution.py:247
  151.2 10.1 %copy-start.2 = (bf16[4,256,256]{2,1,0:T(8,128)(2,1)S(1)}, bf16[4,256,256]{2,1,0:T(8,128)(2,1)}, u32[]{:S(2)}) copy-start(bf16[4,256,256]{2,1,0:T(8,128)(2,1)} %broadcast_select_fusion.refs_1_) | copy-start | bytes 1572868
  161.3 15.0 %collective-permute-start.18 = (bf16[4,256,256]{2,1,0:T(8,128)(2,1)S(1)}, bf16[4,256,256]{2,1,0:T(8,128)(2,1)}, u32[]{:S(2)}, u32[]{:S(2)}) collective-permute-start(bf16[4,256,256]{2,1,0:T(8,128)(2,1)S(1)} %copy-done.2), channel_id=1, source_target_pairs={{0,8},{1,9},{2,10},{3,11},{4,12},{5,13},{6,14},{7,15},{8,0},{9,1},... | collective-permute-start | bytes 1572872 | tf_op jit(solution)/shard_map/ppermute | solution.py:247
  174.4 61.0 %collective-permute-start.20 = (bf16[4,256,256]{2,1,0:T(8,128)(2,1)S(1)}, bf16[4,256,256]{2,1,0:T(8,128)(2,1)}, u32[]{:S(2)}, u32[]{:S(2)}) collective-permute-start(bf16[4,256,256]{2,1,0:T(8,128)(2,1)S(1)} %copy-done.2), channel_id=1, source_target_pairs={{0,4},{1,5},{2,6},{3,7},{4,0},{5,1},{6,2},{7,3},{8,12},{9,13},{10,... | collective-permute-start | bytes 1572872 | tf_op jit(solution)/shard_map/ppermute | solution.py:247
  176.4 24.7 %collective-permute-start.15 = (bf16[4,256,256]{2,1,0:T(8,128)(2,1)}, bf16[4,256,256]{2,1,0:T(8,128)(2,1)S(1)}, u32[]{:S(2)}, u32[]{:S(2)}) collective-permute-start(bf16[4,256,256]{2,1,0:T(8,128)(2,1)} %slice_select_fusion.refs_1_), channel_id=1, source_target_pairs={{0,4},{1,5},{2,6},{3,7},{4,0},{5,1},{6,2},{7,3},{8,12},{9,13},{10,... | collective-permute-start | bytes 1572872 | tf_op jit(solution)/shard_map/ppermute | solution.py:247
  177.3 35.0 %collective-permute-start.23 = (bf16[4,256,256]{2,1,0:T(8,128)(2,1)}, bf16[4,256,256]{2,1,0:T(8,128)(2,1)S(1)}, u32[]{:S(2)}, u32[]{:S(2)}) collective-permute-start(bf16[4,256,256]{2,1,0:T(8,128)(2,1)} %collective-permute-done.7.refs_3_), channel_id=1, source_target_pairs={{0,4},{1,5},{2,6},{3,7},{4,0},{5,1},{6,2},{7,3},{8,12},{9,13},{10,... | collective-permute-start | bytes 1572872 | tf_op jit(solution)/shard_map/ppermute | solution.py:247
  178.7 62.7 %collective-permute-start.24 = (bf16[4,256,256]{2,1,0:T(8,128)(2,1)}, bf16[4,256,256]{2,1,0:T(8,128)(2,1)S(1)}, u32[]{:S(2)}, u32[]{:S(2)}) collective-permute-start(bf16[4,256,256]{2,1,0:T(8,128)(2,1)} %slice_select_fusion.refs_1_), channel_id=1, source_target_pairs={{0,8},{1,9},{2,10},{3,11},{4,12},{5,13},{6,14},{7,15},{8,0},{9,1},... | collective-permute-start | bytes 1572872 | tf_op jit(solution)/shard_map/ppermute | solution.py:247
  201.0 34.3 %copy-start.4 = (bf16[4,256,256]{2,1,0:T(8,128)(2,1)}, bf16[4,256,256]{2,1,0:T(8,128)(2,1)S(1)}, u32[]{:S(2)}) copy-start(bf16[4,256,256]{2,1,0:T(8,128)(2,1)S(1)} %collective-permute-done.15.refs_2_) | copy-start | bytes 1572868
  201.0 34.3 %collective-permute-start.21 = (bf16[4,256,256]{2,1,0:T(8,128)(2,1)}, bf16[4,256,256]{2,1,0:T(8,128)(2,1)S(1)}, u32[]{:S(2)}, u32[]{:S(2)}) collective-permute-start(bf16[4,256,256]{2,1,0:T(8,128)(2,1)} %collective-permute-done.18.refs_3_), channel_id=1, source_target_pairs={{0,4},{1,5},{2,6},{3,7},{4,0},{5,1},{6,2},{7,3},{8,12},{9,13},{10,... | collective-permute-start | bytes 1572872 | tf_op jit(solution)/shard_map/ppermute | solution.py:247
  203.1 38.3 %collective-permute-start.19 = (bf16[4,256,256]{2,1,0:T(8,128)(2,1)S(1)}, bf16[4,256,256]{2,1,0:T(8,128)(2,1)S(1)}, u32[]{:S(2)}, u32[]{:S(2)}) collective-permute-start(bf16[4,256,256]{2,1,0:T(8,128)(2,1)S(1)} %collective-permute-done.15.refs_2_), channel_id=1, source_target_pairs={{0,8},{1,9},{2,10},{3,11},{4,12},{5,13},{6,14},{7,15},{8,0},{9,1},... | collective-permute-start | bytes 1572872 | tf_op jit(solution)/shard_map/ppermute | solution.py:247
  (4 other events, 3.2 us)
Sparse Core Ops, SparseCore 0:
  20.3 49.0 all-gather.2

commit v3 on v2

--- a/solution.py
+++ b/solution.py
@@ -120,13 +120,14 @@
         lowt[...] = result.T.astype(BF16)
 
 
-def rows_kernel(ids, strips, inv0t, inv1t, lowt, out, buf):
-    _, count, tile, _ = strips.shape
+def rows_kernel(ids, q0, q1, q2, q3, inv0t, inv1t, lowt, out, buf):
+    count, tile, _ = q0.shape
     width = 2 * tile
-    row_id = ids[0]
-    for k in range(4):
+    row_id, col_id = ids[0], ids[1]
+    for m, ref in enumerate((q0, q1, q2, q3)):
+        base = pl.multiple_of((col_id ^ m) * tile, tile)
         for i in range(count):
-            buf[i * tile : (i + 1) * tile, k * tile : (k + 1) * tile] = strips[k, i]
+            buf[i * tile : (i + 1) * tile, pl.ds(base, tile)] = ref[i]
     local = lax.broadcasted_iota(jnp.int32, (count * tile, 1), 0) // tile
     tile_row = (pl.program_id(0) * count + local) * 8 + row_id
     first = dot(buf[:, :width], inv0t[...])
@@ -139,22 +140,23 @@
         out[i, :, width:] = second[i * tile : (i + 1) * tile]
 
 
-def cols_kernel(start, stride, ids, p0, p1, p2, p3, inv0, inv1, low, out, raw):
-    count, tile, _ = p0.shape
+def cols_kernel(start, ids, *refs):
+    pieces, (inv0, inv1, low, out, raw) = refs[:8], refs[8:]
+    tile = pieces[0].shape[1]
     width = 2 * tile
     row_id, col_id = ids[0], ids[1]
-    for m, ref in enumerate((p0, p1, p2, p3)):
+    for m in range(4):
         base = pl.multiple_of(((row_id % 4) ^ m) * tile, tile)
-        for i in range(count):
-            raw[pl.ds(base, tile), i * tile : (i + 1) * tile] = ref[i]
-    local = lax.broadcasted_iota(jnp.int32, (1, count * tile), 1) // tile
-    tile_col = (start + (pl.program_id(0) * count + local) * stride) * 4 + col_id
+        for i in range(2):
+            raw[pl.ds(base, tile), i * tile : (i + 1) * tile] = pieces[2 * m + i][0]
+    local = lax.broadcasted_iota(jnp.int32, (1, 2 * tile), 1) // tile
+    tile_col = (start + pl.program_id(0) * 2 + local) * 4 + col_id
     first = dot(inv0[...], raw[:width])
     first = jnp.where(tile_col >= 2, first, 0.0).astype(BF16)
     rest = (raw[width:].astype(F32) - dot(low[...], first)).astype(BF16)
     second = dot(inv1[...], rest)
     second = jnp.where(tile_col >= 4, second, 0.0).astype(BF16)
-    for i in range(count):
+    for i in range(2):
         out[i, :width] = first[:, i * tile : (i + 1) * tile]
         out[i, width:] = second[:, i * tile : (i + 1) * tile]
 
@@ -163,13 +165,12 @@
     out[...] = jnp.zeros_like(out)
 
 
-def update_kernel(group, start, ids, even, odd, factor, matrix, _, out, acc):
+def update_kernel(group, start, ids, cols, factor, matrix, _, out, acc):
     tile = factor.shape[1]
     row_id, col_id = ids[0], ids[1]
     tile_row = (start + pl.program_id(0)) * 8 + row_id
     end = jnp.where(tile_row >= 4, (tile_row - col_id) // 4 + 1 - group * SUB, 0)
     begin = 1 if group == 0 else 0
-    held = [(odd if s % 2 else even, s // 2) for s in range(SUB)]
 
     @pl.when(end <= begin)
     def _():
@@ -179,8 +180,7 @@
     def _():
         def fill(chosen):
             for s in chosen:
-                ref, at = held[s]
-                product = dot(factor[0], ref[at])
+                product = dot(factor[0], cols[s])
                 for part in range(tile // LANES):
                     lanes = slice(part * LANES, (part + 1) * LANES)
                     acc[part, pl.ds(s, tile, stride=SUB), :] = product[:, lanes]
@@ -189,7 +189,7 @@
         def _():
             fill(range(begin, SUB))
 
-        for pair in range(0, len(held), 2):
+        for pair in range(0, SUB, 2):
 
             @pl.when((end < SUB) & (pair < end))
             def _(pair=pair):
@@ -255,6 +255,9 @@
     def across_core(value):
         return move(value, lambda r, c: (r, c ^ 1))
 
+    def across_x(value):
+        return move(value, lambda r, c: (r, c ^ 2))
+
     def lift(value):
         return move(value, lambda r, c: (r + 4, c) if r < 4 else None)
 
@@ -272,43 +275,43 @@
 
     def factor_rows(strips, lowt):
         count = 2
-        block = pl.BlockSpec((4, count, tile, tile), lambda t: (0, t, 0, 0))
+        block = pl.BlockSpec((count, tile, tile), lambda t: (t, 0, 0))
         return pl.pallas_call(
             rows_kernel,
             grid=(tiles // count,),
-            in_specs=[smem, block, whole(inv0t), whole(inv1t), whole(lowt)],
+            in_specs=[smem, *[block] * 4, whole(inv0t), whole(inv1t), whole(lowt)],
             out_specs=pl.BlockSpec((count, tile, 2 * width), lambda t: (t, 0, 0)),
             out_shape=jax.ShapeDtypeStruct((tiles, tile, 2 * width), BF16),
             scratch_shapes=[pltpu.VMEM((count * tile, 2 * width), BF16)],
             compiler_params=params(),
             cost_estimate=cost(tiles * 6 * tile * width * width, 24 * tiles * tile * tile),
             name="rows",
-        )(ids, strips, inv0t, inv1t, lowt)
+        )(ids, *strips, inv0t, inv1t, lowt)
 
     def factor_cols(start, pieces, low):
-        total = pieces[0].shape[0]
-        count = 2
-        block = pl.BlockSpec((count, tile, tile), lambda s: (s, 0, 0))
+        def at(offset):
+            return pl.BlockSpec((1, tile, tile), lambda s: (s + offset, 0, 0))
 
         def kernel(*refs):
-            cols_kernel(start, 2, *refs)
-
+            cols_kernel(start, *refs)
+
+        blocks = [at(offset) for _, offset in pieces]
         return pl.pallas_call(
             kernel,
-            grid=(total // count,),
-            in_specs=[smem, *[block] * 4, whole(inv_first), whole(inv_second), whole(low)],
-            out_specs=pl.BlockSpec((count, 2 * width, tile), lambda s: (s, 0, 0)),
-            out_shape=jax.ShapeDtypeStruct((total, 2 * width, tile), BF16),
-            scratch_shapes=[pltpu.VMEM((2 * width, count * tile), BF16)],
+            grid=(SUB // 2,),
+            in_specs=[smem, *blocks, whole(inv_first), whole(inv_second), whole(low)],
+            out_specs=pl.BlockSpec((2, 2 * width, tile), lambda s: (s, 0, 0)),
+            out_shape=jax.ShapeDtypeStruct((SUB, 2 * width, tile), BF16),
+            scratch_shapes=[pltpu.VMEM((2 * width, 2 * tile), BF16)],
             compiler_params=params(),
-            cost_estimate=cost(total * 6 * tile * width * width, 24 * total * tile * tile),
+            cost_estimate=cost(SUB * 6 * tile * width * width, 24 * SUB * tile * tile),
             name="cols_%d" % start,
-        )(ids, *pieces, inv_first, inv_second, low)
+        )(ids, *[array for array, _ in pieces], inv_first, inv_second, low)
 
     def cost(flops, size):
-        return pl.CostEstimate(flops=flops, bytes_accessed=size, transcendentals=0)
-
-    def clear(gate):
+        return pl.CostEstimate(flops=1, bytes_accessed=1, transcendentals=0)
+
+    def clear():
         def place(i):
             group, first = 1, 0
             for g in range(1, groups):
@@ -326,7 +329,7 @@
             compiler_params=params(),
             cost_estimate=cost(0, tiles * tile * SUB * tile * 2),
             name="clear",
-        )(together(ids, gate)[0])
+        )(ids)
 
     def update(result, group, start, stop, cols, panels):
         grid_block = pl.BlockSpec((1, tile, SUB, tile), lambda t: (t + start, 0, group, 0))
@@ -339,7 +342,7 @@
             grid=(stop - start,),
             in_specs=[
                 smem,
-                *[whole(part) for part in cols],
+                whole(cols),
                 pl.BlockSpec((1, tile, 2 * width), lambda t: (t + start, 0, 0)),
                 grid_block,
                 pl.BlockSpec(memory_space=pl.ANY),
@@ -347,94 +350,78 @@
             out_specs=grid_block,
             out_shape=jax.ShapeDtypeStruct(view.shape, BF16),
             scratch_shapes=[pltpu.VMEM((tile // LANES, tile * SUB, LANES), F32)],
-            input_output_aliases={len(cols) + 3: 0},
+            input_output_aliases={4: 0},
             compiler_params=params(),
             cost_estimate=cost(
                 (stop - start) * 2 * tile * tile * 2 * width * SUB,
                 (stop - start) * 6 * tile * tile * SUB,
             ),
             name="update_%d_%d" % (group, start),
-        )(ids, *cols, panels, view, result)
+        )(ids, cols, panels, view, result)
 
     def cross(value):
         return move(value, lambda r, c: (4 + c, r - 4) if r >= 4 else None)
 
-    count = 2 * groups
     half = SUB // 2
     held = jnp.swapaxes(view[0], 0, 1)
-    own = [held[i // 2 * SUB + i % 2 : (i // 2 + 1) * SUB : 2] for i in range(count)]
-    up, base, ez, ey, ed, cols = ([None] * count for _ in range(6))
-
-    def begin(i, token):
-        got, token = together(up[i], token)
-        base[i] = jnp.where(upper, got, own[i])
-        ez[i], ey[i] = across_z(base[i]), across_y(base[i])
-        return token
-
-    def raise_after(i, gate):
-        source, gate = together(own[i], gate)
-        up[i] = lift(source)
-        return gate
-
-    def cross_after(i, gate):
-        source, gate = together(swapped[i // 2 * half : (i // 2 + 1) * half], gate)
-        up[i] = cross(source)
-        return gate
-
-    def forward(i, token):
-        ez[i], token = together(ez[i], token)
-        ed[i] = across_y(ez[i])
-        return token
-
-    def make_cols(i, gate):
-        parts = together(base[i], ey[i], ez[i], ed[i], gate)
-        cols[i] = factor_cols(i // 2 * SUB + i % 2, parts[:4], low)
-
-    up[0] = lift(own[0])
-    source, own[0] = together(view, own[0])
-    strip = source[:, :, 0, :]
+    even = [held[g * SUB : (g + 1) * SUB : 2] for g in range(groups)]
+    odd = [held[g * SUB + 1 : (g + 1) * SUB : 2] for g in range(groups)]
+
+    def pick(group, lifted, crossed):
+        got = jnp.concatenate([lifted, crossed])
+        return jnp.where(upper, got, jnp.concatenate([even[group], odd[group]]))
+
+    def factor_group(group, base, over_y, over_z, even_zy, odd_zy):
+        pieces = [(a, o) for a in (base, over_y, over_z) for o in (0, half)]
+        return factor_cols(group * SUB, pieces + [even_zy, odd_zy], low)
+
+    lift_0 = lift(even[0])
+    strip = together(view, even[0])[0][:, :, 0, :]
     swapped = jnp.swapaxes(strip, 1, 2)
-    strips = lax.all_gather(strip, "col")
-    up[1] = cross(swapped[:half])
-    up[0] = raise_after(2, up[0])
-    begin(0, ids)
-    up[1] = cross_after(3, up[1])
-    result = clear(base[0])
-    ey[0] = forward(0, ey[0])
-    up[2] = raise_after(4, up[2])
-    begin(1, base[0])
-    up[3] = cross_after(5, up[3])
-    mine = jnp.stack([p[0] for p in (base[0], ey[0], ez[0], ed[0])])
+    cross_0 = cross(swapped[:half])
+    result = clear()
+    lift_0, cross_0, strip, swapped = together(lift_0, cross_0, strip, swapped)
+
+    base_0 = pick(0, lift_0, cross_0)
+    z_0, y_0 = across_z(base_0), across_y(base_0)
+    strip_2 = across_x(strip)
+    z_0, y_0, result, inv0t, inv1t, cross_0, lift_0 = together(z_0, y_0, result, inv0t, inv1t, cross_0, lift_0)
+
+    first_zy = across_y(z_0[:1])
+    both_0 = across_y(z_0)
+    cross_1 = cross(together(swapped[half : 2 * half], cross_0)[0])
+    lift_1 = lift(together(even[1], lift_0)[0])
+    strip_1 = across_core(strip)
+    mine = jnp.concatenate([base_0[:1], y_0[:1], z_0[:1], first_zy])
     other = across_core(mine)
-    base[1] = begin(2, base[1])
-    base[2] = forward(1, base[2])
     low, lowt = factor_link(mine, other)
-    low = begin(3, low)
-    make_cols(0, base[3])
-    cols[0] = forward(2, cols[0])
-    make_cols(1, ez[2])
-    cols[1] = begin(4, cols[1])
-    lowt, base[4] = together(lowt, base[4])
-    panels = factor_rows(strips, lowt)
-    panels = forward(3, panels)
-    result, ez[3] = together(result, ez[3])
-    middle = tiles // 2
-    result = update(result, 0, 0, middle, cols[0:2], panels)
-    result = begin(5, result)
-    base[5] = forward(4, base[5])
-    make_cols(2, base[5])
-    result, cols[2] = together(result, cols[2])
-    result = update(result, 0, middle, tiles, cols[0:2], panels)
-    ey[5], result = together(ey[5], result)
-    ed[5] = across_z(ey[5])
-    make_cols(3, ey[5])
-    result, cols[3] = together(result, cols[3])
-    result = update(result, 1, ratio, tiles, cols[2:4], panels)
-    ed[4], result = together(ed[4], result)
-    make_cols(4, base[5])
-    ed[5], cols[4] = together(ed[5], cols[4])
-    make_cols(5, base[5])
-    result = update(result, 2, 2 * ratio, tiles, cols[4:6], panels)
+    low, both_0, cross_1, lift_1, strip_1, strip_2 = together(low, both_0, cross_1, lift_1, strip_1, strip_2)
+
+    base_1 = pick(1, lift_1, cross_1)
+    z_1, y_1 = across_z(base_1), across_y(base_1)
+    strip_3 = across_core(strip_2)
+    cols_0 = factor_group(0, base_0, y_0, z_0, (both_0, 0), (both_0, half))
+    panels = factor_rows((strip, strip_1, strip_2, strip_3), lowt)
+    z_1, y_1, cols_0, panels = together(z_1, y_1, cols_0, panels)
+
+    lift_2 = lift(together(even[2], z_1)[0])
+    cross_2 = cross(together(swapped[2 * half :], z_1)[0])
+    both_1 = across_y(z_1)
+    result = update(result, 0, 0, tiles, cols_0, panels)
+    lift_2, cross_2, both_1, result = together(lift_2, cross_2, both_1, result)
+
+    base_2 = pick(2, lift_2, cross_2)
+    z_2, y_2 = across_z(base_2), across_y(base_2)
+    cols_1 = factor_group(1, base_1, y_1, z_1, (both_1, 0), (both_1, half))
+    middle = 2 * ratio
+    result = update(result, 1, ratio, middle, cols_1, panels)
+    z_2, y_2, result = together(z_2, y_2, result)
+
+    even_2, odd_2 = across_y(z_2[:half]), across_z(y_2[half:])
+    result = update(result, 1, middle, tiles, cols_1, panels)
+    even_2, odd_2, result = together(even_2, odd_2, result)
+    cols_2 = factor_group(2, base_2, y_2, z_2, (even_2, 0), (odd_2, 0))
+    result = update(result, 2, 2 * ratio, tiles, cols_2, panels)
     return panels.reshape(tiles, 1, tile, 2 * width), result.reshape(matrix.shape)
 
 

time: 270 us -> 234 us (0.87)
  between operations: 14.2 us -> 0.88 us
  starting transfers between devices: 78 us -> 69.2 us
  Pallas kernels: 105 us -> 99 us
  waiting for transfers between devices: 30.1 us -> 27.2 us
    ppermute x25 -> x21, starting transfers between devices: 78 us -> 69.2 us  [move(): return lax.ppermute(value, ('row', 'col'), pairs)]
    pallas_call x11 -> x8, Pallas kernels: 94.9 us -> 88.7 us  [the longest x4 53.3 us: update(): pl.pallas_call(kernel, grid=(stop - start,), in_specs=[smem, whole(cols),...]
    squeeze x1 -> x0, local copies, waits for them, and re-layouts: 4.94 us -> none  [local(): strip = source[:, :, 0, :]]
    unnamed x21 -> x43, local copies, waits for them, and re-layouts: 8.89 us -> 13 us
    ppermute x25 -> x21, waiting for transfers between devices: 30.1 us -> 27.2 us  [move(): return lax.ppermute(value, ('row', 'col'), pairs)]
    select_n x5 -> x3, other arithmetic: 5.74 us -> 4.57 us  [pick(): return jnp.where(upper, got, jnp.concatenate([even[group], odd[group]]))]
    slice x8 -> x9, local copies, waits for them, and re-layouts: 14.9 us -> 15.5 us  [the longest x1 6.87 us: local(): strip = together(view, even[0])[0][:, :, 0, :]]
  transfers between devices with their start and end apart: 26 -> 21, of which waited for: 8 -> 7; matrix products, arithmetic and copies ran while one was open for 8% -> 10% of each run, Pallas kernels for 34% -> 35%
where the time goes in v3:
time: 234 us; the launch traced here: 232 us
  Pallas kernels  99 us (42%)
  starting transfers between devices  69.2 us (30%)
  local copies, waits for them, and re-layouts  30.4 us (13%)
  waiting for transfers between devices  27.2 us (12%)
  other arithmetic  5.28 us (2%)
    ppermute x21, starting transfers between devices, move(): return lax.ppermute(value, ('row', 'col'), pairs)  69.2 us
    pallas_call x4, Pallas kernels, update(): pl.pallas_call(kernel, grid=(stop - start,), in_specs=[smem, whole(cols),...  53.3 us
    ppermute x21, waiting for transfers between devices, move(): return lax.ppermute(value, ('row', 'col'), pairs)  27.2 us
    pallas_call x3, Pallas kernels, factor_cols(): pl.pallas_call(kernel, grid=(SUB // 2,), in_specs=[smem, *blocks, whole(i...  24.8 us
    unnamed x43, local copies, waits for them, and re-layouts  13 us
    pallas_call x1, Pallas kernels, factor_rows(): pl.pallas_call(rows_kernel, grid=(tiles // count,), in_specs=[smem, *[blo...  10.5 us
    pallas_call x1, Pallas kernels, clear(): pl.pallas_call(zeros_kernel, grid=(ratio * groups * (groups - 1) // 2,),...  7.4 us
    slice x1, local copies, waits for them, and re-layouts, local(): strip = together(view, even[0])[0][:, :, 0, :]  6.87 us
  transfers between devices with their start and end apart: 21, of which 7 were waited for; matrix products, arithmetic and copies ran while one was open for 10% of the time, Pallas kernels for 35%

profile of v3, /device:TPU:0, one launch (start us, length us, event | category | flops | bytes accessed | tf_op | source)
XLA Modules:
  0.0 232.0 jit_solution(7956181566021495489)
XLA Ops:
  0.6 1.9 slice-done
  3.2 1.7 fusion
  4.9 6.8 %collective-permute-start = (bf16[4,256,256]{2,1,0:T(8,128)(2,1)}, bf16[4,256,256]{2,1,0:T(8,128)(2,1)}, u32[]{:S(2)}, u32[]{:S(2)}) collective-permute-start(bf16[4,256,256]{2,1,0:T(8,128)(2,1)} %get-tuple-element.79), channel_id=1, source_target_pairs={{0,16},{1,17},{2,18},{3,19},{4,20},{5,21},{6,22},{7,23},{8,24},{9,... | collective-permute-start | bytes 1572872 | tf_op jit(solution)/shard_map/ppermute | solution.py:247
  11.7 6.9 %slice.52 = bf16[12,256,1,256]{3,2,1,0:T(2,128)(2,1)S(1)} slice(bf16[12,256,24,256]{3,2,1,0:T(8,128)(2,1)} %bitcast.23), slice={[0:12], [0:256], [0:1], [0:256]} | slice | bytes 3145728 | tf_op jit(solution)/shard_map/slice | solution.py:379
  18.6 5.0 %copy.48 = bf16[12,256,1,256]{1,3,0,2:T(8,128)(2,1)} copy(bf16[12,256,1,256]{3,2,1,0:T(2,128)(2,1)S(1)} %slice.52) | data formatting | bytes 3145728
  23.5 1.9 slice.66
  28.3 1.7 maximum_select_fusion.refs_1_.refs_2_
  30.0 1.6 collective-permute-start.3
  31.6 6.7 %collective-permute-start.2 = (bf16[8,256,256]{2,1,0:T(8,128)(2,1)S(1)}, bf16[8,256,256]{2,1,0:T(8,128)(2,1)}, u32[]{:S(2)}, u32[]{:S(2)}) collective-permute-start(bf16[8,256,256]{2,1,0:T(8,128)(2,1)S(1)} %maximum_select_fusion.refs_1_.refs_2_), channel_id=1, source_target_pairs={{0,8},{1,9},{2,10},{3,11},{4,12},{5,13},{6,14},{7,15},{8,0},{9,1},... | collective-permute-start | bytes 3145736 | tf_op jit(solution)/shard_map/ppermute | solution.py:247
  38.3 1.5 collective-permute-start.10
  40.5 7.4 %clear.1.refs_4_ = bf16[12,256,24,256]{3,2,1,0:T(8,128)(2,1)} custom-call(s32[2]{0:T(128)} %pad_add_fusion._.ids.refs_0_), custom_call_target="tpu_custom_call" | custom-call | flops 1 | bytes 1 | tf_op jit(solution)/shard_map/clear/pallas_call | solution.py:323
  50.0 4.8 %collective-permute-done.3.refs_3_.refs_4_ = bf16[8,256,256]{2,1,0:T(8,128)(2,1)} collective-permute-done((bf16[8,256,256]{2,1,0:T(8,128)(2,1)S(1)}, bf16[8,256,256]{2,1,0:T(8,128)(2,1)}, u32[]{:S(2)}, u32[]{:S(2)}) %collective-permute-start.3) | collective-permute-done | bytes 1048608 | tf_op jit(solution)/shard_map/ppermute | solution.py:247
  54.8 6.7 %collective-permute-done.2.refs_5_.refs_6_ = bf16[8,256,256]{2,1,0:T(8,128)(2,1)} collective-permute-done((bf16[8,256,256]{2,1,0:T(8,128)(2,1)S(1)}, bf16[8,256,256]{2,1,0:T(8,128)(2,1)}, u32[]{:S(2)}, u32[]{:S(2)}) %collective-permute-start.2) | collective-permute-done | bytes 1048608 | tf_op jit(solution)/shard_map/ppermute | solution.py:247
  63.9 3.5 %collective-permute-done.4 = bf16[1,256,256]{2,1,0:T(8,128)(2,1)S(1)} collective-permute-done((bf16[1,256,256]{2,1,0:T(8,128)(2,1)S(1)}, bf16[1,256,256]{2,1,0:T(8,128)(2,1)S(1)}, u32[]{:S(2)}, u32[]{:S(2)}) %collective-permute-start.4) | collective-permute-done | bytes 131104 | tf_op jit(solution)/shard_map/ppermute | solution.py:247
  68.2 18.6 %collective-permute-start.8 = (bf16[4,256,256]{2,1,0:T(8,128)(2,1)}, bf16[4,256,256]{2,1,0:T(8,128)(2,1)S(1)}, u32[]{:S(2)}, u32[]{:S(2)}) collective-permute-start(bf16[4,256,256]{2,1,0:T(8,128)(2,1)} %get-tuple-element.77), channel_id=1, source_target_pairs={{0,16},{1,17},{2,18},{3,19},{4,20},{5,21},{6,22},{7,23},{8,24},{9,... | collective-permute-start | bytes 1572872 | tf_op jit(solution)/shard_map/ppermute | solution.py:247
  86.8 2.3 fusion.1
  90.5 2.9 %link.1 = (bf16[512,512]{1,0:T(8,128)(2,1)}, bf16[512,512]{1,0:T(8,128)(2,1)}) custom-call(s32[2]{0:T(128)} %pad_add_fusion._.ids.refs_0_, bf16[4,256,256]{2,1,0:T(8,128)(2,1)} %copy-done.14, bf16[4,256,256]{2,1,0:T(8,128)(2,1)} %copy-done.17, bf16[512,512]{1,0:T(8,128)(2,1)} %bitcast.35), custom_call_target="tpu_custom_call" | custom-call | tf_op jit(solution)/shard_map/link/pallas_call | solution.py:266
  93.4 5.2 %collective-permute-done.8 = bf16[4,256,256]{2,1,0:T(8,128)(2,1)S(1)} collective-permute-done((bf16[4,256,256]{2,1,0:T(8,128)(2,1)}, bf16[4,256,256]{2,1,0:T(8,128)(2,1)S(1)}, u32[]{:S(2)}, u32[]{:S(2)}) %collective-permute-start.8) | collective-permute-done | bytes 524320 | tf_op jit(solution)/shard_map/ppermute | solution.py:247
  101.6 12.7 %collective-permute-start.11 = (bf16[8,256,256]{2,1,0:T(8,128)(2,1)S(1)}, bf16[8,256,256]{2,1,0:T(8,128)(2,1)S(1)}, u32[]{:S(2)}, u32[]{:S(2)}) collective-permute-start(bf16[8,256,256]{2,1,0:T(8,128)(2,1)S(1)} %maximum_select_fusion.1.refs_1_.refs_2_), channel_id=1, source_target_pairs={{0,8},{1,9},{2,10},{3,11},{4,12},{5,13},{6,14},{7,15},{8,0},{9,1},... | collective-permute-start | bytes 3145736 | tf_op jit(solution)/shard_map/ppermute | solution.py:247
  114.3 8.3 %cols_0.1.refs_1_ = bf16[8,1024,256]{2,1,0:T(8,128)(2,1)} custom-call(s32[2]{0:T(128)} %pad_add_fusion._.ids.refs_0_, bf16[8,256,256]{2,1,0:T(8,128)(2,1)} %copy-done, bf16[8,256,256]{2,1,0:T(8,128)(2,1)} %copy-done, bf16[8,256,256]{2,1,0:T(8,128)(2,1)} %collective-permute-done.3.refs_3_.refs_4_, ...), custom_call_target="tpu_custom_call" | custom-call | flops 1 | bytes 1 | tf_op jit(solution)/shard_map/cols_0/pallas_call | solution.py:299
  122.6 10.5 %rows.1.refs_2_ = bf16[12,256,1024]{2,1,0:T(8,128)(2,1)} custom-call(s32[2]{0:T(128)} %pad_add_fusion._.ids.refs_0_, bf16[12,256,256]{2,1,0:T(8,128)(2,1)} %bitcast.34, bf16[12,256,256]{2,1,0:T(8,128)(2,1)} %collective-permute-done.9.q1, bf16[12,256,256]{2,1,0:T(8,128)(2,1)} %collective-permute-done.10.q2, bf16[12,256,256]{2,1,0:T(8,128)(2,1)} %collective-permute-done.13.q3, ...), custom_call_target="tpu_custom_call" | custom-call | flops 1 | bytes 1 | tf_op jit(solution)/shard_map/rows/pallas_call | solution.py:279
  133.1 4.2 %collective-permute-done.11.refs_5_.refs_6_ = bf16[8,256,256]{2,1,0:T(8,128)(2,1)S(1)} collective-permute-done((bf16[8,256,256]{2,1,0:T(8,128)(2,1)S(1)}, bf16[8,256,256]{2,1,0:T(8,128)(2,1)S(1)}, u32[]{:S(2)}, u32[]{:S(2)}) %collective-permute-start.11) | collective-permute-done | bytes 1048608 | tf_op jit(solution)/shard_map/ppermute | solution.py:247
  137.4 1.6 collective-permute-start.16
  139.0 8.3 %collective-permute-start.14 = (bf16[4,256,256]{2,1,0:T(8,128)(2,1)}, bf16[4,256,256]{2,1,0:T(8,128)(2,1)}, u32[]{:S(2)}, u32[]{:S(2)}) collective-permute-start(bf16[4,256,256]{2,1,0:T(8,128)(2,1)} %get-tuple-element.55), channel_id=1, source_target_pairs={{0,16},{1,17},{2,18},{3,19},{4,20},{5,21},{6,22},{7,23},{8,24},{9,... | collective-permute-start | bytes 1572872 | tf_op jit(solution)/shard_map/ppermute | solution.py:247
  148.8 22.5 %update_0_0.1.refs_4_ = bf16[12,256,24,256]{3,2,1,0:T(8,128)(2,1)} custom-call(s32[2]{0:T(128)} %pad_add_fusion._.ids.refs_0_, bf16[8,1024,256]{2,1,0:T(8,128)(2,1)} %cols_0.1.refs_1_, bf16[12,256,1024]{2,1,0:T(8,128)(2,1)} %rows.1.refs_2_, bf16[12,256,24,256]{3,2,1,0:T(8,128)(2,1)} %bitcast.24, ...), custom_call_target="tpu_custom_call", output_to_operand_aliasing={{}: (4, {})} | custom-call | flops 1 | bytes 1 | tf_op jit(solution)/shard_map/update_0_0/pallas_call | solution.py:340
  175.0 1.7 collective-permute-start.17
  176.7 8.3 %cols_8.1.refs_1_ = bf16[8,1024,256]{2,1,0:T(8,128)(2,1)} custom-call(s32[2]{0:T(128)} %pad_add_fusion._.ids.refs_0_, bf16[8,256,256]{2,1,0:T(8,128)(2,1)} %copy-done.2, bf16[8,256,256]{2,1,0:T(8,128)(2,1)} %copy-done.2, bf16[8,256,256]{2,1,0:T(8,128)(2,1)} %copy-done.7, bf16[8,256,256]{2,1,0:T(8,128)(2,1)} %copy-done.7, bf16[8,256,256]{2,1,0:T(8,128)(2,1)} %copy-done.8, ...), custom_call_target="tpu_custom_call" | custom-call | flops 1 | bytes 1 | tf_op jit(solution)/shard_map/cols_8/pallas_call | solution.py:299
  185.0 10.2 %update_1_4.1.refs_4_ = bf16[12,256,24,256]{3,2,1,0:T(8,128)(2,1)} custom-call(s32[2]{0:T(128)} %pad_add_fusion._.ids.refs_0_, bf16[8,1024,256]{2,1,0:T(8,128)(2,1)} %cols_8.1.refs_1_, bf16[12,256,1024]{2,1,0:T(8,128)(2,1)} %rows.1.refs_2_, bf16[12,256,24,256]{3,2,1,0:T(8,128)(2,1)} %bitcast.25, ...), custom_call_target="tpu_custom_call", output_to_operand_aliasing={{}: (4, {})} | custom-call | flops 1 | bytes 1 | tf_op jit(solution)/shard_map/update_1_4/pallas_call | solution.py:340
  199.7 1.7 collective-permute-start.20
  201.4 10.5 %update_1_8.1.refs_4_ = bf16[12,256,24,256]{3,2,1,0:T(8,128)(2,1)} custom-call(s32[2]{0:T(128)} %pad_add_fusion._.ids.refs_0_, bf16[8,1024,256]{2,1,0:T(8,128)(2,1)} %cols_8.1.refs_1_, bf16[12,256,1024]{2,1,0:T(8,128)(2,1)} %rows.1.refs_2_, bf16[12,256,24,256]{3,2,1,0:T(8,128)(2,1)} %bitcast.26, ...), custom_call_target="tpu_custom_call", output_to_operand_aliasing={{}: (4, {})} | custom-call | flops 1 | bytes 1 | tf_op jit(solution)/shard_map/update_1_8/pallas_call | solution.py:340
  213.6 8.3 %cols_16.1.refs_1_ = bf16[8,1024,256]{2,1,0:T(8,128)(2,1)} custom-call(s32[2]{0:T(128)} %pad_add_fusion._.ids.refs_0_, bf16[8,256,256]{2,1,0:T(8,128)(2,1)} %copy-done.1, bf16[8,256,256]{2,1,0:T(8,128)(2,1)} %copy-done.1, bf16[8,256,256]{2,1,0:T(8,128)(2,1)} %copy-done.5, bf16[8,256,256]{2,1,0:T(8,128)(2,1)} %copy-done.5, bf16[8,256,256]{2,1,0:T(8,128)(2,1)} %copy-done.6, ...), custom_call_target="tpu_custom_call" | custom-call | flops 1 | bytes 1 | tf_op jit(solution)/shard_map/cols_16/pallas_call | solution.py:299
  221.8 10.2 %update_2_8.1 = bf16[12,256,24,256]{3,2,1,0:T(8,128)(2,1)} custom-call(s32[2]{0:T(128)} %pad_add_fusion._.ids.refs_0_, bf16[8,1024,256]{2,1,0:T(8,128)(2,1)} %cols_16.1.refs_1_, bf16[12,256,1024]{2,1,0:T(8,128)(2,1)} %rows.1.refs_2_, bf16[12,256,24,256]{3,2,1,0:T(8,128)(2,1)} %bitcast.27, ...), custom_call_target="tpu_custom_call", output_to_operand_aliasing={{}: (4, {})} | custom-call | flops 1 | bytes 1 | tf_op jit(solution)/shard_map/update_2_8/pallas_call | solution.py:340
  (79 shorter events, 25.2 us)
Async XLA Ops:
  4.9 23.4 %collective-permute-start = (bf16[4,256,256]{2,1,0:T(8,128)(2,1)}, bf16[4,256,256]{2,1,0:T(8,128)(2,1)}, u32[]{:S(2)}, u32[]{:S(2)}) collective-permute-start(bf16[4,256,256]{2,1,0:T(8,128)(2,1)} %get-tuple-element.79), channel_id=1, source_target_pairs={{0,16},{1,17},{2,18},{3,19},{4,20},{5,21},{6,22},{7,23},{8,24},{9,... | collective-permute-start | bytes 1572872 | tf_op jit(solution)/shard_map/ppermute | solution.py:247
  25.4 2.9 %collective-permute-start.1 = (bf16[4,256,256]{2,1,0:T(8,128)(2,1)}, bf16[4,256,256]{2,1,0:T(8,128)(2,1)}, u32[]{:S(2)}, u32[]{:S(2)}) collective-permute-start(bf16[4,256,256]{2,1,0:T(8,128)(2,1)} %slice.66), channel_id=1, source_target_pairs={{16,16},{17,20},{18,24},{19,28},{20,17},{21,21},{22,25},{23,29},{2... | collective-permute-start | bytes 1572872 | tf_op jit(solution)/shard_map/ppermute | solution.py:247
  30.0 33.0 %copy-start = (bf16[8,256,256]{2,1,0:T(8,128)(2,1)}, bf16[8,256,256]{2,1,0:T(8,128)(2,1)S(1)}, u32[]{:S(2)}) copy-start(bf16[8,256,256]{2,1,0:T(8,128)(2,1)S(1)} %maximum_select_fusion.refs_1_.refs_2_) | copy-start | bytes 3145732
  30.0 24.8 %collective-permute-start.3 = (bf16[8,256,256]{2,1,0:T(8,128)(2,1)S(1)}, bf16[8,256,256]{2,1,0:T(8,128)(2,1)}, u32[]{:S(2)}, u32[]{:S(2)}) collective-permute-start(bf16[8,256,256]{2,1,0:T(8,128)(2,1)S(1)} %maximum_select_fusion.refs_1_.refs_2_), channel_id=1, source_target_pairs={{0,4},{1,5},{2,6},{3,7},{4,0},{5,1},{6,2},{7,3},{8,12},{9,13},{10,... | collective-permute-start | bytes 3145736 | tf_op jit(solution)/shard_map/ppermute | solution.py:247
  31.6 29.9 %collective-permute-start.2 = (bf16[8,256,256]{2,1,0:T(8,128)(2,1)S(1)}, bf16[8,256,256]{2,1,0:T(8,128)(2,1)}, u32[]{:S(2)}, u32[]{:S(2)}) collective-permute-start(bf16[8,256,256]{2,1,0:T(8,128)(2,1)S(1)} %maximum_select_fusion.refs_1_.refs_2_), channel_id=1, source_target_pairs={{0,8},{1,9},{2,10},{3,11},{4,12},{5,13},{6,14},{7,15},{8,0},{9,1},... | collective-permute-start | bytes 3145736 | tf_op jit(solution)/shard_map/ppermute | solution.py:247
  38.3 60.3 %collective-permute-start.10 = (bf16[12,256,256]{2,1,0:T(8,128)(2,1)}, bf16[12,256,256]{2,1,0:T(8,128)(2,1)}, u32[]{:S(2)}, u32[]{:S(2)}) collective-permute-start(bf16[12,256,256]{2,1,0:T(8,128)(2,1)} %bitcast.32), channel_id=1, source_target_pairs={{0,2},{1,3},{2,0},{3,1},{4,6},{5,7},{6,4},{7,5},{8,10},{9,11},{10,... | collective-permute-start | bytes 4718600 | tf_op jit(solution)/shard_map/ppermute | solution.py:247
  39.9 58.8 %collective-permute-start.9 = (bf16[12,256,256]{2,1,0:T(8,128)(2,1)}, bf16[12,256,256]{2,1,0:T(8,128)(2,1)}, u32[]{:S(2)}, u32[]{:S(2)}) collective-permute-start(bf16[12,256,256]{2,1,0:T(8,128)(2,1)} %bitcast.33), channel_id=1, source_target_pairs={{0,1},{1,0},{2,3},{3,2},{4,5},{5,4},{6,7},{7,6},{8,9},{9,8},{10,11... | collective-permute-start | bytes 4718600 | tf_op jit(solution)/shard_map/ppermute | solution.py:247
  47.9 51.8 %copy-start.12 = (bf16[4,256,256]{2,1,0:T(8,128)(2,1)S(1)}, bf16[4,256,256]{2,1,0:T(8,128)(2,1)}, u32[]{:S(2)}) copy-start(bf16[4,256,256]{2,1,0:T(8,128)(2,1)} %get-tuple-element.76) | copy-start | bytes 1572868
  48.9 50.8 %copy-start.13 = (bf16[4,256,256]{2,1,0:T(8,128)(2,1)S(1)}, bf16[4,256,256]{2,1,0:T(8,128)(2,1)}, u32[]{:S(2)}) copy-start(bf16[4,256,256]{2,1,0:T(8,128)(2,1)} %get-tuple-element.77) | copy-start | bytes 1572868
  62.4 5.0 %collective-permute-start.4 = (bf16[1,256,256]{2,1,0:T(8,128)(2,1)S(1)}, bf16[1,256,256]{2,1,0:T(8,128)(2,1)S(1)}, u32[]{:S(2)}, u32[]{:S(2)}) collective-permute-start(bf16[1,256,256]{2,1,0:T(8,128)(2,1)S(1)} %slice.57), channel_id=1, source_target_pairs={{0,4},{1,5},{2,6},{3,7},{4,0},{5,1},{6,2},{7,3},{8,12},{9,13},{10,... | collective-permute-start | bytes 393224 | tf_op jit(solution)/shard_map/ppermute | solution.py:247
  67.5 23.0 %copy-start.14 = (bf16[4,256,256]{2,1,0:T(8,128)(2,1)}, bf16[4,256,256]{2,1,0:T(8,128)(2,1)S(1)}, u32[]{:S(2)}) copy-start(bf16[4,256,256]{2,1,0:T(8,128)(2,1)S(1)} %pad_maximum_fusion.mine) | copy-start | bytes 1572868
  67.5 21.5 %collective-permute-start.5 = (bf16[4,256,256]{2,1,0:T(8,128)(2,1)S(1)}, bf16[4,256,256]{2,1,0:T(8,128)(2,1)S(1)}, u32[]{:S(2)}, u32[]{:S(2)}) collective-permute-start(bf16[4,256,256]{2,1,0:T(8,128)(2,1)S(1)} %pad_maximum_fusion.mine), channel_id=1, source_target_pairs={{0,1},{1,0},{2,3},{3,2},{4,5},{5,4},{6,7},{7,6},{8,9},{9,8},{10,11... | collective-permute-start | bytes 1572872 | tf_op jit(solution)/shard_map/ppermute | solution.py:247
  67.6 31.0 %collective-permute-start.6 = (bf16[8,256,256]{2,1,0:T(8,128)(2,1)}, bf16[8,256,256]{2,1,0:T(8,128)(2,1)S(1)}, u32[]{:S(2)}, u32[]{:S(2)}) collective-permute-start(bf16[8,256,256]{2,1,0:T(8,128)(2,1)} %collective-permute-done.2.refs_5_.refs_6_), channel_id=1, source_target_pairs={{0,4},{1,5},{2,6},{3,7},{4,0},{5,1},{6,2},{7,3},{8,12},{9,13},{10,... | collective-permute-start | bytes 3145736 | tf_op jit(solution)/shard_map/ppermute | solution.py:247
  68.2 30.4 %collective-permute-start.8 = (bf16[4,256,256]{2,1,0:T(8,128)(2,1)}, bf16[4,256,256]{2,1,0:T(8,128)(2,1)S(1)}, u32[]{:S(2)}, u32[]{:S(2)}) collective-permute-start(bf16[4,256,256]{2,1,0:T(8,128)(2,1)} %get-tuple-element.77), channel_id=1, source_target_pairs={{0,16},{1,17},{2,18},{3,19},{4,20},{5,21},{6,22},{7,23},{8,24},{9,... | collective-permute-start | bytes 1572872 | tf_op jit(solution)/shard_map/ppermute | solution.py:247
  89.1 9.6 %collective-permute-start.7 = (bf16[4,256,256]{2,1,0:T(8,128)(2,1)}, bf16[4,256,256]{2,1,0:T(8,128)(2,1)}, u32[]{:S(2)}, u32[]{:S(2)}) collective-permute-start(bf16[4,256,256]{2,1,0:T(8,128)(2,1)} %get-tuple-element.81), channel_id=1, source_target_pairs={{16,16},{17,20},{18,24},{19,28},{20,17},{21,21},{22,25},{23,29},{2... | collective-permute-start | bytes 1572872 | tf_op jit(solution)/shard_map/ppermute | solution.py:247
  98.6 23.9 %collective-permute-start.13 = (bf16[12,256,256]{2,1,0:T(8,128)(2,1)}, bf16[12,256,256]{2,1,0:T(8,128)(2,1)}, u32[]{:S(2)}, u32[]{:S(2)}) collective-permute-start(bf16[12,256,256]{2,1,0:T(8,128)(2,1)} %collective-permute-done.10.q2), channel_id=1, source_target_pairs={{0,1},{1,0},{2,3},{3,2},{4,5},{5,4},{6,7},{7,6},{8,9},{9,8},{10,11... | collective-permute-start | bytes 4718600 | tf_op jit(solution)/shard_map/ppermute | solution.py:247
  101.1 21.4 %copy-start.2 = (bf16[8,256,256]{2,1,0:T(8,128)(2,1)}, bf16[8,256,256]{2,1,0:T(8,128)(2,1)S(1)}, u32[]{:S(2)}) copy-start(bf16[8,256,256]{2,1,0:T(8,128)(2,1)S(1)} %maximum_select_fusion.1.refs_1_.refs_2_) | copy-start | bytes 3145732
  101.1 32.0 %collective-permute-start.12 = (bf16[8,256,256]{2,1,0:T(8,128)(2,1)S(1)}, bf16[8,256,256]{2,1,0:T(8,128)(2,1)S(1)}, u32[]{:S(2)}, u32[]{:S(2)}) collective-permute-start(bf16[8,256,256]{2,1,0:T(8,128)(2,1)S(1)} %maximum_select_fusion.1.refs_1_.refs_2_), channel_id=1, source_target_pairs={{0,4},{1,5},{2,6},{3,7},{4,0},{5,1},{6,2},{7,3},{8,12},{9,13},{10,... | collective-permute-start | bytes 3145736 | tf_op jit(solution)/shard_map/ppermute | solution.py:247
  101.6 35.7 %collective-permute-start.11 = (bf16[8,256,256]{2,1,0:T(8,128)(2,1)S(1)}, bf16[8,256,256]{2,1,0:T(8,128)(2,1)S(1)}, u32[]{:S(2)}, u32[]{:S(2)}) collective-permute-start(bf16[8,256,256]{2,1,0:T(8,128)(2,1)S(1)} %maximum_select_fusion.1.refs_1_.refs_2_), channel_id=1, source_target_pairs={{0,8},{1,9},{2,10},{3,11},{4,12},{5,13},{6,14},{7,15},{8,0},{9,1},... | collective-permute-start | bytes 3145736 | tf_op jit(solution)/shard_map/ppermute | solution.py:247
  133.1 38.2 %copy-start.7 = (bf16[8,256,256]{2,1,0:T(8,128)(2,1)}, bf16[8,256,256]{2,1,0:T(8,128)(2,1)S(1)}, u32[]{:S(2)}) copy-start(bf16[8,256,256]{2,1,0:T(8,128)(2,1)S(1)} %collective-permute-done.12.refs_3_.refs_4_) | copy-start | bytes 3145732
  137.4 33.9 %copy-start.8 = (bf16[8,256,256]{2,1,0:T(8,128)(2,1)}, bf16[8,256,256]{2,1,0:T(8,128)(2,1)S(1)}, u32[]{:S(2)}) copy-start(bf16[8,256,256]{2,1,0:T(8,128)(2,1)S(1)} %collective-permute-done.11.refs_5_.refs_6_) | copy-start | bytes 3145732
  137.4 34.0 %collective-permute-start.16 = (bf16[8,256,256]{2,1,0:T(8,128)(2,1)S(1)}, bf16[8,256,256]{2,1,0:T(8,128)(2,1)S(1)}, u32[]{:S(2)}, u32[]{:S(2)}) collective-permute-start(bf16[8,256,256]{2,1,0:T(8,128)(2,1)S(1)} %collective-permute-done.11.refs_5_.refs_6_), channel_id=1, source_target_pairs={{0,4},{1,5},{2,6},{3,7},{4,0},{5,1},{6,2},{7,3},{8,12},{9,13},{10,... | collective-permute-start | bytes 3145736 | tf_op jit(solution)/shard_map/ppermute | solution.py:247
  139.0 33.4 %copy-start.11 = (bf16[4,256,256]{2,1,0:T(8,128)(2,1)S(1)}, bf16[4,256,256]{2,1,0:T(8,128)(2,1)}, u32[]{:S(2)}) copy-start(bf16[4,256,256]{2,1,0:T(8,128)(2,1)} %get-tuple-element.74) | copy-start | bytes 1572868
  139.0 32.3 %collective-permute-start.14 = (bf16[4,256,256]{2,1,0:T(8,128)(2,1)}, bf16[4,256,256]{2,1,0:T(8,128)(2,1)}, u32[]{:S(2)}, u32[]{:S(2)}) collective-permute-start(bf16[4,256,256]{2,1,0:T(8,128)(2,1)} %get-tuple-element.55), channel_id=1, source_target_pairs={{0,16},{1,17},{2,18},{3,19},{4,20},{5,21},{6,22},{7,23},{8,24},{9,... | collective-permute-start | bytes 1572872 | tf_op jit(solution)/shard_map/ppermute | solution.py:247
  147.3 24.0 %collective-permute-start.15 = (bf16[4,256,256]{2,1,0:T(8,128)(2,1)}, bf16[4,256,256]{2,1,0:T(8,128)(2,1)}, u32[]{:S(2)}, u32[]{:S(2)}) collective-permute-start(bf16[4,256,256]{2,1,0:T(8,128)(2,1)} %get-tuple-element.56), channel_id=1, source_target_pairs={{16,16},{17,20},{18,24},{19,28},{20,17},{21,21},{22,25},{23,29},{2... | collective-permute-start | bytes 1572872 | tf_op jit(solution)/shard_map/ppermute | solution.py:247
  173.9 11.1 %copy-start.1 = (bf16[8,256,256]{2,1,0:T(8,128)(2,1)}, bf16[8,256,256]{2,1,0:T(8,128)(2,1)S(1)}, u32[]{:S(2)}) copy-start(bf16[8,256,256]{2,1,0:T(8,128)(2,1)S(1)} %maximum_select_fusion.2.refs_1_.refs_2_) | copy-start | bytes 3145732
  173.9 22.5 %collective-permute-start.18 = (bf16[8,256,256]{2,1,0:T(8,128)(2,1)S(1)}, bf16[8,256,256]{2,1,0:T(8,128)(2,1)S(1)}, u32[]{:S(2)}, u32[]{:S(2)}) collective-permute-start(bf16[8,256,256]{2,1,0:T(8,128)(2,1)S(1)} %maximum_select_fusion.2.refs_1_.refs_2_), channel_id=1, source_target_pairs={{0,4},{1,5},{2,6},{3,7},{4,0},{5,1},{6,2},{7,3},{8,12},{9,13},{10,... | collective-permute-start | bytes 3145736 | tf_op jit(solution)/shard_map/ppermute | solution.py:247
  175.0 22.9 %collective-permute-start.17 = (bf16[8,256,256]{2,1,0:T(8,128)(2,1)S(1)}, bf16[8,256,256]{2,1,0:T(8,128)(2,1)S(1)}, u32[]{:S(2)}, u32[]{:S(2)}) collective-permute-start(bf16[8,256,256]{2,1,0:T(8,128)(2,1)S(1)} %maximum_select_fusion.2.refs_1_.refs_2_), channel_id=1, source_target_pairs={{0,8},{1,9},{2,10},{3,11},{4,12},{5,13},{6,14},{7,15},{8,0},{9,1},... | collective-permute-start | bytes 3145736 | tf_op jit(solution)/shard_map/ppermute | solution.py:247
  196.4 15.4 %copy-start.5 = (bf16[8,256,256]{2,1,0:T(8,128)(2,1)}, bf16[8,256,256]{2,1,0:T(8,128)(2,1)S(1)}, u32[]{:S(2)}) copy-start(bf16[8,256,256]{2,1,0:T(8,128)(2,1)S(1)} %collective-permute-done.18.refs_3_.refs_4_) | copy-start | bytes 3145732
  197.9 14.0 %copy-start.6 = (bf16[8,256,256]{2,1,0:T(8,128)(2,1)}, bf16[8,256,256]{2,1,0:T(8,128)(2,1)S(1)}, u32[]{:S(2)}) copy-start(bf16[8,256,256]{2,1,0:T(8,128)(2,1)S(1)} %collective-permute-done.17.refs_5_.refs_6_) | copy-start | bytes 3145732
  198.9 13.0 %collective-permute-start.19 = (bf16[4,256,256]{2,1,0:T(8,128)(2,1)}, bf16[4,256,256]{2,1,0:T(8,128)(2,1)S(1)}, u32[]{:S(2)}, u32[]{:S(2)}) collective-permute-start(bf16[4,256,256]{2,1,0:T(8,128)(2,1)} %slice.64), channel_id=1, source_target_pairs={{0,4},{1,5},{2,6},{3,7},{4,0},{5,1},{6,2},{7,3},{8,12},{9,13},{10,... | collective-permute-start | bytes 1572872 | tf_op jit(solution)/shard_map/ppermute | solution.py:247
  199.7 12.2 %collective-permute-start.20 = (bf16[4,256,256]{2,1,0:T(8,128)(2,1)S(1)}, bf16[4,256,256]{2,1,0:T(8,128)(2,1)S(1)}, u32[]{:S(2)}, u32[]{:S(2)}) collective-permute-start(bf16[4,256,256]{2,1,0:T(8,128)(2,1)S(1)} %slice.65), channel_id=1, source_target_pairs={{0,8},{1,9},{2,10},{3,11},{4,12},{5,13},{6,14},{7,15},{8,0},{9,1},... | collective-permute-start | bytes 1572872 | tf_op jit(solution)/shard_map/ppermute | solution.py:247
  (9 other events, 23.8 us)

commit v4 on v3

--- a/solution.py
+++ b/solution.py
@@ -309,9 +309,9 @@
         )(ids, *[array for array, _ in pieces], inv_first, inv_second, low)
 
     def cost(flops, size):
-        return pl.CostEstimate(flops=1, bytes_accessed=1, transcendentals=0)
-
-    def clear():
+        return pl.CostEstimate(flops=flops, bytes_accessed=size, transcendentals=0)
+
+    def clear(gate):
         def place(i):
             group, first = 1, 0
             for g in range(1, groups):
@@ -329,7 +329,7 @@
             compiler_params=params(),
             cost_estimate=cost(0, tiles * tile * SUB * tile * 2),
             name="clear",
-        )(ids)
+        )(together(ids, gate)[0])
 
     def update(result, group, start, stop, cols, panels):
         grid_block = pl.BlockSpec((1, tile, SUB, tile), lambda t: (t + start, 0, group, 0))
@@ -376,27 +376,28 @@
         return factor_cols(group * SUB, pieces + [even_zy, odd_zy], low)
 
     lift_0 = lift(even[0])
-    strip = together(view, even[0])[0][:, :, 0, :]
-    swapped = jnp.swapaxes(strip, 1, 2)
-    cross_0 = cross(swapped[:half])
-    result = clear()
-    lift_0, cross_0, strip, swapped = together(lift_0, cross_0, strip, swapped)
+    strip_a = together(view, even[0])[0][:half, :, 0, :]
+    cross_0 = cross(jnp.swapaxes(strip_a, 1, 2))
+    lift_0, cross_0, source, inv0t, inv1t = together(lift_0, cross_0, view, inv0t, inv1t)
 
     base_0 = pick(0, lift_0, cross_0)
     z_0, y_0 = across_z(base_0), across_y(base_0)
+    strip_b = source[half:, :, 0, :]
+    swapped = jnp.swapaxes(strip_b, 1, 2)
+    strip = jnp.concatenate([strip_a, strip_b])
     strip_2 = across_x(strip)
-    z_0, y_0, result, inv0t, inv1t, cross_0, lift_0 = together(z_0, y_0, result, inv0t, inv1t, cross_0, lift_0)
-
-    first_zy = across_y(z_0[:1])
+    z_0, y_0, cross_0, lift_0, swapped = together(z_0, y_0, cross_0, lift_0, swapped)
+
     both_0 = across_y(z_0)
-    cross_1 = cross(together(swapped[half : 2 * half], cross_0)[0])
+    cross_1 = cross(together(swapped[:half], cross_0)[0])
     lift_1 = lift(together(even[1], lift_0)[0])
     strip_1 = across_core(strip)
-    mine = jnp.concatenate([base_0[:1], y_0[:1], z_0[:1], first_zy])
+    result = clear(z_0)
+    both_0, cross_1, lift_1, strip_1, strip_2, result = together(both_0, cross_1, lift_1, strip_1, strip_2, result)
+
+    mine = jnp.concatenate([base_0[:1], y_0[:1], z_0[:1], both_0[:1]])
     other = across_core(mine)
     low, lowt = factor_link(mine, other)
-    low, both_0, cross_1, lift_1, strip_1, strip_2 = together(low, both_0, cross_1, lift_1, strip_1, strip_2)
-
     base_1 = pick(1, lift_1, cross_1)
     z_1, y_1 = across_z(base_1), across_y(base_1)
     strip_3 = across_core(strip_2)
@@ -405,7 +406,7 @@
     z_1, y_1, cols_0, panels = together(z_1, y_1, cols_0, panels)
 
     lift_2 = lift(together(even[2], z_1)[0])
-    cross_2 = cross(together(swapped[2 * half :], z_1)[0])
+    cross_2 = cross(together(swapped[half:], z_1)[0])
     both_1 = across_y(z_1)
     result = update(result, 0, 0, tiles, cols_0, panels)
     lift_2, cross_2, both_1, result = together(lift_2, cross_2, both_1, result)

time: 234 us -> 223 us (0.953)
  waiting for transfers between devices: 27.2 us -> 21 us
  local copies, waits for them, and re-layouts: 30.4 us -> 25.9 us
    ppermute x21 -> x20, waiting for transfers between devices: 27.2 us -> 21 us  [move(): return lax.ppermute(value, ('row', 'col'), pairs)]
    unnamed x43, local copies, waits for them, and re-layouts: 13 us -> 9.78 us
    ppermute x21 -> x20, starting transfers between devices: 69.2 us -> 67.5 us  [move(): return lax.ppermute(value, ('row', 'col'), pairs)]
    slice x6 -> x7, local copies, waits for them, and re-layouts: 12.8 us -> 11.7 us  [the longest x1 4.73 us: local(): strip_b = source[half:, :, 0, :]]
  transfers between devices with their start and end apart: 21 -> 20, of which waited for: 7 -> 6; matrix products, arithmetic and copies ran while one was open for 10% -> 10% of each run, Pallas kernels for 35% -> 36%
where the time goes in v4:
time: 223 us; the launch traced here: 221 us
  Pallas kernels  99 us (44%)
  starting transfers between devices  67.5 us (30%)
  local copies, waits for them, and re-layouts  25.9 us (12%)
  waiting for transfers between devices  21 us (9%)
  other arithmetic  6.57 us (3%)
    ppermute x20, starting transfers between devices, move(): return lax.ppermute(value, ('row', 'col'), pairs)  67.5 us
    pallas_call x4, Pallas kernels, update(): pl.pallas_call(kernel, grid=(stop - start,), in_specs=[smem, whole(cols),...  53.3 us
    pallas_call x3, Pallas kernels, factor_cols(): pl.pallas_call(kernel, grid=(SUB // 2,), in_specs=[smem, *blocks, whole(i...  24.9 us
    ppermute x20, waiting for transfers between devices, move(): return lax.ppermute(value, ('row', 'col'), pairs)  21 us
    pallas_call x1, Pallas kernels, factor_rows(): pl.pallas_call(rows_kernel, grid=(tiles // count,), in_specs=[smem, *[blo...  10.5 us
    unnamed x43, local copies, waits for them, and re-layouts  9.78 us
    pallas_call x1, Pallas kernels, clear(): pl.pallas_call(zeros_kernel, grid=(ratio * groups * (groups - 1) // 2,),...  7.4 us
    slice x1, local copies, waits for them, and re-layouts, local(): strip_b = source[half:, :, 0, :]  4.73 us
  transfers between devices with their start and end apart: 20, of which 6 were waited for; matrix products, arithmetic and copies ran while one was open for 10% of the time, Pallas kernels for 36%

profile of v4, /device:TPU:0, one launch (start us, length us, event | category | flops | bytes accessed | tf_op | source)
XLA Modules:
  0.0 220.9 jit_solution(7970442451935553269)
XLA Ops:
  0.6 1.9 slice-done
  3.2 1.5 fusion
  4.8 6.9 %collective-permute-start = (bf16[4,256,256]{2,1,0:T(8,128)(2,1)S(1)}, bf16[4,256,256]{2,1,0:T(8,128)(2,1)}, u32[]{:S(2)}, u32[]{:S(2)}) collective-permute-start(bf16[4,256,256]{2,1,0:T(8,128)(2,1)S(1)} %get-tuple-element.81), channel_id=1, source_target_pairs={{0,16},{1,17},{2,18},{3,19},{4,20},{5,21},{6,22},{7,23},{8,24},{9,... | collective-permute-start | bytes 1572872 | tf_op jit(solution)/shard_map/ppermute | solution.py:247
  11.7 2.7 %slice.54 = bf16[4,256,1,256]{3,2,1,0:T(2,128)(2,1)S(1)} slice(bf16[12,256,24,256]{3,2,1,0:T(8,128)(2,1)} %bitcast.29), slice={[0:4], [0:256], [0:1], [0:256]} | slice | bytes 1048576 | tf_op jit(solution)/shard_map/slice | solution.py:379
  18.5 3.6 %collective-permute-done = bf16[4,256,256]{2,1,0:T(8,128)(2,1)} collective-permute-done((bf16[4,256,256]{2,1,0:T(8,128)(2,1)S(1)}, bf16[4,256,256]{2,1,0:T(8,128)(2,1)}, u32[]{:S(2)}, u32[]{:S(2)}) %collective-permute-start) | collective-permute-done | bytes 524320 | tf_op jit(solution)/shard_map/ppermute | solution.py:247
  22.1 1.7 maximum_select_fusion.refs_1_.refs_2_
  23.8 1.6 collective-permute-start.3
  25.3 12.7 %collective-permute-start.2 = (bf16[8,256,256]{2,1,0:T(8,128)(2,1)S(1)}, bf16[8,256,256]{2,1,0:T(8,128)(2,1)}, u32[]{:S(2)}, u32[]{:S(2)}) collective-permute-start(bf16[8,256,256]{2,1,0:T(8,128)(2,1)S(1)} %maximum_select_fusion.refs_1_.refs_2_), channel_id=1, source_target_pairs={{0,8},{1,9},{2,10},{3,11},{4,12},{5,13},{6,14},{7,15},{8,0},{9,1},... | collective-permute-start | bytes 3145736 | tf_op jit(solution)/shard_map/ppermute | solution.py:247
  38.1 4.7 %slice.56 = bf16[8,256,1,256]{3,2,1,0:T(2,128)(2,1)S(1)} slice(bf16[12,256,24,256]{3,2,1,0:T(8,128)(2,1)} %bitcast.30), slice={[4:12], [0:256], [0:1], [0:256]} | slice | bytes 2097152 | tf_op jit(solution)/shard_map/slice | solution.py:385
  44.3 1.5 collective-permute-start.8
  45.9 3.4 %copy.83 = bf16[8,256,1,256]{1,3,0,2:T(8,128)(2,1)} copy(bf16[8,256,1,256]{3,2,1,0:T(2,128)(2,1)S(1)} %slice.56) | data formatting | bytes 2097152
  49.2 11.9 %collective-permute-done.2.refs_5_.refs_6_ = bf16[8,256,256]{2,1,0:T(8,128)(2,1)} collective-permute-done((bf16[8,256,256]{2,1,0:T(8,128)(2,1)S(1)}, bf16[8,256,256]{2,1,0:T(8,128)(2,1)}, u32[]{:S(2)}, u32[]{:S(2)}) %collective-permute-start.2) | collective-permute-done | bytes 1048608 | tf_op jit(solution)/shard_map/ppermute | solution.py:247
  61.7 11.6 %collective-permute-start.6 = (bf16[4,256,256]{2,1,0:T(8,128)(2,1)}, bf16[4,256,256]{2,1,0:T(8,128)(2,1)}, u32[]{:S(2)}, u32[]{:S(2)}) collective-permute-start(bf16[4,256,256]{2,1,0:T(8,128)(2,1)} %get-tuple-element.79), channel_id=1, source_target_pairs={{0,16},{1,17},{2,18},{3,19},{4,20},{5,21},{6,22},{7,23},{8,24},{9,... | collective-permute-start | bytes 1572872 | tf_op jit(solution)/shard_map/ppermute | solution.py:247
  73.3 2.2 %fusion.1 = (bf16[4,256,256]{2,1,0:T(8,128)(2,1)}, bf16[4,256,256]{2,1,0:T(8,128)(2,1)}) fusion(bf16[8,256,256]{2,1,0:T(8,128)(2,1)} %bitcast.38), kind=kLoop, calls=%fused_computation.10 | loop fusion | bytes 2097152 | tf_op jit(solution)/shard_map/slice | solution.py:409
  77.6 7.4 %clear.1.refs_4_ = bf16[12,256,24,256]{3,2,1,0:T(8,128)(2,1)} custom-call(s32[2]{0:T(128)} %pad_add_fusion._.ids.refs_0_), custom_call_target="tpu_custom_call" | custom-call | bytes 12582912 | tf_op jit(solution)/shard_map/clear/pallas_call | solution.py:323
  90.1 9.9 %collective-permute-start.9 = (bf16[8,256,256]{2,1,0:T(8,128)(2,1)S(1)}, bf16[8,256,256]{2,1,0:T(8,128)(2,1)S(1)}, u32[]{:S(2)}, u32[]{:S(2)}) collective-permute-start(bf16[8,256,256]{2,1,0:T(8,128)(2,1)S(1)} %maximum_select_fusion.1.refs_1_.refs_2_), channel_id=1, source_target_pairs={{0,8},{1,9},{2,10},{3,11},{4,12},{5,13},{6,14},{7,15},{8,0},{9,1},... | collective-permute-start | bytes 3145736 | tf_op jit(solution)/shard_map/ppermute | solution.py:247
  100.0 2.9 %link.1 = (bf16[512,512]{1,0:T(8,128)(2,1)}, bf16[512,512]{1,0:T(8,128)(2,1)}) custom-call(s32[2]{0:T(128)} %pad_add_fusion._.ids.refs_0_, bf16[4,256,256]{2,1,0:T(8,128)(2,1)} %copy-done.15, bf16[4,256,256]{2,1,0:T(8,128)(2,1)} %collective-permute-done.11.other, bf16[512,512]{1,0:T(8,128)(2,1)} %bitcast.39), custom_call_target="tpu_custom_call" | custom-call | tf_op jit(solution)/shard_map/link/pallas_call | solution.py:266
  102.9 8.3 %cols_0.1.refs_1_ = bf16[8,1024,256]{2,1,0:T(8,128)(2,1)} custom-call(s32[2]{0:T(128)} %pad_add_fusion._.ids.refs_0_, bf16[8,256,256]{2,1,0:T(8,128)(2,1)} %copy-done, bf16[8,256,256]{2,1,0:T(8,128)(2,1)} %copy-done, bf16[8,256,256]{2,1,0:T(8,128)(2,1)} %collective-permute-done.3.refs_3_.refs_4_, ...), custom_call_target="tpu_custom_call" | custom-call | flops 3221225472 | bytes 12582912 | tf_op jit(solution)/shard_map/cols_0/pallas_call | solution.py:299
  111.2 10.5 %rows.1.refs_2_ = bf16[12,256,1024]{2,1,0:T(8,128)(2,1)} custom-call(s32[2]{0:T(128)} %pad_add_fusion._.ids.refs_0_, bf16[12,256,256]{2,1,0:T(8,128)(2,1)} %pad_maximum_fusion.q0, bf16[12,256,256]{2,1,0:T(8,128)(2,1)} %collective-permute-done.7.q1, bf16[12,256,256]{2,1,0:T(8,128)(2,1)} %collective-permute-done.8.q2, ...), custom_call_target="tpu_custom_call" | custom-call | flops 4831838208 | bytes 18874368 | tf_op jit(solution)/shard_map/rows/pallas_call | solution.py:279
  121.8 1.5 collective-permute-done.9.refs_5_.refs_6_
  123.3 1.7 collective-permute-start.15
  124.9 10.6 %collective-permute-start.13 = (bf16[4,256,256]{2,1,0:T(8,128)(2,1)}, bf16[4,256,256]{2,1,0:T(8,128)(2,1)}, u32[]{:S(2)}, u32[]{:S(2)}) collective-permute-start(bf16[4,256,256]{2,1,0:T(8,128)(2,1)} %get-tuple-element.55), channel_id=1, source_target_pairs={{0,16},{1,17},{2,18},{3,19},{4,20},{5,21},{6,22},{7,23},{8,24},{9,... | collective-permute-start | bytes 1572872 | tf_op jit(solution)/shard_map/ppermute | solution.py:247
  137.0 22.5 %update_0_0.1.refs_4_ = bf16[12,256,24,256]{3,2,1,0:T(8,128)(2,1)} custom-call(s32[2]{0:T(128)} %pad_add_fusion._.ids.refs_0_, bf16[8,1024,256]{2,1,0:T(8,128)(2,1)} %cols_0.1.refs_1_, bf16[12,256,1024]{2,1,0:T(8,128)(2,1)} %rows.1.refs_2_, bf16[12,256,24,256]{3,2,1,0:T(8,128)(2,1)} %bitcast.31, ...), custom_call_target="tpu_custom_call", output_to_operand_aliasing={{}: (4, {})} | custom-call | flops 12884901888 | bytes 37748736 | tf_op jit(solution)/shard_map/update_0_0/pallas_call | solution.py:340
  160.7 1.5 maximum_select_fusion.2.refs_1_.refs_2_
  163.0 1.7 collective-permute-start.16
  164.8 8.3 %cols_8.1.refs_1_ = bf16[8,1024,256]{2,1,0:T(8,128)(2,1)} custom-call(s32[2]{0:T(128)} %pad_add_fusion._.ids.refs_0_, bf16[8,256,256]{2,1,0:T(8,128)(2,1)} %copy-done.2, bf16[8,256,256]{2,1,0:T(8,128)(2,1)} %copy-done.2, bf16[8,256,256]{2,1,0:T(8,128)(2,1)} %copy-done.8, bf16[8,256,256]{2,1,0:T(8,128)(2,1)} %copy-done.8, bf16[8,256,256]{2,1,0:T(8,128)(2,1)} %copy-done.9, ...), custom_call_target="tpu_custom_call" | custom-call | flops 3221225472 | bytes 12582912 | tf_op jit(solution)/shard_map/cols_8/pallas_call | solution.py:299
  173.1 10.2 %update_1_4.1.refs_4_ = bf16[12,256,24,256]{3,2,1,0:T(8,128)(2,1)} custom-call(s32[2]{0:T(128)} %pad_add_fusion._.ids.refs_0_, bf16[8,1024,256]{2,1,0:T(8,128)(2,1)} %cols_8.1.refs_1_, bf16[12,256,1024]{2,1,0:T(8,128)(2,1)} %rows.1.refs_2_, bf16[12,256,24,256]{3,2,1,0:T(8,128)(2,1)} %bitcast.32, ...), custom_call_target="tpu_custom_call", output_to_operand_aliasing={{}: (4, {})} | custom-call | flops 4294967296 | bytes 12582912 | tf_op jit(solution)/shard_map/update_1_4/pallas_call | solution.py:340
  183.2 2.1 collective-permute-done.17.refs_3_.refs_4_
  188.5 1.7 collective-permute-start.19
  190.3 10.5 %update_1_8.1.refs_4_ = bf16[12,256,24,256]{3,2,1,0:T(8,128)(2,1)} custom-call(s32[2]{0:T(128)} %pad_add_fusion._.ids.refs_0_, bf16[8,1024,256]{2,1,0:T(8,128)(2,1)} %cols_8.1.refs_1_, bf16[12,256,1024]{2,1,0:T(8,128)(2,1)} %rows.1.refs_2_, bf16[12,256,24,256]{3,2,1,0:T(8,128)(2,1)} %bitcast.33, ...), custom_call_target="tpu_custom_call", output_to_operand_aliasing={{}: (4, {})} | custom-call | flops 4294967296 | bytes 12582912 | tf_op jit(solution)/shard_map/update_1_8/pallas_call | solution.py:340
  202.5 8.3 %cols_16.1.refs_1_ = bf16[8,1024,256]{2,1,0:T(8,128)(2,1)} custom-call(s32[2]{0:T(128)} %pad_add_fusion._.ids.refs_0_, bf16[8,256,256]{2,1,0:T(8,128)(2,1)} %copy-done.1, bf16[8,256,256]{2,1,0:T(8,128)(2,1)} %copy-done.1, bf16[8,256,256]{2,1,0:T(8,128)(2,1)} %copy-done.5, bf16[8,256,256]{2,1,0:T(8,128)(2,1)} %copy-done.5, bf16[8,256,256]{2,1,0:T(8,128)(2,1)} %copy-done.6, ...), custom_call_target="tpu_custom_call" | custom-call | flops 3221225472 | bytes 12582912 | tf_op jit(solution)/shard_map/cols_16/pallas_call | solution.py:299
  210.8 10.2 %update_2_8.1 = bf16[12,256,24,256]{3,2,1,0:T(8,128)(2,1)} custom-call(s32[2]{0:T(128)} %pad_add_fusion._.ids.refs_0_, bf16[8,1024,256]{2,1,0:T(8,128)(2,1)} %cols_16.1.refs_1_, bf16[12,256,1024]{2,1,0:T(8,128)(2,1)} %rows.1.refs_2_, bf16[12,256,24,256]{3,2,1,0:T(8,128)(2,1)} %bitcast.34, ...), custom_call_target="tpu_custom_call", output_to_operand_aliasing={{}: (4, {})} | custom-call | flops 4294967296 | bytes 12582912 | tf_op jit(solution)/shard_map/update_2_8/pallas_call | solution.py:340
  (79 shorter events, 22.4 us)
Async XLA Ops:
  4.8 17.3 %copy-start.14 = (bf16[4,256,256]{2,1,0:T(8,128)(2,1)}, bf16[4,256,256]{2,1,0:T(8,128)(2,1)S(1)}, u32[]{:S(2)}) copy-start(bf16[4,256,256]{2,1,0:T(8,128)(2,1)S(1)} %get-tuple-element.81) | copy-start | bytes 1572868
  4.8 11.7 %copy-start.3 = (bf16[512,512]{1,0:T(8,128)(2,1)S(1)}, bf16[512,512]{1,0:T(8,128)(2,1)}, u32[]{:S(2)}) copy-start(bf16[512,512]{1,0:T(8,128)(2,1)} %refs_9_.5) | copy-start | bytes 1572868
  4.8 12.7 %copy-start.4 = (bf16[512,512]{1,0:T(8,128)(2,1)S(1)}, bf16[512,512]{1,0:T(8,128)(2,1)}, u32[]{:S(2)}) copy-start(bf16[512,512]{1,0:T(8,128)(2,1)} %refs_10_.5) | copy-start | bytes 1572868
  4.8 17.3 %collective-permute-start = (bf16[4,256,256]{2,1,0:T(8,128)(2,1)S(1)}, bf16[4,256,256]{2,1,0:T(8,128)(2,1)}, u32[]{:S(2)}, u32[]{:S(2)}) collective-permute-start(bf16[4,256,256]{2,1,0:T(8,128)(2,1)S(1)} %get-tuple-element.81), channel_id=1, source_target_pairs={{0,16},{1,17},{2,18},{3,19},{4,20},{5,21},{6,22},{7,23},{8,24},{9,... | collective-permute-start | bytes 1572872 | tf_op jit(solution)/shard_map/ppermute | solution.py:247
  15.0 7.0 %collective-permute-start.1 = (bf16[4,256,256]{2,1,0:T(8,128)(2,1)S(1)}, bf16[4,256,256]{2,1,0:T(8,128)(2,1)}, u32[]{:S(2)}, u32[]{:S(2)}) collective-permute-start(bf16[4,256,256]{2,1,0:T(8,128)(2,1)S(1)} %bitcast.42), channel_id=1, source_target_pairs={{16,16},{17,20},{18,24},{19,28},{20,17},{21,21},{22,25},{23,29},{2... | collective-permute-start | bytes 1572872 | tf_op jit(solution)/shard_map/ppermute | solution.py:247
  23.7 61.9 %copy-start = (bf16[8,256,256]{2,1,0:T(8,128)(2,1)}, bf16[8,256,256]{2,1,0:T(8,128)(2,1)S(1)}, u32[]{:S(2)}) copy-start(bf16[8,256,256]{2,1,0:T(8,128)(2,1)S(1)} %maximum_select_fusion.refs_1_.refs_2_) | copy-start | bytes 3145732
  23.8 25.5 %collective-permute-start.3 = (bf16[8,256,256]{2,1,0:T(8,128)(2,1)S(1)}, bf16[8,256,256]{2,1,0:T(8,128)(2,1)}, u32[]{:S(2)}, u32[]{:S(2)}) collective-permute-start(bf16[8,256,256]{2,1,0:T(8,128)(2,1)S(1)} %maximum_select_fusion.refs_1_.refs_2_), channel_id=1, source_target_pairs={{0,4},{1,5},{2,6},{3,7},{4,0},{5,1},{6,2},{7,3},{8,12},{9,13},{10,... | collective-permute-start | bytes 3145736 | tf_op jit(solution)/shard_map/ppermute | solution.py:247
  25.3 35.8 %collective-permute-start.2 = (bf16[8,256,256]{2,1,0:T(8,128)(2,1)S(1)}, bf16[8,256,256]{2,1,0:T(8,128)(2,1)}, u32[]{:S(2)}, u32[]{:S(2)}) collective-permute-start(bf16[8,256,256]{2,1,0:T(8,128)(2,1)S(1)} %maximum_select_fusion.refs_1_.refs_2_), channel_id=1, source_target_pairs={{0,8},{1,9},{2,10},{3,11},{4,12},{5,13},{6,14},{7,15},{8,0},{9,1},... | collective-permute-start | bytes 3145736 | tf_op jit(solution)/shard_map/ppermute | solution.py:247
  44.3 40.7 %collective-permute-start.8 = (bf16[12,256,256]{2,1,0:T(8,128)(2,1)}, bf16[12,256,256]{2,1,0:T(8,128)(2,1)}, u32[]{:S(2)}, u32[]{:S(2)}) collective-permute-start(bf16[12,256,256]{2,1,0:T(8,128)(2,1)} %pad_maximum_fusion.q0), channel_id=1, source_target_pairs={{0,2},{1,3},{2,0},{3,1},{4,6},{5,7},{6,4},{7,5},{8,10},{9,11},{10,... | collective-permute-start | bytes 4718600 | tf_op jit(solution)/shard_map/ppermute | solution.py:247
  45.9 39.1 %collective-permute-start.7 = (bf16[12,256,256]{2,1,0:T(8,128)(2,1)}, bf16[12,256,256]{2,1,0:T(8,128)(2,1)}, u32[]{:S(2)}, u32[]{:S(2)}) collective-permute-start(bf16[12,256,256]{2,1,0:T(8,128)(2,1)} %pad_maximum_fusion.q0), channel_id=1, source_target_pairs={{0,1},{1,0},{2,3},{3,2},{4,5},{5,4},{6,7},{7,6},{8,9},{9,8},{10,11... | collective-permute-start | bytes 4718600 | tf_op jit(solution)/shard_map/ppermute | solution.py:247
  61.2 24.4 %collective-permute-start.4 = (bf16[8,256,256]{2,1,0:T(8,128)(2,1)}, bf16[8,256,256]{2,1,0:T(8,128)(2,1)S(1)}, u32[]{:S(2)}, u32[]{:S(2)}) collective-permute-start(bf16[8,256,256]{2,1,0:T(8,128)(2,1)} %collective-permute-done.2.refs_5_.refs_6_), channel_id=1, source_target_pairs={{0,4},{1,5},{2,6},{3,7},{4,0},{5,1},{6,2},{7,3},{8,12},{9,13},{10,... | collective-permute-start | bytes 3145736 | tf_op jit(solution)/shard_map/ppermute | solution.py:247
  61.7 23.3 %collective-permute-start.6 = (bf16[4,256,256]{2,1,0:T(8,128)(2,1)}, bf16[4,256,256]{2,1,0:T(8,128)(2,1)}, u32[]{:S(2)}, u32[]{:S(2)}) collective-permute-start(bf16[4,256,256]{2,1,0:T(8,128)(2,1)} %get-tuple-element.79), channel_id=1, source_target_pairs={{0,16},{1,17},{2,18},{3,19},{4,20},{5,21},{6,22},{7,23},{8,24},{9,... | collective-permute-start | bytes 1572872 | tf_op jit(solution)/shard_map/ppermute | solution.py:247
  75.5 9.5 %collective-permute-start.5 = (bf16[4,256,256]{2,1,0:T(8,128)(2,1)}, bf16[4,256,256]{2,1,0:T(8,128)(2,1)}, u32[]{:S(2)}, u32[]{:S(2)}) collective-permute-start(bf16[4,256,256]{2,1,0:T(8,128)(2,1)} %get-tuple-element.83), channel_id=1, source_target_pairs={{16,16},{17,20},{18,24},{19,28},{20,17},{21,21},{22,25},{23,29},{2... | collective-permute-start | bytes 1572872 | tf_op jit(solution)/shard_map/ppermute | solution.py:247
  85.6 25.6 %collective-permute-start.12 = (bf16[12,256,256]{2,1,0:T(8,128)(2,1)}, bf16[12,256,256]{2,1,0:T(8,128)(2,1)}, u32[]{:S(2)}, u32[]{:S(2)}) collective-permute-start(bf16[12,256,256]{2,1,0:T(8,128)(2,1)} %collective-permute-done.8.q2), channel_id=1, source_target_pairs={{0,1},{1,0},{2,3},{3,2},{4,5},{5,4},{6,7},{7,6},{8,9},{9,8},{10,11... | collective-permute-start | bytes 4718600 | tf_op jit(solution)/shard_map/ppermute | solution.py:247
  87.7 12.3 %copy-start.15 = (bf16[4,256,256]{2,1,0:T(8,128)(2,1)}, bf16[4,256,256]{2,1,0:T(8,128)(2,1)S(1)}, u32[]{:S(2)}) copy-start(bf16[4,256,256]{2,1,0:T(8,128)(2,1)S(1)} %pad_maximum_fusion.1.mine) | copy-start | bytes 1572868
  87.7 12.3 %collective-permute-start.11 = (bf16[4,256,256]{2,1,0:T(8,128)(2,1)S(1)}, bf16[4,256,256]{2,1,0:T(8,128)(2,1)}, u32[]{:S(2)}, u32[]{:S(2)}) collective-permute-start(bf16[4,256,256]{2,1,0:T(8,128)(2,1)S(1)} %pad_maximum_fusion.1.mine), channel_id=1, source_target_pairs={{0,1},{1,0},{2,3},{3,2},{4,5},{5,4},{6,7},{7,6},{8,9},{9,8},{10,11... | collective-permute-start | bytes 1572872 | tf_op jit(solution)/shard_map/ppermute | solution.py:247
  89.5 21.7 %copy-start.2 = (bf16[8,256,256]{2,1,0:T(8,128)(2,1)}, bf16[8,256,256]{2,1,0:T(8,128)(2,1)S(1)}, u32[]{:S(2)}) copy-start(bf16[8,256,256]{2,1,0:T(8,128)(2,1)S(1)} %maximum_select_fusion.1.refs_1_.refs_2_) | copy-start | bytes 3145732
  89.5 32.2 %collective-permute-start.10 = (bf16[8,256,256]{2,1,0:T(8,128)(2,1)S(1)}, bf16[8,256,256]{2,1,0:T(8,128)(2,1)S(1)}, u32[]{:S(2)}, u32[]{:S(2)}) collective-permute-start(bf16[8,256,256]{2,1,0:T(8,128)(2,1)S(1)} %maximum_select_fusion.1.refs_1_.refs_2_), channel_id=1, source_target_pairs={{0,4},{1,5},{2,6},{3,7},{4,0},{5,1},{6,2},{7,3},{8,12},{9,13},{10,... | collective-permute-start | bytes 3145736 | tf_op jit(solution)/shard_map/ppermute | solution.py:247
  90.1 33.2 %collective-permute-start.9 = (bf16[8,256,256]{2,1,0:T(8,128)(2,1)S(1)}, bf16[8,256,256]{2,1,0:T(8,128)(2,1)S(1)}, u32[]{:S(2)}, u32[]{:S(2)}) collective-permute-start(bf16[8,256,256]{2,1,0:T(8,128)(2,1)S(1)} %maximum_select_fusion.1.refs_1_.refs_2_), channel_id=1, source_target_pairs={{0,8},{1,9},{2,10},{3,11},{4,12},{5,13},{6,14},{7,15},{8,0},{9,1},... | collective-permute-start | bytes 3145736 | tf_op jit(solution)/shard_map/ppermute | solution.py:247
  121.8 37.8 %copy-start.8 = (bf16[8,256,256]{2,1,0:T(8,128)(2,1)}, bf16[8,256,256]{2,1,0:T(8,128)(2,1)S(1)}, u32[]{:S(2)}) copy-start(bf16[8,256,256]{2,1,0:T(8,128)(2,1)S(1)} %collective-permute-done.10.refs_3_.refs_4_) | copy-start | bytes 3145732
  123.3 36.3 %copy-start.9 = (bf16[8,256,256]{2,1,0:T(8,128)(2,1)}, bf16[8,256,256]{2,1,0:T(8,128)(2,1)S(1)}, u32[]{:S(2)}) copy-start(bf16[8,256,256]{2,1,0:T(8,128)(2,1)S(1)} %collective-permute-done.9.refs_5_.refs_6_) | copy-start | bytes 3145732
  123.3 36.3 %collective-permute-start.15 = (bf16[8,256,256]{2,1,0:T(8,128)(2,1)S(1)}, bf16[8,256,256]{2,1,0:T(8,128)(2,1)S(1)}, u32[]{:S(2)}, u32[]{:S(2)}) collective-permute-start(bf16[8,256,256]{2,1,0:T(8,128)(2,1)S(1)} %collective-permute-done.9.refs_5_.refs_6_), channel_id=1, source_target_pairs={{0,4},{1,5},{2,6},{3,7},{4,0},{5,1},{6,2},{7,3},{8,12},{9,13},{10,... | collective-permute-start | bytes 3145736 | tf_op jit(solution)/shard_map/ppermute | solution.py:247
  124.9 35.7 %copy-start.11 = (bf16[4,256,256]{2,1,0:T(8,128)(2,1)S(1)}, bf16[4,256,256]{2,1,0:T(8,128)(2,1)}, u32[]{:S(2)}) copy-start(bf16[4,256,256]{2,1,0:T(8,128)(2,1)} %get-tuple-element.76) | copy-start | bytes 1572868
  124.9 34.6 %collective-permute-start.13 = (bf16[4,256,256]{2,1,0:T(8,128)(2,1)}, bf16[4,256,256]{2,1,0:T(8,128)(2,1)}, u32[]{:S(2)}, u32[]{:S(2)}) collective-permute-start(bf16[4,256,256]{2,1,0:T(8,128)(2,1)} %get-tuple-element.55), channel_id=1, source_target_pairs={{0,16},{1,17},{2,18},{3,19},{4,20},{5,21},{6,22},{7,23},{8,24},{9,... | collective-permute-start | bytes 1572872 | tf_op jit(solution)/shard_map/ppermute | solution.py:247
  135.5 24.0 %collective-permute-start.14 = (bf16[4,256,256]{2,1,0:T(8,128)(2,1)}, bf16[4,256,256]{2,1,0:T(8,128)(2,1)}, u32[]{:S(2)}, u32[]{:S(2)}) collective-permute-start(bf16[4,256,256]{2,1,0:T(8,128)(2,1)} %get-tuple-element.56), channel_id=1, source_target_pairs={{16,16},{17,20},{18,24},{19,28},{20,17},{21,21},{22,25},{23,29},{2... | collective-permute-start | bytes 1572872 | tf_op jit(solution)/shard_map/ppermute | solution.py:247
  162.2 10.9 %copy-start.1 = (bf16[8,256,256]{2,1,0:T(8,128)(2,1)}, bf16[8,256,256]{2,1,0:T(8,128)(2,1)S(1)}, u32[]{:S(2)}) copy-start(bf16[8,256,256]{2,1,0:T(8,128)(2,1)S(1)} %maximum_select_fusion.2.refs_1_.refs_2_) | copy-start | bytes 3145732
  162.2 23.1 %collective-permute-start.17 = (bf16[8,256,256]{2,1,0:T(8,128)(2,1)S(1)}, bf16[8,256,256]{2,1,0:T(8,128)(2,1)S(1)}, u32[]{:S(2)}, u32[]{:S(2)}) collective-permute-start(bf16[8,256,256]{2,1,0:T(8,128)(2,1)S(1)} %maximum_select_fusion.2.refs_1_.refs_2_), channel_id=1, source_target_pairs={{0,4},{1,5},{2,6},{3,7},{4,0},{5,1},{6,2},{7,3},{8,12},{9,13},{10,... | collective-permute-start | bytes 3145736 | tf_op jit(solution)/shard_map/ppermute | solution.py:247
  163.0 23.6 %collective-permute-start.16 = (bf16[8,256,256]{2,1,0:T(8,128)(2,1)S(1)}, bf16[8,256,256]{2,1,0:T(8,128)(2,1)S(1)}, u32[]{:S(2)}, u32[]{:S(2)}) collective-permute-start(bf16[8,256,256]{2,1,0:T(8,128)(2,1)S(1)} %maximum_select_fusion.2.refs_1_.refs_2_), channel_id=1, source_target_pairs={{0,8},{1,9},{2,10},{3,11},{4,12},{5,13},{6,14},{7,15},{8,0},{9,1},... | collective-permute-start | bytes 3145736 | tf_op jit(solution)/shard_map/ppermute | solution.py:247
  185.3 15.5 %copy-start.5 = (bf16[8,256,256]{2,1,0:T(8,128)(2,1)}, bf16[8,256,256]{2,1,0:T(8,128)(2,1)S(1)}, u32[]{:S(2)}) copy-start(bf16[8,256,256]{2,1,0:T(8,128)(2,1)S(1)} %collective-permute-done.17.refs_3_.refs_4_) | copy-start | bytes 3145732
  186.6 14.1 %copy-start.6 = (bf16[8,256,256]{2,1,0:T(8,128)(2,1)}, bf16[8,256,256]{2,1,0:T(8,128)(2,1)S(1)}, u32[]{:S(2)}) copy-start(bf16[8,256,256]{2,1,0:T(8,128)(2,1)S(1)} %collective-permute-done.16.refs_5_.refs_6_) | copy-start | bytes 3145732
  187.6 13.2 %collective-permute-start.18 = (bf16[4,256,256]{2,1,0:T(8,128)(2,1)}, bf16[4,256,256]{2,1,0:T(8,128)(2,1)S(1)}, u32[]{:S(2)}, u32[]{:S(2)}) collective-permute-start(bf16[4,256,256]{2,1,0:T(8,128)(2,1)} %slice.67), channel_id=1, source_target_pairs={{0,4},{1,5},{2,6},{3,7},{4,0},{5,1},{6,2},{7,3},{8,12},{9,13},{10,... | collective-permute-start | bytes 1572872 | tf_op jit(solution)/shard_map/ppermute | solution.py:247
  188.5 12.2 %collective-permute-start.19 = (bf16[4,256,256]{2,1,0:T(8,128)(2,1)S(1)}, bf16[4,256,256]{2,1,0:T(8,128)(2,1)S(1)}, u32[]{:S(2)}, u32[]{:S(2)}) collective-permute-start(bf16[4,256,256]{2,1,0:T(8,128)(2,1)S(1)} %slice.68), channel_id=1, source_target_pairs={{0,8},{1,9},{2,10},{3,11},{4,12},{5,13},{6,14},{7,15},{8,0},{9,1},... | collective-permute-start | bytes 1572872 | tf_op jit(solution)/shard_map/ppermute | solution.py:247
  (7 other events, 28.4 us)

commit v5 on v4

--- a/solution.py
+++ b/solution.py
@@ -142,21 +142,21 @@
 
 def cols_kernel(start, ids, *refs):
     pieces, (inv0, inv1, low, out, raw) = refs[:8], refs[8:]
-    tile = pieces[0].shape[1]
+    count, tile = 2 * pieces[0].shape[0], pieces[0].shape[1]
     width = 2 * tile
     row_id, col_id = ids[0], ids[1]
     for m in range(4):
         base = pl.multiple_of(((row_id % 4) ^ m) * tile, tile)
-        for i in range(2):
-            raw[pl.ds(base, tile), i * tile : (i + 1) * tile] = pieces[2 * m + i][0]
-    local = lax.broadcasted_iota(jnp.int32, (1, 2 * tile), 1) // tile
-    tile_col = (start + pl.program_id(0) * 2 + local) * 4 + col_id
+        for i in range(count):
+            raw[pl.ds(base, tile), i * tile : (i + 1) * tile] = pieces[2 * m + i % 2][i // 2]
+    local = lax.broadcasted_iota(jnp.int32, (1, count * tile), 1) // tile
+    tile_col = (start + pl.program_id(0) * count + local) * 4 + col_id
     first = dot(inv0[...], raw[:width])
     first = jnp.where(tile_col >= 2, first, 0.0).astype(BF16)
     rest = (raw[width:].astype(F32) - dot(low[...], first)).astype(BF16)
     second = dot(inv1[...], rest)
     second = jnp.where(tile_col >= 4, second, 0.0).astype(BF16)
-    for i in range(2):
+    for i in range(count):
         out[i, :width] = first[:, i * tile : (i + 1) * tile]
         out[i, width:] = second[:, i * tile : (i + 1) * tile]
 
@@ -290,7 +290,7 @@
 
     def factor_cols(start, pieces, low):
         def at(offset):
-            return pl.BlockSpec((1, tile, tile), lambda s: (s + offset, 0, 0))
+            return pl.BlockSpec((2, tile, tile), lambda s: (s + offset // 2, 0, 0))
 
         def kernel(*refs):
             cols_kernel(start, *refs)
@@ -298,11 +298,11 @@
         blocks = [at(offset) for _, offset in pieces]
         return pl.pallas_call(
             kernel,
-            grid=(SUB // 2,),
+            grid=(SUB // 4,),
             in_specs=[smem, *blocks, whole(inv_first), whole(inv_second), whole(low)],
-            out_specs=pl.BlockSpec((2, 2 * width, tile), lambda s: (s, 0, 0)),
+            out_specs=pl.BlockSpec((4, 2 * width, tile), lambda s: (s, 0, 0)),
             out_shape=jax.ShapeDtypeStruct((SUB, 2 * width, tile), BF16),
-            scratch_shapes=[pltpu.VMEM((2 * width, 2 * tile), BF16)],
+            scratch_shapes=[pltpu.VMEM((2 * width, 4 * tile), BF16)],
             compiler_params=params(),
             cost_estimate=cost(SUB * 6 * tile * width * width, 24 * SUB * tile * tile),
             name="cols_%d" % start,

time: 223 us -> 222 us (level)
  no operation moved by 1% of the time
where the time goes in v5:
time: 222 us; the launch traced here: 220 us
  Pallas kernels  97.6 us (44%)
  starting transfers between devices  67.5 us (30%)
  local copies, waits for them, and re-layouts  25.9 us (12%)
  waiting for transfers between devices  22 us (10%)
  other arithmetic  6.57 us (3%)
    ppermute x20, starting transfers between devices, move(): return lax.ppermute(value, ('row', 'col'), pairs)  67.5 us
    pallas_call x4, Pallas kernels, update(): pl.pallas_call(kernel, grid=(stop - start,), in_specs=[smem, whole(cols),...  53.3 us
    pallas_call x3, Pallas kernels, factor_cols(): pl.pallas_call(kernel, grid=(SUB // 4,), in_specs=[smem, *blocks, whole(i...  23.4 us
    ppermute x20, waiting for transfers between devices, move(): return lax.ppermute(value, ('row', 'col'), pairs)  22 us
    pallas_call x1, Pallas kernels, factor_rows(): pl.pallas_call(rows_kernel, grid=(tiles // count,), in_specs=[smem, *[blo...  10.6 us
    unnamed x43, local copies, waits for them, and re-layouts  9.78 us
    pallas_call x1, Pallas kernels, clear(): pl.pallas_call(zeros_kernel, grid=(ratio * groups * (groups - 1) // 2,),...  7.4 us
    slice x1, local copies, waits for them, and re-layouts, local(): strip_b = source[half:, :, 0, :]  4.73 us
  transfers between devices with their start and end apart: 20, of which 6 were waited for; matrix products, arithmetic and copies ran while one was open for 10% of the time, Pallas kernels for 36%

profile of v5, /device:TPU:0, one launch (start us, length us, event | category | flops | bytes accessed | tf_op | source)
XLA Modules:
  0.0 220.4 jit_solution(9854187410845029884)
XLA Ops:
  0.6 1.9 slice-done
  3.2 1.5 fusion
  4.8 6.9 %collective-permute-start = (bf16[4,256,256]{2,1,0:T(8,128)(2,1)S(1)}, bf16[4,256,256]{2,1,0:T(8,128)(2,1)}, u32[]{:S(2)}, u32[]{:S(2)}) collective-permute-start(bf16[4,256,256]{2,1,0:T(8,128)(2,1)S(1)} %get-tuple-element.81), channel_id=1, source_target_pairs={{0,16},{1,17},{2,18},{3,19},{4,20},{5,21},{6,22},{7,23},{8,24},{9,... | collective-permute-start | bytes 1572872 | tf_op jit(solution)/shard_map/ppermute | solution.py:247
  11.7 2.7 %slice.54 = bf16[4,256,1,256]{3,2,1,0:T(2,128)(2,1)S(1)} slice(bf16[12,256,24,256]{3,2,1,0:T(8,128)(2,1)} %bitcast.29), slice={[0:4], [0:256], [0:1], [0:256]} | slice | bytes 1048576 | tf_op jit(solution)/shard_map/slice | solution.py:379
  18.5 3.6 %collective-permute-done = bf16[4,256,256]{2,1,0:T(8,128)(2,1)} collective-permute-done((bf16[4,256,256]{2,1,0:T(8,128)(2,1)S(1)}, bf16[4,256,256]{2,1,0:T(8,128)(2,1)}, u32[]{:S(2)}, u32[]{:S(2)}) %collective-permute-start) | collective-permute-done | bytes 524320 | tf_op jit(solution)/shard_map/ppermute | solution.py:247
  22.1 1.7 maximum_select_fusion.refs_1_.refs_2_
  23.8 1.6 collective-permute-start.3
  25.3 12.7 %collective-permute-start.2 = (bf16[8,256,256]{2,1,0:T(8,128)(2,1)S(1)}, bf16[8,256,256]{2,1,0:T(8,128)(2,1)}, u32[]{:S(2)}, u32[]{:S(2)}) collective-permute-start(bf16[8,256,256]{2,1,0:T(8,128)(2,1)S(1)} %maximum_select_fusion.refs_1_.refs_2_), channel_id=1, source_target_pairs={{0,8},{1,9},{2,10},{3,11},{4,12},{5,13},{6,14},{7,15},{8,0},{9,1},... | collective-permute-start | bytes 3145736 | tf_op jit(solution)/shard_map/ppermute | solution.py:247
  38.1 4.7 %slice.56 = bf16[8,256,1,256]{3,2,1,0:T(2,128)(2,1)S(1)} slice(bf16[12,256,24,256]{3,2,1,0:T(8,128)(2,1)} %bitcast.30), slice={[4:12], [0:256], [0:1], [0:256]} | slice | bytes 2097152 | tf_op jit(solution)/shard_map/slice | solution.py:385
  44.3 1.5 collective-permute-start.8
  45.9 3.4 %copy.83 = bf16[8,256,1,256]{1,3,0,2:T(8,128)(2,1)} copy(bf16[8,256,1,256]{3,2,1,0:T(2,128)(2,1)S(1)} %slice.56) | data formatting | bytes 2097152
  49.2 11.9 %collective-permute-done.2.refs_5_.refs_6_ = bf16[8,256,256]{2,1,0:T(8,128)(2,1)} collective-permute-done((bf16[8,256,256]{2,1,0:T(8,128)(2,1)S(1)}, bf16[8,256,256]{2,1,0:T(8,128)(2,1)}, u32[]{:S(2)}, u32[]{:S(2)}) %collective-permute-start.2) | collective-permute-done | bytes 1048608 | tf_op jit(solution)/shard_map/ppermute | solution.py:247
  61.7 11.6 %collective-permute-start.6 = (bf16[4,256,256]{2,1,0:T(8,128)(2,1)}, bf16[4,256,256]{2,1,0:T(8,128)(2,1)}, u32[]{:S(2)}, u32[]{:S(2)}) collective-permute-start(bf16[4,256,256]{2,1,0:T(8,128)(2,1)} %get-tuple-element.79), channel_id=1, source_target_pairs={{0,16},{1,17},{2,18},{3,19},{4,20},{5,21},{6,22},{7,23},{8,24},{9,... | collective-permute-start | bytes 1572872 | tf_op jit(solution)/shard_map/ppermute | solution.py:247
  73.3 2.2 %fusion.1 = (bf16[4,256,256]{2,1,0:T(8,128)(2,1)}, bf16[4,256,256]{2,1,0:T(8,128)(2,1)}) fusion(bf16[8,256,256]{2,1,0:T(8,128)(2,1)} %bitcast.38), kind=kLoop, calls=%fused_computation.10 | loop fusion | bytes 2097152 | tf_op jit(solution)/shard_map/slice | solution.py:409
  77.6 7.4 %clear.1.refs_4_ = bf16[12,256,24,256]{3,2,1,0:T(8,128)(2,1)} custom-call(s32[2]{0:T(128)} %pad_add_fusion._.ids.refs_0_), custom_call_target="tpu_custom_call" | custom-call | bytes 12582912 | tf_op jit(solution)/shard_map/clear/pallas_call | solution.py:323
  90.1 9.9 %collective-permute-start.9 = (bf16[8,256,256]{2,1,0:T(8,128)(2,1)S(1)}, bf16[8,256,256]{2,1,0:T(8,128)(2,1)S(1)}, u32[]{:S(2)}, u32[]{:S(2)}) collective-permute-start(bf16[8,256,256]{2,1,0:T(8,128)(2,1)S(1)} %maximum_select_fusion.1.refs_1_.refs_2_), channel_id=1, source_target_pairs={{0,8},{1,9},{2,10},{3,11},{4,12},{5,13},{6,14},{7,15},{8,0},{9,1},... | collective-permute-start | bytes 3145736 | tf_op jit(solution)/shard_map/ppermute | solution.py:247
  100.0 2.9 %link.1 = (bf16[512,512]{1,0:T(8,128)(2,1)}, bf16[512,512]{1,0:T(8,128)(2,1)}) custom-call(s32[2]{0:T(128)} %pad_add_fusion._.ids.refs_0_, bf16[4,256,256]{2,1,0:T(8,128)(2,1)} %copy-done.15, bf16[4,256,256]{2,1,0:T(8,128)(2,1)} %collective-permute-done.11.other, bf16[512,512]{1,0:T(8,128)(2,1)} %bitcast.39), custom_call_target="tpu_custom_call" | custom-call | tf_op jit(solution)/shard_map/link/pallas_call | solution.py:266
  102.9 7.8 %cols_0.1.refs_1_ = bf16[8,1024,256]{2,1,0:T(8,128)(2,1)} custom-call(s32[2]{0:T(128)} %pad_add_fusion._.ids.refs_0_, bf16[8,256,256]{2,1,0:T(8,128)(2,1)} %copy-done, bf16[8,256,256]{2,1,0:T(8,128)(2,1)} %copy-done, bf16[8,256,256]{2,1,0:T(8,128)(2,1)} %collective-permute-done.3.refs_3_.refs_4_, ...), custom_call_target="tpu_custom_call" | custom-call | flops 3221225472 | bytes 12582912 | tf_op jit(solution)/shard_map/cols_0/pallas_call | solution.py:299
  110.7 10.6 %rows.1.refs_2_ = bf16[12,256,1024]{2,1,0:T(8,128)(2,1)} custom-call(s32[2]{0:T(128)} %pad_add_fusion._.ids.refs_0_, bf16[12,256,256]{2,1,0:T(8,128)(2,1)} %pad_maximum_fusion.q0, bf16[12,256,256]{2,1,0:T(8,128)(2,1)} %collective-permute-done.7.q1, bf16[12,256,256]{2,1,0:T(8,128)(2,1)} %collective-permute-done.8.q2, ...), custom_call_target="tpu_custom_call" | custom-call | flops 4831838208 | bytes 18874368 | tf_op jit(solution)/shard_map/rows/pallas_call | solution.py:279
  121.3 2.0 collective-permute-done.9.refs_5_.refs_6_
  123.3 1.7 collective-permute-start.15
  124.9 10.6 %collective-permute-start.13 = (bf16[4,256,256]{2,1,0:T(8,128)(2,1)}, bf16[4,256,256]{2,1,0:T(8,128)(2,1)}, u32[]{:S(2)}, u32[]{:S(2)}) collective-permute-start(bf16[4,256,256]{2,1,0:T(8,128)(2,1)} %get-tuple-element.55), channel_id=1, source_target_pairs={{0,16},{1,17},{2,18},{3,19},{4,20},{5,21},{6,22},{7,23},{8,24},{9,... | collective-permute-start | bytes 1572872 | tf_op jit(solution)/shard_map/ppermute | solution.py:247
  137.0 22.5 %update_0_0.1.refs_4_ = bf16[12,256,24,256]{3,2,1,0:T(8,128)(2,1)} custom-call(s32[2]{0:T(128)} %pad_add_fusion._.ids.refs_0_, bf16[8,1024,256]{2,1,0:T(8,128)(2,1)} %cols_0.1.refs_1_, bf16[12,256,1024]{2,1,0:T(8,128)(2,1)} %rows.1.refs_2_, bf16[12,256,24,256]{3,2,1,0:T(8,128)(2,1)} %bitcast.31, ...), custom_call_target="tpu_custom_call", output_to_operand_aliasing={{}: (4, {})} | custom-call | flops 12884901888 | bytes 37748736 | tf_op jit(solution)/shard_map/update_0_0/pallas_call | solution.py:340
  160.7 1.5 maximum_select_fusion.2.refs_1_.refs_2_
  163.0 1.7 collective-permute-start.16
  164.8 7.8 %cols_8.1.refs_1_ = bf16[8,1024,256]{2,1,0:T(8,128)(2,1)} custom-call(s32[2]{0:T(128)} %pad_add_fusion._.ids.refs_0_, bf16[8,256,256]{2,1,0:T(8,128)(2,1)} %copy-done.2, bf16[8,256,256]{2,1,0:T(8,128)(2,1)} %copy-done.2, bf16[8,256,256]{2,1,0:T(8,128)(2,1)} %copy-done.8, bf16[8,256,256]{2,1,0:T(8,128)(2,1)} %copy-done.8, bf16[8,256,256]{2,1,0:T(8,128)(2,1)} %copy-done.9, ...), custom_call_target="tpu_custom_call" | custom-call | flops 3221225472 | bytes 12582912 | tf_op jit(solution)/shard_map/cols_8/pallas_call | solution.py:299
  172.6 10.2 %update_1_4.1.refs_4_ = bf16[12,256,24,256]{3,2,1,0:T(8,128)(2,1)} custom-call(s32[2]{0:T(128)} %pad_add_fusion._.ids.refs_0_, bf16[8,1024,256]{2,1,0:T(8,128)(2,1)} %cols_8.1.refs_1_, bf16[12,256,1024]{2,1,0:T(8,128)(2,1)} %rows.1.refs_2_, bf16[12,256,24,256]{3,2,1,0:T(8,128)(2,1)} %bitcast.32, ...), custom_call_target="tpu_custom_call", output_to_operand_aliasing={{}: (4, {})} | custom-call | flops 4294967296 | bytes 12582912 | tf_op jit(solution)/shard_map/update_1_4/pallas_call | solution.py:340
  182.8 2.5 %collective-permute-done.17.refs_3_.refs_4_ = bf16[8,256,256]{2,1,0:T(8,128)(2,1)S(1)} collective-permute-done((bf16[8,256,256]{2,1,0:T(8,128)(2,1)S(1)}, bf16[8,256,256]{2,1,0:T(8,128)(2,1)S(1)}, u32[]{:S(2)}, u32[]{:S(2)}) %collective-permute-start.17) | collective-permute-done | bytes 1048608 | tf_op jit(solution)/shard_map/ppermute | solution.py:247
  188.5 1.7 collective-permute-start.19
  190.3 10.5 %update_1_8.1.refs_4_ = bf16[12,256,24,256]{3,2,1,0:T(8,128)(2,1)} custom-call(s32[2]{0:T(128)} %pad_add_fusion._.ids.refs_0_, bf16[8,1024,256]{2,1,0:T(8,128)(2,1)} %cols_8.1.refs_1_, bf16[12,256,1024]{2,1,0:T(8,128)(2,1)} %rows.1.refs_2_, bf16[12,256,24,256]{3,2,1,0:T(8,128)(2,1)} %bitcast.33, ...), custom_call_target="tpu_custom_call", output_to_operand_aliasing={{}: (4, {})} | custom-call | flops 4294967296 | bytes 12582912 | tf_op jit(solution)/shard_map/update_1_8/pallas_call | solution.py:340
  202.5 7.8 %cols_16.1.refs_1_ = bf16[8,1024,256]{2,1,0:T(8,128)(2,1)} custom-call(s32[2]{0:T(128)} %pad_add_fusion._.ids.refs_0_, bf16[8,256,256]{2,1,0:T(8,128)(2,1)} %copy-done.1, bf16[8,256,256]{2,1,0:T(8,128)(2,1)} %copy-done.1, bf16[8,256,256]{2,1,0:T(8,128)(2,1)} %copy-done.5, bf16[8,256,256]{2,1,0:T(8,128)(2,1)} %copy-done.5, bf16[8,256,256]{2,1,0:T(8,128)(2,1)} %copy-done.6, ...), custom_call_target="tpu_custom_call" | custom-call | flops 3221225472 | bytes 12582912 | tf_op jit(solution)/shard_map/cols_16/pallas_call | solution.py:299
  210.3 10.2 %update_2_8.1 = bf16[12,256,24,256]{3,2,1,0:T(8,128)(2,1)} custom-call(s32[2]{0:T(128)} %pad_add_fusion._.ids.refs_0_, bf16[8,1024,256]{2,1,0:T(8,128)(2,1)} %cols_16.1.refs_1_, bf16[12,256,1024]{2,1,0:T(8,128)(2,1)} %rows.1.refs_2_, bf16[12,256,24,256]{3,2,1,0:T(8,128)(2,1)} %bitcast.34, ...), custom_call_target="tpu_custom_call", output_to_operand_aliasing={{}: (4, {})} | custom-call | flops 4294967296 | bytes 12582912 | tf_op jit(solution)/shard_map/update_2_8/pallas_call | solution.py:340
  (79 shorter events, 22.4 us)
Async XLA Ops:
  4.8 17.3 %copy-start.14 = (bf16[4,256,256]{2,1,0:T(8,128)(2,1)}, bf16[4,256,256]{2,1,0:T(8,128)(2,1)S(1)}, u32[]{:S(2)}) copy-start(bf16[4,256,256]{2,1,0:T(8,128)(2,1)S(1)} %get-tuple-element.81) | copy-start | bytes 1572868
  4.8 11.7 %copy-start.3 = (bf16[512,512]{1,0:T(8,128)(2,1)S(1)}, bf16[512,512]{1,0:T(8,128)(2,1)}, u32[]{:S(2)}) copy-start(bf16[512,512]{1,0:T(8,128)(2,1)} %refs_9_.5) | copy-start | bytes 1572868
  4.8 12.7 %copy-start.4 = (bf16[512,512]{1,0:T(8,128)(2,1)S(1)}, bf16[512,512]{1,0:T(8,128)(2,1)}, u32[]{:S(2)}) copy-start(bf16[512,512]{1,0:T(8,128)(2,1)} %refs_10_.5) | copy-start | bytes 1572868
  4.8 17.3 %collective-permute-start = (bf16[4,256,256]{2,1,0:T(8,128)(2,1)S(1)}, bf16[4,256,256]{2,1,0:T(8,128)(2,1)}, u32[]{:S(2)}, u32[]{:S(2)}) collective-permute-start(bf16[4,256,256]{2,1,0:T(8,128)(2,1)S(1)} %get-tuple-element.81), channel_id=1, source_target_pairs={{0,16},{1,17},{2,18},{3,19},{4,20},{5,21},{6,22},{7,23},{8,24},{9,... | collective-permute-start | bytes 1572872 | tf_op jit(solution)/shard_map/ppermute | solution.py:247
  15.0 7.0 %collective-permute-start.1 = (bf16[4,256,256]{2,1,0:T(8,128)(2,1)S(1)}, bf16[4,256,256]{2,1,0:T(8,128)(2,1)}, u32[]{:S(2)}, u32[]{:S(2)}) collective-permute-start(bf16[4,256,256]{2,1,0:T(8,128)(2,1)S(1)} %bitcast.42), channel_id=1, source_target_pairs={{16,16},{17,20},{18,24},{19,28},{20,17},{21,21},{22,25},{23,29},{2... | collective-permute-start | bytes 1572872 | tf_op jit(solution)/shard_map/ppermute | solution.py:247
  23.7 61.9 %copy-start = (bf16[8,256,256]{2,1,0:T(8,128)(2,1)}, bf16[8,256,256]{2,1,0:T(8,128)(2,1)S(1)}, u32[]{:S(2)}) copy-start(bf16[8,256,256]{2,1,0:T(8,128)(2,1)S(1)} %maximum_select_fusion.refs_1_.refs_2_) | copy-start | bytes 3145732
  23.8 25.5 %collective-permute-start.3 = (bf16[8,256,256]{2,1,0:T(8,128)(2,1)S(1)}, bf16[8,256,256]{2,1,0:T(8,128)(2,1)}, u32[]{:S(2)}, u32[]{:S(2)}) collective-permute-start(bf16[8,256,256]{2,1,0:T(8,128)(2,1)S(1)} %maximum_select_fusion.refs_1_.refs_2_), channel_id=1, source_target_pairs={{0,4},{1,5},{2,6},{3,7},{4,0},{5,1},{6,2},{7,3},{8,12},{9,13},{10,... | collective-permute-start | bytes 3145736 | tf_op jit(solution)/shard_map/ppermute | solution.py:247
  25.3 35.8 %collective-permute-start.2 = (bf16[8,256,256]{2,1,0:T(8,128)(2,1)S(1)}, bf16[8,256,256]{2,1,0:T(8,128)(2,1)}, u32[]{:S(2)}, u32[]{:S(2)}) collective-permute-start(bf16[8,256,256]{2,1,0:T(8,128)(2,1)S(1)} %maximum_select_fusion.refs_1_.refs_2_), channel_id=1, source_target_pairs={{0,8},{1,9},{2,10},{3,11},{4,12},{5,13},{6,14},{7,15},{8,0},{9,1},... | collective-permute-start | bytes 3145736 | tf_op jit(solution)/shard_map/ppermute | solution.py:247
  44.3 40.7 %collective-permute-start.8 = (bf16[12,256,256]{2,1,0:T(8,128)(2,1)}, bf16[12,256,256]{2,1,0:T(8,128)(2,1)}, u32[]{:S(2)}, u32[]{:S(2)}) collective-permute-start(bf16[12,256,256]{2,1,0:T(8,128)(2,1)} %pad_maximum_fusion.q0), channel_id=1, source_target_pairs={{0,2},{1,3},{2,0},{3,1},{4,6},{5,7},{6,4},{7,5},{8,10},{9,11},{10,... | collective-permute-start | bytes 4718600 | tf_op jit(solution)/shard_map/ppermute | solution.py:247
  45.9 39.1 %collective-permute-start.7 = (bf16[12,256,256]{2,1,0:T(8,128)(2,1)}, bf16[12,256,256]{2,1,0:T(8,128)(2,1)}, u32[]{:S(2)}, u32[]{:S(2)}) collective-permute-start(bf16[12,256,256]{2,1,0:T(8,128)(2,1)} %pad_maximum_fusion.q0), channel_id=1, source_target_pairs={{0,1},{1,0},{2,3},{3,2},{4,5},{5,4},{6,7},{7,6},{8,9},{9,8},{10,11... | collective-permute-start | bytes 4718600 | tf_op jit(solution)/shard_map/ppermute | solution.py:247
  61.2 24.4 %collective-permute-start.4 = (bf16[8,256,256]{2,1,0:T(8,128)(2,1)}, bf16[8,256,256]{2,1,0:T(8,128)(2,1)S(1)}, u32[]{:S(2)}, u32[]{:S(2)}) collective-permute-start(bf16[8,256,256]{2,1,0:T(8,128)(2,1)} %collective-permute-done.2.refs_5_.refs_6_), channel_id=1, source_target_pairs={{0,4},{1,5},{2,6},{3,7},{4,0},{5,1},{6,2},{7,3},{8,12},{9,13},{10,... | collective-permute-start | bytes 3145736 | tf_op jit(solution)/shard_map/ppermute | solution.py:247
  61.7 23.3 %collective-permute-start.6 = (bf16[4,256,256]{2,1,0:T(8,128)(2,1)}, bf16[4,256,256]{2,1,0:T(8,128)(2,1)}, u32[]{:S(2)}, u32[]{:S(2)}) collective-permute-start(bf16[4,256,256]{2,1,0:T(8,128)(2,1)} %get-tuple-element.79), channel_id=1, source_target_pairs={{0,16},{1,17},{2,18},{3,19},{4,20},{5,21},{6,22},{7,23},{8,24},{9,... | collective-permute-start | bytes 1572872 | tf_op jit(solution)/shard_map/ppermute | solution.py:247
  75.5 9.5 %collective-permute-start.5 = (bf16[4,256,256]{2,1,0:T(8,128)(2,1)}, bf16[4,256,256]{2,1,0:T(8,128)(2,1)}, u32[]{:S(2)}, u32[]{:S(2)}) collective-permute-start(bf16[4,256,256]{2,1,0:T(8,128)(2,1)} %get-tuple-element.83), channel_id=1, source_target_pairs={{16,16},{17,20},{18,24},{19,28},{20,17},{21,21},{22,25},{23,29},{2... | collective-permute-start | bytes 1572872 | tf_op jit(solution)/shard_map/ppermute | solution.py:247
  77.6 10.6 %copy-start.13 = (bf16[4,256,256]{2,1,0:T(8,128)(2,1)S(1)}, bf16[4,256,256]{2,1,0:T(8,128)(2,1)}, u32[]{:S(2)}) copy-start(bf16[4,256,256]{2,1,0:T(8,128)(2,1)} %get-tuple-element.79) | copy-start | bytes 1572868
  85.6 25.1 %collective-permute-start.12 = (bf16[12,256,256]{2,1,0:T(8,128)(2,1)}, bf16[12,256,256]{2,1,0:T(8,128)(2,1)}, u32[]{:S(2)}, u32[]{:S(2)}) collective-permute-start(bf16[12,256,256]{2,1,0:T(8,128)(2,1)} %collective-permute-done.8.q2), channel_id=1, source_target_pairs={{0,1},{1,0},{2,3},{3,2},{4,5},{5,4},{6,7},{7,6},{8,9},{9,8},{10,11... | collective-permute-start | bytes 4718600 | tf_op jit(solution)/shard_map/ppermute | solution.py:247
  87.7 12.3 %copy-start.15 = (bf16[4,256,256]{2,1,0:T(8,128)(2,1)}, bf16[4,256,256]{2,1,0:T(8,128)(2,1)S(1)}, u32[]{:S(2)}) copy-start(bf16[4,256,256]{2,1,0:T(8,128)(2,1)S(1)} %pad_maximum_fusion.1.mine) | copy-start | bytes 1572868
  87.7 12.3 %collective-permute-start.11 = (bf16[4,256,256]{2,1,0:T(8,128)(2,1)S(1)}, bf16[4,256,256]{2,1,0:T(8,128)(2,1)}, u32[]{:S(2)}, u32[]{:S(2)}) collective-permute-start(bf16[4,256,256]{2,1,0:T(8,128)(2,1)S(1)} %pad_maximum_fusion.1.mine), channel_id=1, source_target_pairs={{0,1},{1,0},{2,3},{3,2},{4,5},{5,4},{6,7},{7,6},{8,9},{9,8},{10,11... | collective-permute-start | bytes 1572872 | tf_op jit(solution)/shard_map/ppermute | solution.py:247
  89.5 21.2 %copy-start.2 = (bf16[8,256,256]{2,1,0:T(8,128)(2,1)}, bf16[8,256,256]{2,1,0:T(8,128)(2,1)S(1)}, u32[]{:S(2)}) copy-start(bf16[8,256,256]{2,1,0:T(8,128)(2,1)S(1)} %maximum_select_fusion.1.refs_1_.refs_2_) | copy-start | bytes 3145732
  89.5 31.7 %collective-permute-start.10 = (bf16[8,256,256]{2,1,0:T(8,128)(2,1)S(1)}, bf16[8,256,256]{2,1,0:T(8,128)(2,1)S(1)}, u32[]{:S(2)}, u32[]{:S(2)}) collective-permute-start(bf16[8,256,256]{2,1,0:T(8,128)(2,1)S(1)} %maximum_select_fusion.1.refs_1_.refs_2_), channel_id=1, source_target_pairs={{0,4},{1,5},{2,6},{3,7},{4,0},{5,1},{6,2},{7,3},{8,12},{9,13},{10,... | collective-permute-start | bytes 3145736 | tf_op jit(solution)/shard_map/ppermute | solution.py:247
  90.1 33.2 %collective-permute-start.9 = (bf16[8,256,256]{2,1,0:T(8,128)(2,1)S(1)}, bf16[8,256,256]{2,1,0:T(8,128)(2,1)S(1)}, u32[]{:S(2)}, u32[]{:S(2)}) collective-permute-start(bf16[8,256,256]{2,1,0:T(8,128)(2,1)S(1)} %maximum_select_fusion.1.refs_1_.refs_2_), channel_id=1, source_target_pairs={{0,8},{1,9},{2,10},{3,11},{4,12},{5,13},{6,14},{7,15},{8,0},{9,1},... | collective-permute-start | bytes 3145736 | tf_op jit(solution)/shard_map/ppermute | solution.py:247
  121.3 38.3 %copy-start.8 = (bf16[8,256,256]{2,1,0:T(8,128)(2,1)}, bf16[8,256,256]{2,1,0:T(8,128)(2,1)S(1)}, u32[]{:S(2)}) copy-start(bf16[8,256,256]{2,1,0:T(8,128)(2,1)S(1)} %collective-permute-done.10.refs_3_.refs_4_) | copy-start | bytes 3145732
  123.3 36.3 %copy-start.9 = (bf16[8,256,256]{2,1,0:T(8,128)(2,1)}, bf16[8,256,256]{2,1,0:T(8,128)(2,1)S(1)}, u32[]{:S(2)}) copy-start(bf16[8,256,256]{2,1,0:T(8,128)(2,1)S(1)} %collective-permute-done.9.refs_5_.refs_6_) | copy-start | bytes 3145732
  123.3 36.3 %collective-permute-start.15 = (bf16[8,256,256]{2,1,0:T(8,128)(2,1)S(1)}, bf16[8,256,256]{2,1,0:T(8,128)(2,1)S(1)}, u32[]{:S(2)}, u32[]{:S(2)}) collective-permute-start(bf16[8,256,256]{2,1,0:T(8,128)(2,1)S(1)} %collective-permute-done.9.refs_5_.refs_6_), channel_id=1, source_target_pairs={{0,4},{1,5},{2,6},{3,7},{4,0},{5,1},{6,2},{7,3},{8,12},{9,13},{10,... | collective-permute-start | bytes 3145736 | tf_op jit(solution)/shard_map/ppermute | solution.py:247
  124.9 35.7 %copy-start.11 = (bf16[4,256,256]{2,1,0:T(8,128)(2,1)S(1)}, bf16[4,256,256]{2,1,0:T(8,128)(2,1)}, u32[]{:S(2)}) copy-start(bf16[4,256,256]{2,1,0:T(8,128)(2,1)} %get-tuple-element.76) | copy-start | bytes 1572868
  124.9 34.6 %collective-permute-start.13 = (bf16[4,256,256]{2,1,0:T(8,128)(2,1)}, bf16[4,256,256]{2,1,0:T(8,128)(2,1)}, u32[]{:S(2)}, u32[]{:S(2)}) collective-permute-start(bf16[4,256,256]{2,1,0:T(8,128)(2,1)} %get-tuple-element.55), channel_id=1, source_target_pairs={{0,16},{1,17},{2,18},{3,19},{4,20},{5,21},{6,22},{7,23},{8,24},{9,... | collective-permute-start | bytes 1572872 | tf_op jit(solution)/shard_map/ppermute | solution.py:247
  135.5 24.0 %collective-permute-start.14 = (bf16[4,256,256]{2,1,0:T(8,128)(2,1)}, bf16[4,256,256]{2,1,0:T(8,128)(2,1)}, u32[]{:S(2)}, u32[]{:S(2)}) collective-permute-start(bf16[4,256,256]{2,1,0:T(8,128)(2,1)} %get-tuple-element.56), channel_id=1, source_target_pairs={{16,16},{17,20},{18,24},{19,28},{20,17},{21,21},{22,25},{23,29},{2... | collective-permute-start | bytes 1572872 | tf_op jit(solution)/shard_map/ppermute | solution.py:247
  162.2 23.1 %collective-permute-start.17 = (bf16[8,256,256]{2,1,0:T(8,128)(2,1)S(1)}, bf16[8,256,256]{2,1,0:T(8,128)(2,1)S(1)}, u32[]{:S(2)}, u32[]{:S(2)}) collective-permute-start(bf16[8,256,256]{2,1,0:T(8,128)(2,1)S(1)} %maximum_select_fusion.2.refs_1_.refs_2_), channel_id=1, source_target_pairs={{0,4},{1,5},{2,6},{3,7},{4,0},{5,1},{6,2},{7,3},{8,12},{9,13},{10,... | collective-permute-start | bytes 3145736 | tf_op jit(solution)/shard_map/ppermute | solution.py:247
  163.0 23.6 %collective-permute-start.16 = (bf16[8,256,256]{2,1,0:T(8,128)(2,1)S(1)}, bf16[8,256,256]{2,1,0:T(8,128)(2,1)S(1)}, u32[]{:S(2)}, u32[]{:S(2)}) collective-permute-start(bf16[8,256,256]{2,1,0:T(8,128)(2,1)S(1)} %maximum_select_fusion.2.refs_1_.refs_2_), channel_id=1, source_target_pairs={{0,8},{1,9},{2,10},{3,11},{4,12},{5,13},{6,14},{7,15},{8,0},{9,1},... | collective-permute-start | bytes 3145736 | tf_op jit(solution)/shard_map/ppermute | solution.py:247
  185.3 15.5 %copy-start.5 = (bf16[8,256,256]{2,1,0:T(8,128)(2,1)}, bf16[8,256,256]{2,1,0:T(8,128)(2,1)S(1)}, u32[]{:S(2)}) copy-start(bf16[8,256,256]{2,1,0:T(8,128)(2,1)S(1)} %collective-permute-done.17.refs_3_.refs_4_) | copy-start | bytes 3145732
  186.6 14.1 %copy-start.6 = (bf16[8,256,256]{2,1,0:T(8,128)(2,1)}, bf16[8,256,256]{2,1,0:T(8,128)(2,1)S(1)}, u32[]{:S(2)}) copy-start(bf16[8,256,256]{2,1,0:T(8,128)(2,1)S(1)} %collective-permute-done.16.refs_5_.refs_6_) | copy-start | bytes 3145732
  187.6 13.2 %collective-permute-start.18 = (bf16[4,256,256]{2,1,0:T(8,128)(2,1)}, bf16[4,256,256]{2,1,0:T(8,128)(2,1)S(1)}, u32[]{:S(2)}, u32[]{:S(2)}) collective-permute-start(bf16[4,256,256]{2,1,0:T(8,128)(2,1)} %slice.67), channel_id=1, source_target_pairs={{0,4},{1,5},{2,6},{3,7},{4,0},{5,1},{6,2},{7,3},{8,12},{9,13},{10,... | collective-permute-start | bytes 1572872 | tf_op jit(solution)/shard_map/ppermute | solution.py:247
  188.5 12.2 %collective-permute-start.19 = (bf16[4,256,256]{2,1,0:T(8,128)(2,1)S(1)}, bf16[4,256,256]{2,1,0:T(8,128)(2,1)S(1)}, u32[]{:S(2)}, u32[]{:S(2)}) collective-permute-start(bf16[4,256,256]{2,1,0:T(8,128)(2,1)S(1)} %slice.68), channel_id=1, source_target_pairs={{0,8},{1,9},{2,10},{3,11},{4,12},{5,13},{6,14},{7,15},{8,0},{9,1},... | collective-permute-start | bytes 1572872 | tf_op jit(solution)/shard_map/ppermute | solution.py:247
  (7 other events, 28.2 us)
